TPU v7x, 32 devices: a whole 2x2x4 slice. The times are simulated.
32 devices in a mesh: slab: 32 (over z, y, x, core).
Axes of the slice: x: 2, y: 2, z: 4, core: 2. Of those that a mesh axis runs over, the one named last changes fastest.
Arguments:
- series: float32 [80, 1048576], P(None, 'slab'), as said below
- noise_mask: int32 [1048576], P('slab'), may hold values 0 or 1
- probes: float32 [80, 5], replicated, may hold values from -6 to 6
- sample_weights: bfloat16 [1536, 256, 128], P('slab'), may hold values from -0.375 to 0.375
- block_ids: int32 [1536], P('slab'), may hold values from 0 to 127
- tile_ids: int32 [1536], P('slab'), may hold values from -1 to 127, as said below
- tile_owner: int32 [128], replicated, may hold values from 0 to 31, as said below
Outputs:
- vertex_series: float32 [128, 80, 128], P('slab')
Inputs may be any that keep to these rules, and one draw needn't show every extreme that they name: `tile_ids`: on each device the used entries come first and are at least half of its 48 entries; some device uses all. Used entry k of the device with index d names vertex tile (d * 4 + o_d + k) mod 128, with o_d in [0, 4) fixed per device; unused entries hold -1. tile_owner[j] = p[j mod the number of devices] for a permutation p of the devices, so every device owns 4 tiles. `series`: values of order one to some tens; each voxel carries its own baseline.
All inputs are finite; a program needn't handle non-finite values. No bound on the sum of `noise_mask` on one device may be relied on, other than what follows from the above.
Results may differ from a plain program's by a relative error of at most 0.005.
Values may be sent and summed in bfloat16 or wider, within the bound.
No kernel may reach another device: no remote copies, remote signals or barrier semaphores. Data moves between devices by JAX's collectives and lax.ppermute only.
A program may use at most 128 MiB of HBM per device.

v0:
```python
import jax
import jax.numpy as jnp
from jax import lax
from jax.sharding import PartitionSpec as P

HIGHEST = lax.Precision.HIGHEST


def make_projector(components):
    inner = jnp.dot(components.T, components, precision=HIGHEST)
    factor = jnp.linalg.cholesky(inner)
    solved = jax.scipy.linalg.cho_solve((factor, True), components.T)
    return jnp.dot(components, solved, precision=HIGHEST)


def body(series, noise_mask, probes, sample_weights, block_ids, tile_ids, tile_owner):
    frames, voxels = series.shape
    devices = lax.axis_size("slab")
    tile_width = sample_weights.shape[2]
    block_width = sample_weights.shape[1]
    owned = tile_owner.shape[0] // devices
    demeaned = series - jnp.mean(series, axis=0, keepdims=True)
    weighted = demeaned * noise_mask.astype(jnp.float32)[None, :]
    local_gram = lax.dot_general(weighted, demeaned, (((1,), (1,)), ((), ())), precision=HIGHEST)
    noise_gram = lax.psum(local_gram, "slab")
    components = jnp.dot(noise_gram, probes, precision=HIGHEST)
    projector = make_projector(components)
    cleaned = (demeaned - jnp.dot(projector, demeaned, precision=HIGHEST)).astype(jnp.bfloat16)
    blocks = cleaned.reshape(frames, voxels // block_width, block_width)
    picked = jnp.take(blocks, block_ids, axis=1)
    partial_value = jnp.einsum(
        "fkv,kvt->kft", picked, sample_weights, preferred_element_type=jnp.float32
    ).astype(jnp.bfloat16)
    used = tile_ids >= 0
    matches = tile_ids[:, None] == jnp.arange(tile_owner.shape[0], dtype=jnp.int32)[None, :]
    owners = jnp.sum(jnp.where(matches, tile_owner[None, :], 0), axis=1)
    local_slot = jnp.where(used, tile_ids // devices, -1)
    total_rows = owned * devices
    rows = jnp.where(used, owners * owned + local_slot, total_rows)
    widened = partial_value.astype(jnp.float32)
    inside = (rows >= 0) & (rows < owned * lax.axis_size("slab"))
    target = jnp.where(inside, rows, owned * lax.axis_size("slab"))
    empty = jnp.zeros((owned * lax.axis_size("slab"), frames, tile_width), jnp.float32)
    return lax.psum_scatter(
        empty.at[target].add(widened, mode="drop"), "slab", scatter_dimension=0, tiled=True
    )


def solution(mesh):
    return jax.shard_map(
        body,
        mesh=mesh,
        in_specs=(
            P(None, "slab"),
            P("slab"),
            P(),
            P("slab", None, None),
            P("slab"),
            P("slab"),
            P(),
        ),
        out_specs=P("slab", None, None),
        check_vma=False,
    )
```

profile of v0, /device:TPU:0, one launch (start us, length us, event | category | flops | bytes accessed | tf_op | source)
XLA Modules:
  0.0 259.7 jit_solution(14531749879565290467)
XLA Ops:
  6.5 0.0 copy-start
  6.5 0.0 reduce-scatter.2.cloned.1.call-start
  6.5 0.8 compare_and_fusion
  7.4 0.8 compare_select_fusion
  8.2 0.8 select_reduce_fusion
  9.0 0.7 compare_select_fusion.1
  9.7 0.9 convert_element_type.12
  10.6 4.7 %reduce_sum.19 = f32[32768]{0:T(1024)S(1)} reduce(f32[80,32768]{1,0:T(8,128)} %param.7, f32[]{:T(128)} %constant.78.clone.1), dimensions={0}, to_apply=%region_1.0 | reduce | flops 2588672 | bytes 10616836 | tf_op jit(solution)/shard_map/reduce_sum | solution.py:22
  15.3 0.0 copy-start.1
  15.3 13.9 %fusion.1 = f32[80,80]{1,0:T(8,128)S(1)} fusion(f32[80,32768]{1,0:T(8,128)} %param.7, f32[32768]{0:T(1024)S(1)} %convert_element_type.12, f32[32768]{0:T(1024)S(1)} %broadcast_multiply_fusion), kind=kOutput, calls=%fused_computation.4 | convolution fusion | flops 2524446720 | bytes 10773504 | tf_op jit(solution)/shard_map/dot_general | solution.py:24
  29.2 42.6 %psum.7 = f32[80,80]{1,0:T(8,128)S(1)} all-reduce(f32[80,80]{1,0:T(8,128)S(1)} %fusion.1), channel_id=1, replica_groups=mesh['slab'=32] {'slab'}, use_global_device_ids=true, to_apply=%region_2.3 | all-reduce | flops 6400 | bytes 51200 | tf_op jit(solution)/shard_map/psum | solution.py:25
  71.8 0.0 copy-done.1
  71.8 0.2 fusion.27
  71.9 0.2 fusion.28
  72.1 0.1 copy.13
  72.2 0.4 cholesky.16
  72.6 0.1 select_reduce_fusion.1
  72.7 0.6 compare_reduce_fusion
  73.3 0.6 fusion.19
  74.0 0.4 custom-call.10
  74.4 0.2 fusion.20
  74.6 0.1 fusion.22
  74.7 0.3 fusion.29
  75.0 12.9 %fusion = bf16[80,32768]{1,0:T(8,128)(2,1)S(1)} fusion(f32[80,80]{1,0:T(8,128)S(1)} %fusion.29, f32[80,32768]{1,0:T(8,128)} %param.7, f32[32768]{0:T(1024)S(1)} %broadcast_multiply_fusion), kind=kOutput, calls=%fused_computation.3 | convolution fusion | flops 2524446720 | bytes 15885312 | tf_op jit(solution)/shard_map/dot_general | solution.py:28
  87.9 2.8 %copy.18 = bf16[10,128,8,256]{3,2,0,1:T(8,128)(2,1)} copy(bf16[10,128,8,256]{3,2,1,0:T(8,128)(2,1)S(1)} %bitcast.34) | data formatting | bytes 10485760 | tf_op jit(solution)/shard_map/reshape | solution.py:29
  90.7 4.5 %gather_fusion = bf16[48,80,256]{2,1,0:T(8,128)(2,1)} fusion(bf16[80,128,256]{2,0,1:T(8,128)(2,1)} %bitcast.35, s32[1024]{0:T(1024)S(1)} %pad_clamp_fusion), kind=kCustom, calls=%fused_computation | custom fusion | bytes 3932352 | tf_op jit(solution)/shard_map/jit(_take)/gather | solution.py:30
  95.2 0.0 copy-done
  95.2 3.7 %fusion.15 = f32[48,80,128]{2,1,0:T(8,128)} fusion(bf16[48,256,128]{2,1,0:T(8,128)(2,1)S(1)} %copy-done, bf16[48,80,256]{2,1,0:T(8,128)(2,1)} %gather_fusion, pred[48]{0:T(512)(128)(4,1)S(1)} %compare_and_fusion), kind=kOutput, calls=%fused_computation.17 | convolution fusion | flops 253624320 | bytes 7077936 | tf_op jit(solution)/shard_map/fkv,kvt->kft/dot_general | solution.py:31
  98.9 2.7 %broadcast_in_dim.41 = f32[128,80,128]{2,1,0:T(8,128)} broadcast(f32[]{:T(128)} %constant.78.clone.1), dimensions={} | broadcast | bytes 5242884 | tf_op jit(solution)/shard_map/broadcast_in_dim | solution.py:43
  101.5 8.4 %scatter_fusion = f32[128,80,128]{2,1,0:T(8,128)} fusion(f32[128,80,128]{2,1,0:T(8,128)} %broadcast_in_dim.41, s32[48]{0:T(128)S(1)} %compare_select_fusion.1, f32[48,80,128]{2,1,0:T(8,128)} %fusion.15), kind=kCustom, calls=%fused_computation.1 | custom fusion | flops 491520 | bytes 5898432 | tf_op jit(solution)/shard_map/scatter-add | solution.py:45
  110.0 0.0 reduce-scatter.2.cloned.1.call-update
  110.0 142.8 %reduce-scatter.2.cloned.1.call-done = f32[4,80,128]{2,1,0:T(8,128)} async-done(((f32[128,80,128]{2,1,0:T(8,128)}), f32[4,80,128]{2,1,0:T(8,128)}) %reduce-scatter.2.cloned.1.call-update) | async-done | bytes 163856 | tf_op jit(solution)/shard_map/reduce_scatter | solution.py:44
  (3 shorter events, 0.0 us)
Async XLA Ops:
  6.5 88.7 %copy-start = (bf16[48,256,128]{2,1,0:T(8,128)(2,1)S(1)}, bf16[48,256,128]{2,1,0:T(8,128)(2,1)}, u32[]{:S(2)}) copy-start(bf16[48,256,128]{2,1,0:T(8,128)(2,1)} %param.10) | copy-start | bytes 9437188
  6.5 246.3 %reduce-scatter.2.cloned.1.call-start = ((), (), s32[]{:S(2)}) async-start(), calls=%async_computation.1 | async-start | bytes 5406720 | tf_op jit(solution)/shard_map/reduce_scatter | solution.py:44
  15.3 56.5 %copy-start.1 = (f32[80,5]{0,1:T(8,128)S(1)}, f32[80,5]{0,1:T(8,128)}, u32[]{:S(2)}) copy-start(f32[80,5]{0,1:T(8,128)} %param.9) | copy-start | bytes 4804
Sparse Core Ops, SparseCore 0:
  110.1 142.6 reduce-scatter.1
where the time goes:
time: 260 us
  waiting for transfers between devices  143 us (55%)
  blocking collectives  42.6 us (16%)
  matrix products  31.4 us (12%)
  other arithmetic  19.3 us (7%)
  between operations  13.5 us (5%)
  local copies, waits for them, and re-layouts  10 us (4%)
    reduce_scatter x1, waiting for transfers between devices, body(): lax.psum_scatter(empty.at[target].add(widened, mode='drop'), 'slab', scat...  143 us
    psum x1, blocking collectives, body(): noise_gram = lax.psum(local_gram, 'slab')  42.6 us
    dot_general x1, matrix products, body(): lax.dot_general(weighted, demeaned, (((1,), (1,)), ((), ())), precision=H...  13.9 us
    dot_general x1, matrix products, body(): jnp.dot(projector, demeaned, precision=HIGHEST)  12.9 us
    scatter-add x1, other arithmetic, body(): empty.at[target].add(widened, mode='drop')  8.41 us
  transfers between devices with their start and end apart: 1, of which 1 were waited for; matrix products, arithmetic and copies ran while one was open for 0% of the time, Pallas kernels for 0%

commit v1 on v0

v1 whole, which is shorter than its diff:
```python
import functools

import jax
import jax.numpy as jnp
from jax import lax
from jax.experimental import pallas as pl
from jax.experimental.pallas import tpu as pltpu
from jax.sharding import PartitionSpec as P

AXIS = "slab"
HIGHEST = lax.Precision.HIGHEST
LANES = 128
COEF_ROWS = 8
STEP_BLOCKS = 8


class Plan:
    def __init__(self, devices, tiles, entries, frames, block_width, tile_width):
        self.devices = devices
        self.tiles = tiles
        self.entries = entries
        self.frames = frames
        self.block_width = block_width
        self.tile_width = tile_width
        self.owned = tiles // devices
        self.log = devices.bit_length() - 1
        assert 1 << self.log == devices and self.owned * devices == tiles
        widths = [1]
        while sum(widths) < self.log:
            widths.append(min(2, self.log - sum(widths)))
        self.widths = widths
        self.done = [sum(widths[:i]) for i in range(len(widths) + 1)]
        self.slots = [
            min(self.owned, -(-(self.owned * (1 << b) + entries - 1) // devices))
            for b in self.done
        ]
        self.slots[-1] = self.owned
        self.owners = [devices >> self.done[i + 1] for i in range(len(widths))]

    def rows(self, stage):
        return self.owners[stage] * self.slots[stage] * self.frames + COEF_ROWS

    def position(self, rel, stage):
        place = 0
        for i in range(stage, len(self.widths)):
            digit = (rel >> self.done[i]) & ((1 << self.widths[i]) - 1)
            place = (place << self.widths[i]) | digit
        return place

    def relative(self, place, stage):
        rel = 0
        for i in reversed(range(stage, len(self.widths))):
            rel = rel | ((place & ((1 << self.widths[i]) - 1)) << self.done[i])
            place = place >> self.widths[i]
        return rel


def tile_rows(index, frames):
    return pl.ds(pl.multiple_of(index * frames, 8), frames)


def sample_kernel(
    plan, steps, block_ids, tile_ids, tile_owner, series, mask, probes, weights,
    keep, send, inverse, halves, masked, gram, held, semaphore,
):
    step = pl.program_id(0)
    frames, width = plan.frames, plan.block_width
    columns = series.shape[1]
    weights_copy = pltpu.make_async_copy(weights, held, semaphore)

    @pl.when(step == 0)
    def _():
        weights_copy.start()
        gram[...] = jnp.zeros_like(gram)
        keep[...] = jnp.zeros_like(keep)
        send[...] = jnp.zeros_like(send)

        def note(residue, carry):
            inverse[tile_owner[residue]] = residue
            return carry

        lax.fori_loop(0, plan.devices, note, 0)

    start = step * columns
    for block in range(columns // width):
        place = pl.ds(block * width, width)
        values = series[:, place]
        values = values - jnp.sum(values, axis=0, keepdims=True) * (1.0 / frames)
        high = values.astype(jnp.bfloat16)
        low = (values - high.astype(jnp.float32)).astype(jnp.bfloat16)
        used = mask[:, place].astype(jnp.float32).astype(jnp.bfloat16)
        target = pl.ds(pl.multiple_of(start + block * width, width), width)
        halves[0:frames, target] = high
        halves[frames:, target] = low
        masked[0:frames, place] = high * used
        masked[frames:, place] = low * used
    gram[...] += lax.dot_general(
        masked[...],
        halves[:, pl.ds(pl.multiple_of(start, width), columns)],
        (((1,), (1,)), ((), ())),
        preferred_element_type=jnp.float32,
    )

    @pl.when(step == steps - 1)
    def _():
        device = lax.axis_index(AXIS)
        full = gram[0:frames, 0:frames] + gram[frames:, frames:]
        full = full + gram[0:frames, frames:] + gram[frames:, 0:frames]
        coefs = jnp.dot(
            probes[...], full, precision=HIGHEST, preferred_element_type=jnp.float32
        )
        last = keep.shape[0] - COEF_ROWS
        for out in (keep, send):
            out[pl.ds(last, COEF_ROWS), 0:frames] = coefs
        weights_copy.wait()

        def entry(k, carry):
            tile = tile_ids[k]

            @pl.when(tile >= 0)
            def _():
                columns_of = pl.ds(pl.multiple_of(block_ids[k] * width, width), width)
                both = jnp.dot(
                    halves[:, columns_of], held[k], preferred_element_type=jnp.float32
                )
                total = both[0:frames] + both[frames:]
                rel = tile_owner[tile & (plan.devices - 1)] ^ device
                offset = (tile - device * plan.owned) & (plan.tiles - 1)
                slot = plan.position(rel, 1) * plan.slots[0] + (offset >> plan.log)
                target = tile_rows(slot, frames)

                @pl.when((rel & 1) == 0)
                def _():
                    keep[target, :] = total

                @pl.when((rel & 1) == 1)
                def _():
                    send[target, :] = total

            return carry

        lax.fori_loop(0, plan.entries, entry, 0)


def sample(plan, series, mask, probes, weights, block_ids, tile_ids, tile_owner):
    frames, voxels = series.shape
    columns = STEP_BLOCKS * plan.block_width
    steps = voxels // columns
    smem = pl.BlockSpec(memory_space=pltpu.SMEM)
    block = jax.ShapeDtypeStruct((plan.rows(0), LANES), jnp.float32)
    whole = pl.BlockSpec(block.shape, lambda i: (0, 0), pipeline_mode=pl.Buffered(1))
    return pl.pallas_call(
        functools.partial(sample_kernel, plan, steps),
        name="sample",
        grid=(steps,),
        in_specs=[
            smem,
            smem,
            smem,
            pl.BlockSpec((frames, columns), lambda i: (0, i)),
            pl.BlockSpec((1, columns), lambda i: (0, i)),
            pl.BlockSpec(probes.shape, lambda i: (0, 0)),
            pl.BlockSpec(memory_space=pl.ANY),
        ],
        out_specs=[whole, whole, smem],
        out_shape=[block, block, jax.ShapeDtypeStruct((plan.devices,), jnp.int32)],
        scratch_shapes=[
            pltpu.VMEM((2 * frames, voxels), jnp.bfloat16),
            pltpu.VMEM((2 * frames, columns), jnp.bfloat16),
            pltpu.VMEM((2 * frames, 2 * frames), jnp.float32),
            pltpu.VMEM(weights.shape, weights.dtype),
            pltpu.SemaphoreType.DMA,
        ],
        compiler_params=pltpu.CompilerParams(
            dimension_semantics=("arbitrary",), vmem_limit_bytes=56 << 20
        ),
    )(block_ids, tile_ids, tile_owner, series, mask, probes, weights)


def add_tiles(plan, stage, inverse, sources, place, slot):
    device = lax.axis_index(AXIS)
    done, after = plan.done[stage], plan.done[stage + 1]
    slots, devices, tiles = plan.slots[stage], plan.devices, plan.tiles
    residue = inverse[device ^ plan.relative(place, stage + 1)]
    last = stage + 1 == len(plan.widths)
    base = 0 if last else ((device >> after) << after) * plan.owned
    tile = (base + ((residue - base) & (devices - 1)) + slot * devices) & (tiles - 1)
    total = None
    for digit, source in enumerate(sources):
        sender = device ^ (digit << done)
        first = ((sender >> done) << done) * plan.owned
        offset = (tile - first) & (tiles - 1)
        there = offset < slots * devices
        at = place * slots + jnp.minimum(offset >> plan.log, slots - 1)
        value = source[tile_rows(at, plan.frames), :]
        value = jnp.where(there, value, 0.0)
        total = value if total is None else total + value
    return total


def add_coefs(sources):
    total = None
    for source in sources:
        value = source[pl.ds(source.shape[0] - COEF_ROWS, COEF_ROWS), :]
        total = value if total is None else total + value
    return total


def merge_kernel(plan, stage, inverse, *refs):
    fan = 1 << plan.widths[stage]
    sources, outs = refs[:fan], refs[fan:]
    coefs = add_coefs(sources)
    slots, count = plan.slots[stage + 1], plan.owners[stage + 1]
    for digit, out in enumerate(outs):
        out[pl.ds(out.shape[0] - COEF_ROWS, COEF_ROWS), :] = coefs

        def owner(rest, carry):
            for slot in range(slots):
                value = add_tiles(plan, stage, inverse, sources, digit * count + rest, slot)
                out[tile_rows(rest * slots + slot, plan.frames), :] = value
            return carry

        if count <= 4:
            for rest in range(count):
                owner(rest, 0)
        else:
            lax.fori_loop(0, count, owner, 0)


def merge(plan, stage, inverse, sources):
    fan = 1 << plan.widths[stage + 1]
    block = jax.ShapeDtypeStruct((plan.rows(stage + 1), LANES), jnp.float32)
    vmem = pl.BlockSpec(memory_space=pltpu.VMEM)
    return pl.pallas_call(
        functools.partial(merge_kernel, plan, stage),
        name="merge",
        in_specs=[pl.BlockSpec(memory_space=pltpu.SMEM)] + [vmem] * len(sources),
        out_specs=[vmem] * fan,
        out_shape=[block] * fan,
        compiler_params=pltpu.CompilerParams(vmem_limit_bytes=40 << 20),
    )(inverse, *sources)


def finish_kernel(plan, comps, inverse, *refs):
    stage = len(plan.widths) - 1
    sources, out = refs[:-1], refs[-1]
    frames = plan.frames
    basis = add_coefs(sources)
    lane = lax.broadcasted_iota(jnp.int32, basis.shape, 1)
    row = lax.broadcasted_iota(jnp.int32, basis.shape, 0)
    basis = jnp.where((lane < frames) & (row < comps), basis, 0.0)
    unit = jnp.zeros_like(basis)
    for i in range(comps):
        line = basis[i : i + 1, :]
        line = line * lax.rsqrt(jnp.sum(line * line, axis=1, keepdims=True))
        unit = jnp.where(row == i, line, unit)
        basis = basis - jnp.sum(basis * line, axis=1, keepdims=True) * line
    unit = unit[:, 0:frames]
    for slot in range(plan.owned):
        value = add_tiles(plan, stage, inverse, sources, 0, slot)
        along = jnp.dot(unit, value, precision=HIGHEST, preferred_element_type=jnp.float32)
        out[slot] = value - lax.dot_general(
            unit,
            along,
            (((0,), (0,)), ((), ())),
            precision=HIGHEST,
            preferred_element_type=jnp.float32,
        )


def finish(plan, comps, inverse, sources):
    vmem = pl.BlockSpec(memory_space=pltpu.VMEM)
    return pl.pallas_call(
        functools.partial(finish_kernel, plan, comps),
        name="finish",
        in_specs=[pl.BlockSpec(memory_space=pltpu.SMEM)] + [vmem] * len(sources),
        out_specs=vmem,
        out_shape=jax.ShapeDtypeStruct((plan.owned, plan.frames, plan.tile_width), jnp.float32),
    )(inverse, *sources)


def exchange(plan, stage, blocks):
    received = [blocks[0]]
    for digit in range(1, len(blocks)):
        pairs = [(i, i ^ (digit << plan.done[stage])) for i in range(plan.devices)]
        received.append(lax.ppermute(blocks[digit], AXIS, pairs))
    return received


def body(series, noise_mask, probes, sample_weights, block_ids, tile_ids, tile_owner):
    frames, voxels = series.shape
    entries, block_width, tile_width = sample_weights.shape
    plan = Plan(
        lax.axis_size(AXIS), tile_owner.shape[0], entries, frames, block_width, tile_width
    )
    comps = probes.shape[1]
    rows = jnp.pad(probes.T, ((0, COEF_ROWS - comps), (0, 0)))
    keep, send, inverse = sample(
        plan, series, noise_mask.reshape(1, voxels), rows, sample_weights,
        block_ids, tile_ids, tile_owner,
    )
    blocks = [keep, send]
    for stage in range(len(plan.widths)):
        blocks = exchange(plan, stage, blocks)
        if stage + 1 < len(plan.widths):
            blocks = merge(plan, stage, inverse, blocks)
    return finish(plan, comps, inverse, blocks)


def solution(mesh):
    return jax.shard_map(
        body,
        mesh=mesh,
        in_specs=(
            P(None, AXIS),
            P(AXIS),
            P(),
            P(AXIS, None, None),
            P(AXIS),
            P(AXIS),
            P(),
        ),
        out_specs=P(AXIS, None, None),
        check_vma=False,
    )
```

time: 260 us -> 71 us (0.27)
  waiting for transfers between devices: 143 us -> 27.2 us
  blocking collectives: 42.6 us -> 0 us
  matrix products: 31.4 us -> 0 us
  Pallas kernels: 0 us -> 26 us
  other arithmetic: 19.3 us -> 0 us
  between operations: 13.5 us -> 0.05 us
  starting transfers between devices: 0.01 us -> 12.7 us
  local copies, waits for them, and re-layouts: 10 us -> 4.6 us
    reduce_scatter x1 -> x0, waiting for transfers between devices: 143 us -> none  [body(): lax.psum_scatter(empty.at[target].add(widened, mode='drop'), 'slab', scat...]
    psum x1 -> x0, blocking collectives: 42.6 us -> none  [body(): noise_gram = lax.psum(local_gram, 'slab')]
    dot_general x6 -> x0, matrix products: 31.1 us -> none  [the longest x1 13.9 us: body(): lax.dot_general(weighted, demeaned, (((1,), (1,)), ((), ())), precision=H...]
    ppermute x0 -> x7, waiting for transfers between devices: none -> 27.2 us  [exchange(): received.append(lax.ppermute(blocks[digit], AXIS, pairs))]
    pallas_call x0 -> x4, Pallas kernels: none -> 26 us  [the longest x1 20.9 us: sample(): pl.pallas_call(functools.partial(sample_kernel, plan, steps), name='sampl...]
    ppermute x0 -> x7, starting transfers between devices: none -> 12.7 us  [exchange(): received.append(lax.ppermute(blocks[digit], AXIS, pairs))]
    scatter-add x1 -> x0, other arithmetic: 8.41 us -> none  [body(): empty.at[target].add(widened, mode='drop')]
    reduce_sum x2 -> x0, other arithmetic: 5.51 us -> none  [the longest x1 4.67 us: body(): demeaned = series - jnp.mean(series, axis=0, keepdims=True)]
  transfers between devices with their start and end apart: 1 -> 7, of which waited for: 1 -> 5; matrix products, arithmetic and copies ran while one was open for 0% -> 0% of each run, Pallas kernels for 0% -> 0%
where the time goes in v1:
time: 71 us; the launch traced here: 70.5 us
  waiting for transfers between devices  27.2 us (38%)
  Pallas kernels  26 us (37%)
  starting transfers between devices  12.7 us (18%)
  local copies, waits for them, and re-layouts  4.6 us (6%)
    ppermute x7, waiting for transfers between devices, exchange(): received.append(lax.ppermute(blocks[digit], AXIS, pairs))  27.2 us
    pallas_call x1, Pallas kernels, sample(): pl.pallas_call(functools.partial(sample_kernel, plan, steps), name='sampl...  20.9 us
    ppermute x7, starting transfers between devices, exchange(): received.append(lax.ppermute(blocks[digit], AXIS, pairs))  12.7 us
    pallas_call x1, Pallas kernels, finish(): pl.pallas_call(functools.partial(finish_kernel, plan, comps), name='finis...  3.45 us
    unnamed x12, local copies, waits for them, and re-layouts  3.32 us
    pallas_call x2, Pallas kernels, merge(): pl.pallas_call(functools.partial(merge_kernel, plan, stage), name='merge'...  1.57 us
  transfers between devices with their start and end apart: 7, of which 5 were waited for; matrix products, arithmetic and copies ran while one was open for 0% of the time, Pallas kernels for 0%

profile of v1, /device:TPU:0, one launch (start us, length us, event | category | flops | bytes accessed | tf_op | source)
XLA Modules:
  0.0 70.5 jit_solution(10156133581205098911)
XLA Ops:
  0.0 1.3 %pad.4.probes = f32[8,80]{1,0:T(8,128)} pad(f32[5,80]{1,0:T(8,128)} %bitcast.3, f32[]{:T(128)} %constant.2.clone.1), padding=0_3x0_0 | pad | bytes 4164 | tf_op jit(solution)/shard_map/jit(_pad)/pad | solution.py:297
  1.3 20.9 %sample.1 = (f32[2568,128]{1,0:T(8,128)}, f32[2568,128]{1,0:T(8,128)}, s32[32]{0:T(128)}) custom-call(s32[48]{0:T(128)} %block_ids.1, s32[48]{0:T(128)} %tile_ids.1, s32[128]{0:T(128)} %tile_owner.1, f32[80,32768]{1,0:T(8,128)} %series.1, s32[1,32768]{1,0:T(1,128)} %bitcast.2, f32[8,80]{1,0:T(8,128)} %pad.4.probes, bf16[48,256,128]{2,1,0:T(8,128)(2,1)} %weights.1), custom_call_target="tpu_custom_call" | custom-call | tf_op jit(solution)/shard_map/sample/pallas_call | solution.py:152
  22.2 2.2 %collective-permute-start = (f32[2568,128]{1,0:T(8,128)}, f32[2568,128]{1,0:T(8,128)S(1)}, u32[]{:S(2)}, u32[]{:S(2)}) collective-permute-start(f32[2568,128]{1,0:T(8,128)} %get-tuple-element.18), channel_id=1, source_target_pairs={{0,1},{1,0},{2,3},{3,2},{4,5},{5,4},{6,7},{7,6},{8,9},{9,8},{10,11... | collective-permute-start | bytes 3944456 | tf_op jit(solution)/shard_map/ppermute | solution.py:286
  24.4 2.9 %collective-permute-done.refs_1_ = f32[2568,128]{1,0:T(8,128)S(1)} collective-permute-done((f32[2568,128]{1,0:T(8,128)}, f32[2568,128]{1,0:T(8,128)S(1)}, u32[]{:S(2)}, u32[]{:S(2)}) %collective-permute-start) | collective-permute-done | bytes 1314848 | tf_op jit(solution)/shard_map/ppermute | solution.py:286
  27.3 0.0 copy-start
  27.3 1.3 %copy-done = f32[2568,128]{1,0:T(8,128)S(1)} copy-done((f32[2568,128]{1,0:T(8,128)S(1)}, f32[2568,128]{1,0:T(8,128)}, u32[]{:S(2)}) %copy-start) | copy-done | bytes 1314840
  28.6 0.0 copy-start.2
  28.6 0.7 copy-done.2
  29.3 0.8 %merge.2 = (f32[648,128]{1,0:T(8,128)S(1)}, f32[648,128]{1,0:T(8,128)S(1)}, f32[648,128]{1,0:T(8,128)S(1)}, f32[648,128]{1,0:T(8,128)S(1)}) custom-call(s32[32]{0:T(128)S(1)} %copy-done.2, f32[2568,128]{1,0:T(8,128)S(1)} %copy-done, f32[2568,128]{1,0:T(8,128)S(1)} %collective-permute-done.refs_1_), custom_call_target="tpu_custom_call" | custom-call | tf_op jit(solution)/shard_map/merge/pallas_call | solution.py:234
  30.1 3.1 %collective-permute-start.1 = (f32[648,128]{1,0:T(8,128)S(1)}, f32[648,128]{1,0:T(8,128)S(1)}, u32[]{:S(2)}, u32[]{:S(2)}) collective-permute-start(f32[648,128]{1,0:T(8,128)S(1)} %get-tuple-element.20), channel_id=1, source_target_pairs={{0,2},{1,3},{2,0},{3,1},{4,6},{5,7},{6,4},{7,5},{8,10},{9,11},{10,... | collective-permute-start | bytes 995336 | tf_op jit(solution)/shard_map/ppermute | solution.py:286
  33.2 1.1 %collective-permute-start.2 = (f32[648,128]{1,0:T(8,128)S(1)}, f32[648,128]{1,0:T(8,128)S(1)}, u32[]{:S(2)}, u32[]{:S(2)}) collective-permute-start(f32[648,128]{1,0:T(8,128)S(1)} %get-tuple-element.21), channel_id=1, source_target_pairs={{0,4},{1,5},{2,6},{3,7},{4,0},{5,1},{6,2},{7,3},{8,12},{9,13},{10,... | collective-permute-start | bytes 995336 | tf_op jit(solution)/shard_map/ppermute | solution.py:286
  34.3 1.4 %collective-permute-start.3 = (f32[648,128]{1,0:T(8,128)S(1)}, f32[648,128]{1,0:T(8,128)S(1)}, u32[]{:S(2)}, u32[]{:S(2)}) collective-permute-start(f32[648,128]{1,0:T(8,128)S(1)} %get-tuple-element.22), channel_id=1, source_target_pairs={{0,6},{1,7},{2,4},{3,5},{4,2},{5,3},{6,0},{7,1},{8,14},{9,15},{10,... | collective-permute-start | bytes 995336 | tf_op jit(solution)/shard_map/ppermute | solution.py:286
  35.7 6.2 %collective-permute-done.1.refs_1_ = f32[648,128]{1,0:T(8,128)S(1)} collective-permute-done((f32[648,128]{1,0:T(8,128)S(1)}, f32[648,128]{1,0:T(8,128)S(1)}, u32[]{:S(2)}, u32[]{:S(2)}) %collective-permute-start.1) | collective-permute-done | bytes 331808 | tf_op jit(solution)/shard_map/ppermute | solution.py:286
  41.9 6.9 %collective-permute-done.2.refs_2_ = f32[648,128]{1,0:T(8,128)S(1)} collective-permute-done((f32[648,128]{1,0:T(8,128)S(1)}, f32[648,128]{1,0:T(8,128)S(1)}, u32[]{:S(2)}, u32[]{:S(2)}) %collective-permute-start.2) | collective-permute-done | bytes 331808 | tf_op jit(solution)/shard_map/ppermute | solution.py:286
  48.8 1.8 %collective-permute-done.3.refs_3_ = f32[648,128]{1,0:T(8,128)S(1)} collective-permute-done((f32[648,128]{1,0:T(8,128)S(1)}, f32[648,128]{1,0:T(8,128)S(1)}, u32[]{:S(2)}, u32[]{:S(2)}) %collective-permute-start.3) | collective-permute-done | bytes 331808 | tf_op jit(solution)/shard_map/ppermute | solution.py:286
  50.6 0.7 %merge.3 = (f32[248,128]{1,0:T(8,128)S(1)}, f32[248,128]{1,0:T(8,128)S(1)}, f32[248,128]{1,0:T(8,128)S(1)}, f32[248,128]{1,0:T(8,128)S(1)}) custom-call(s32[32]{0:T(128)S(1)} %copy-done.2, f32[648,128]{1,0:T(8,128)S(1)} %get-tuple-element.19.refs_0_, f32[648,128]{1,0:T(8,128)S(1)} %collective-permute-done.1.refs_1_, ...), custom_call_target="tpu_custom_call" | custom-call | tf_op jit(solution)/shard_map/merge/pallas_call | solution.py:234
  51.3 0.0 copy-start.1
  51.4 0.6 copy-done.1
  52.0 2.0 %collective-permute-start.4 = (f32[248,128]{1,0:T(8,128)S(1)}, f32[248,128]{1,0:T(8,128)S(1)}, u32[]{:S(2)}, u32[]{:S(2)}) collective-permute-start(f32[248,128]{1,0:T(8,128)S(1)} %get-tuple-element.24), channel_id=1, source_target_pairs={{0,8},{1,9},{2,10},{3,11},{4,12},{5,13},{6,14},{7,15},{8,0},{9,1},... | collective-permute-start | bytes 380936 | tf_op jit(solution)/shard_map/ppermute | solution.py:286
  54.0 3.0 %collective-permute-start.5 = (f32[248,128]{1,0:T(8,128)S(1)}, f32[248,128]{1,0:T(8,128)S(1)}, u32[]{:S(2)}, u32[]{:S(2)}) collective-permute-start(f32[248,128]{1,0:T(8,128)S(1)} %get-tuple-element.25), channel_id=1, source_target_pairs={{0,16},{1,17},{2,18},{3,19},{4,20},{5,21},{6,22},{7,23},{8,24},{9,... | collective-permute-start | bytes 380936 | tf_op jit(solution)/shard_map/ppermute | solution.py:286
  57.0 0.0 collective-permute-start.6
  57.0 0.0 collective-permute-done.4.refs_1_
  57.0 0.0 copy-start.3
  57.0 9.4 %collective-permute-done.5.refs_2_ = f32[248,128]{1,0:T(8,128)S(1)} collective-permute-done((f32[248,128]{1,0:T(8,128)S(1)}, f32[248,128]{1,0:T(8,128)S(1)}, u32[]{:S(2)}, u32[]{:S(2)}) %collective-permute-start.5) | collective-permute-done | bytes 127008 | tf_op jit(solution)/shard_map/ppermute | solution.py:286
  66.4 0.0 copy-start.4
  66.4 0.0 collective-permute-done.6.refs_3_
  66.4 0.0 copy-start.5
  66.4 0.0 copy-done.3
  66.4 0.6 copy-done.4
  67.0 0.1 copy-done.5
  67.1 3.5 %finish.1 = f32[4,80,128]{2,1,0:T(8,128)} custom-call(s32[32]{0:T(128)} %get-tuple-element.16.inverse, f32[248,128]{1,0:T(8,128)} %copy-done.1, f32[248,128]{1,0:T(8,128)} %copy-done.3, f32[248,128]{1,0:T(8,128)} %copy-done.4, f32[248,128]{1,0:T(8,128)} %copy-done.5), custom_call_target="tpu_custom_call" | custom-call | tf_op jit(solution)/shard_map/finish/pallas_call | solution.py:273
Async XLA Ops:
  22.2 5.0 %collective-permute-start = (f32[2568,128]{1,0:T(8,128)}, f32[2568,128]{1,0:T(8,128)S(1)}, u32[]{:S(2)}, u32[]{:S(2)}) collective-permute-start(f32[2568,128]{1,0:T(8,128)} %get-tuple-element.18), channel_id=1, source_target_pairs={{0,1},{1,0},{2,3},{3,2},{4,5},{5,4},{6,7},{7,6},{8,9},{9,8},{10,11... | collective-permute-start | bytes 3944456 | tf_op jit(solution)/shard_map/ppermute | solution.py:286
  27.3 1.3 %copy-start = (f32[2568,128]{1,0:T(8,128)S(1)}, f32[2568,128]{1,0:T(8,128)}, u32[]{:S(2)}) copy-start(f32[2568,128]{1,0:T(8,128)} %get-tuple-element.17.refs_0_) | copy-start | bytes 3944452
  28.6 0.7 copy-start.2
  30.1 11.8 %collective-permute-start.1 = (f32[648,128]{1,0:T(8,128)S(1)}, f32[648,128]{1,0:T(8,128)S(1)}, u32[]{:S(2)}, u32[]{:S(2)}) collective-permute-start(f32[648,128]{1,0:T(8,128)S(1)} %get-tuple-element.20), channel_id=1, source_target_pairs={{0,2},{1,3},{2,0},{3,1},{4,6},{5,7},{6,4},{7,5},{8,10},{9,11},{10,... | collective-permute-start | bytes 995336 | tf_op jit(solution)/shard_map/ppermute | solution.py:286
  33.2 15.5 %collective-permute-start.2 = (f32[648,128]{1,0:T(8,128)S(1)}, f32[648,128]{1,0:T(8,128)S(1)}, u32[]{:S(2)}, u32[]{:S(2)}) collective-permute-start(f32[648,128]{1,0:T(8,128)S(1)} %get-tuple-element.21), channel_id=1, source_target_pairs={{0,4},{1,5},{2,6},{3,7},{4,0},{5,1},{6,2},{7,3},{8,12},{9,13},{10,... | collective-permute-start | bytes 995336 | tf_op jit(solution)/shard_map/ppermute | solution.py:286
  34.3 16.3 %collective-permute-start.3 = (f32[648,128]{1,0:T(8,128)S(1)}, f32[648,128]{1,0:T(8,128)S(1)}, u32[]{:S(2)}, u32[]{:S(2)}) collective-permute-start(f32[648,128]{1,0:T(8,128)S(1)} %get-tuple-element.22), channel_id=1, source_target_pairs={{0,6},{1,7},{2,4},{3,5},{4,2},{5,3},{6,0},{7,1},{8,14},{9,15},{10,... | collective-permute-start | bytes 995336 | tf_op jit(solution)/shard_map/ppermute | solution.py:286
  51.3 0.7 copy-start.1
  52.0 5.0 %collective-permute-start.4 = (f32[248,128]{1,0:T(8,128)S(1)}, f32[248,128]{1,0:T(8,128)S(1)}, u32[]{:S(2)}, u32[]{:S(2)}) collective-permute-start(f32[248,128]{1,0:T(8,128)S(1)} %get-tuple-element.24), channel_id=1, source_target_pairs={{0,8},{1,9},{2,10},{3,11},{4,12},{5,13},{6,14},{7,15},{8,0},{9,1},... | collective-permute-start | bytes 380936 | tf_op jit(solution)/shard_map/ppermute | solution.py:286
  54.0 12.4 %collective-permute-start.5 = (f32[248,128]{1,0:T(8,128)S(1)}, f32[248,128]{1,0:T(8,128)S(1)}, u32[]{:S(2)}, u32[]{:S(2)}) collective-permute-start(f32[248,128]{1,0:T(8,128)S(1)} %get-tuple-element.25), channel_id=1, source_target_pairs={{0,16},{1,17},{2,18},{3,19},{4,20},{5,21},{6,22},{7,23},{8,24},{9,... | collective-permute-start | bytes 380936 | tf_op jit(solution)/shard_map/ppermute | solution.py:286
  57.0 9.4 %collective-permute-start.6 = (f32[248,128]{1,0:T(8,128)S(1)}, f32[248,128]{1,0:T(8,128)S(1)}, u32[]{:S(2)}, u32[]{:S(2)}) collective-permute-start(f32[248,128]{1,0:T(8,128)S(1)} %get-tuple-element.26), channel_id=1, source_target_pairs={{0,24},{1,25},{2,26},{3,27},{4,28},{5,29},{6,30},{7,31},{8,16},{9,... | collective-permute-start | bytes 380936 | tf_op jit(solution)/shard_map/ppermute | solution.py:286
  57.0 9.4 %copy-start.3 = (f32[248,128]{1,0:T(8,128)}, f32[248,128]{1,0:T(8,128)S(1)}, u32[]{:S(2)}) copy-start(f32[248,128]{1,0:T(8,128)S(1)} %collective-permute-done.4.refs_1_) | copy-start | bytes 380932
  66.4 0.7 copy-start.4
  66.4 0.7 copy-start.5

commit v2 on v1

v2 whole, which is shorter than its diff:
```python
import functools

import jax
import jax.numpy as jnp
from jax import lax
from jax.experimental import pallas as pl
from jax.experimental.pallas import tpu as pltpu
from jax.sharding import PartitionSpec as P

AXIS = "slab"
HIGHEST = lax.Precision.HIGHEST
LANES = 128
COEF_ROWS = 8
GROUP = 8
WIDE = 256
COEF_STEPS = 4
SAMPLE_VMEM = 56 << 20
COEF_VMEM = 40 << 20


class Plan:
    def __init__(self, devices, tiles, entries, frames, block_width, tile_width):
        self.devices = devices
        self.tiles = tiles
        self.entries = entries
        self.frames = frames
        self.block_width = block_width
        self.tile_width = tile_width
        self.owned = tiles // devices
        self.log = devices.bit_length() - 1
        assert 1 << self.log == devices and self.owned * devices == tiles
        widths = [1]
        while sum(widths) < self.log:
            widths.append(min(2, self.log - sum(widths)))
        self.widths = widths
        self.done = [sum(widths[:i]) for i in range(len(widths) + 1)]
        self.slots = [
            min(self.owned, -(-(self.owned * (1 << b) + entries - 1) // devices))
            for b in self.done
        ]
        self.slots[-1] = self.owned
        self.owners = [devices >> self.done[i + 1] for i in range(len(widths))]

    def rows(self, stage):
        return self.owners[stage] * self.slots[stage] * self.frames

    def position(self, rel, stage):
        place = 0
        for i in range(stage, len(self.widths)):
            digit = (rel >> self.done[i]) & ((1 << self.widths[i]) - 1)
            place = (place << self.widths[i]) | digit
        return place

    def relative(self, place, stage):
        rel = 0
        for i in reversed(range(stage, len(self.widths))):
            rel = rel | ((place & ((1 << self.widths[i]) - 1)) << self.done[i])
            place = place >> self.widths[i]
        return rel


def tile_rows(index, frames):
    return pl.ds(pl.multiple_of(index * frames, 8), frames)


def split(values):
    high = values.astype(jnp.bfloat16)
    low = (values - high.astype(jnp.float32)).astype(jnp.bfloat16)
    return high, low


def demean(values):
    return values - jnp.sum(values, axis=0, keepdims=True) * (1.0 / values.shape[0])


def sample_kernel(
    plan, block_ids, tile_ids, tile_owner, series, weights,
    keep, send, inverse, picked, held, pick_sems, weight_sems,
):
    frames, width = plan.frames, plan.block_width
    groups = plan.entries // GROUP

    def pick(k):
        start = pl.multiple_of(block_ids[k] * width, width)
        return pltpu.make_async_copy(
            series.at[:, pl.ds(start, width)], picked.at[k], pick_sems.at[k]
        )

    def fetch(g):
        span = pl.ds(g * GROUP, GROUP)
        return pltpu.make_async_copy(weights.at[span], held.at[span], weight_sems.at[g])

    def begin(g, carry):
        fetch(g).start()
        for i in range(GROUP):
            pick(g * GROUP + i).start()
        return carry

    lax.fori_loop(0, groups, begin, 0)
    keep[...] = jnp.zeros_like(keep)
    send[...] = jnp.zeros_like(send)
    for residue in range(plan.devices):
        inverse[tile_owner[residue]] = residue
    device = lax.axis_index(AXIS)
    spare = plan.owners[0] * plan.slots[0]

    def group(g, carry):
        fetch(g).wait()
        for i in range(GROUP):
            pick(g * GROUP + i).wait()
        for i in range(GROUP):
            k = g * GROUP + i
            tile = tile_ids[k]
            high, low = split(demean(picked[k]))
            both = jnp.dot(
                jnp.concatenate([high, low], axis=0),
                held[k],
                preferred_element_type=jnp.float32,
            )
            total = both[0:frames] + both[frames:]
            rel = tile_owner[tile & (plan.devices - 1)] ^ device
            offset = (tile - device * plan.owned) & (plan.tiles - 1)
            slot = plan.position(rel, 1) * plan.slots[0] + (offset >> plan.log)
            mine = (rel & 1) == 0
            used = tile >= 0
            to_keep = jnp.where(used & mine, slot, spare)
            to_send = jnp.where(used & jnp.logical_not(mine), slot, spare)
            keep[tile_rows(to_keep, frames), :] = total
            send[tile_rows(to_send, frames), :] = total
        return carry

    lax.fori_loop(0, groups, group, 0)


def sample(plan, series, weights, block_ids, tile_ids, tile_owner):
    frames, width = plan.frames, plan.block_width
    smem = pl.BlockSpec(memory_space=pltpu.SMEM)
    vmem = pl.BlockSpec(memory_space=pltpu.VMEM)
    hbm = pl.BlockSpec(memory_space=pl.ANY)
    block = jax.ShapeDtypeStruct((plan.rows(0) + frames, LANES), jnp.float32)
    return pl.pallas_call(
        functools.partial(sample_kernel, plan),
        name="sample",
        in_specs=[smem, smem, smem, hbm, hbm],
        out_specs=[vmem, vmem, smem],
        out_shape=[block, block, jax.ShapeDtypeStruct((plan.devices,), jnp.int32)],
        scratch_shapes=[
            pltpu.VMEM((plan.entries, frames, width), jnp.float32),
            pltpu.VMEM(weights.shape, weights.dtype),
            pltpu.SemaphoreType.DMA((plan.entries,)),
            pltpu.SemaphoreType.DMA((plan.entries // GROUP,)),
        ],
        compiler_params=pltpu.CompilerParams(vmem_limit_bytes=SAMPLE_VMEM),
    )(
        block_ids, tile_ids, tile_owner,
        pltpu.with_memory_space_constraint(series, pltpu.HBM),
        pltpu.with_memory_space_constraint(weights, pltpu.HBM),
    )


def coef_kernel(
    steps, series, mask, probes, coefs, held, marks, halves, masked, gram, sems, mark_sem
):
    frames = series.shape[0]
    columns = series.shape[1] // steps

    def fetch(step):
        span = pl.ds(pl.multiple_of(step * columns, columns), columns)
        return pltpu.make_async_copy(series.at[:, span], held.at[:, span], sems.at[step])

    mark_copy = pltpu.make_async_copy(mask, marks, mark_sem)
    mark_copy.start()
    for step in range(steps):
        fetch(step).start()
    gram[...] = jnp.zeros_like(gram)
    mark_copy.wait()

    def chunk(step, carry):
        fetch(step).wait()
        start = step * columns
        for at in range(0, columns, WIDE):
            span = pl.ds(pl.multiple_of(start + at, WIDE), WIDE)
            place = pl.ds(at, WIDE)
            high, low = split(demean(held[:, span]))
            used = marks[:, span].astype(jnp.float32).astype(jnp.bfloat16)
            halves[0:frames, place] = high
            halves[frames:, place] = low
            masked[0:frames, place] = high * used
            masked[frames:, place] = low * used
        gram[...] += lax.dot_general(
            masked[...],
            halves[...],
            (((1,), (1,)), ((), ())),
            preferred_element_type=jnp.float32,
        )
        return carry

    lax.fori_loop(0, steps, chunk, 0)
    full = gram[0:frames, 0:frames] + gram[frames:, frames:]
    full = full + gram[0:frames, frames:] + gram[frames:, 0:frames]
    coefs[...] = jnp.zeros_like(coefs)
    coefs[0 : probes.shape[0], 0:frames] = jnp.dot(
        probes[...], full, precision=HIGHEST, preferred_element_type=jnp.float32
    )


def local_coefs(series, noise_mask, probes):
    frames, voxels = series.shape
    columns = voxels // COEF_STEPS
    vmem = pl.BlockSpec(memory_space=pltpu.VMEM)
    hbm = pl.BlockSpec(memory_space=pl.ANY)
    return pl.pallas_call(
        functools.partial(coef_kernel, COEF_STEPS),
        name="coefs",
        in_specs=[hbm, hbm, vmem],
        out_specs=vmem,
        out_shape=jax.ShapeDtypeStruct((COEF_ROWS, LANES), jnp.float32),
        scratch_shapes=[
            pltpu.VMEM(series.shape, series.dtype),
            pltpu.VMEM((1, voxels), noise_mask.dtype),
            pltpu.VMEM((2 * frames, columns), jnp.bfloat16),
            pltpu.VMEM((2 * frames, columns), jnp.bfloat16),
            pltpu.VMEM((2 * frames, 2 * frames), jnp.float32),
            pltpu.SemaphoreType.DMA((COEF_STEPS,)),
            pltpu.SemaphoreType.DMA,
        ],
        compiler_params=pltpu.CompilerParams(vmem_limit_bytes=COEF_VMEM),
        cost_estimate=pl.CostEstimate(
            flops=8 * frames * frames * voxels,
            bytes_accessed=4 * frames * voxels,
            transcendentals=0,
        ),
    )(
        pltpu.with_memory_space_constraint(series, pltpu.HBM),
        pltpu.with_memory_space_constraint(noise_mask.reshape(1, voxels), pltpu.HBM),
        probes.T,
    )


def add_tiles(plan, stage, inverse, sources, place, slot):
    device = lax.axis_index(AXIS)
    done, after = plan.done[stage], plan.done[stage + 1]
    slots, devices, tiles = plan.slots[stage], plan.devices, plan.tiles
    residue = inverse[device ^ plan.relative(place, stage + 1)]
    last = stage + 1 == len(plan.widths)
    base = 0 if last else ((device >> after) << after) * plan.owned
    tile = (base + ((residue - base) & (devices - 1)) + slot * devices) & (tiles - 1)
    total = None
    for digit, source in enumerate(sources):
        sender = device ^ (digit << done)
        first = ((sender >> done) << done) * plan.owned
        offset = (tile - first) & (tiles - 1)
        there = offset < slots * devices
        at = place * slots + jnp.minimum(offset >> plan.log, slots - 1)
        value = source[tile_rows(at, plan.frames), :]
        value = jnp.where(there, value, 0.0)
        total = value if total is None else total + value
    return total


def merge_kernel(plan, stage, inverse, *refs):
    fan = 1 << plan.widths[stage]
    sources, outs = refs[:fan], refs[fan:]
    slots, count = plan.slots[stage + 1], plan.owners[stage + 1]
    for digit, out in enumerate(outs):

        def owner(rest, carry):
            for slot in range(slots):
                value = add_tiles(plan, stage, inverse, sources, digit * count + rest, slot)
                out[tile_rows(rest * slots + slot, plan.frames), :] = value
            return carry

        if count <= 4:
            for rest in range(count):
                owner(rest, 0)
        else:
            lax.fori_loop(0, count, owner, 0)


def merge(plan, stage, inverse, sources):
    fan = 1 << plan.widths[stage + 1]
    block = jax.ShapeDtypeStruct((plan.rows(stage + 1), LANES), jnp.float32)
    vmem = pl.BlockSpec(memory_space=pltpu.VMEM)
    return pl.pallas_call(
        functools.partial(merge_kernel, plan, stage),
        name="merge",
        in_specs=[pl.BlockSpec(memory_space=pltpu.SMEM)] + [vmem] * len(sources),
        out_specs=[vmem] * fan,
        out_shape=[block] * fan,
        compiler_params=pltpu.CompilerParams(vmem_limit_bytes=40 << 20),
    )(inverse, *sources)


def finish_kernel(plan, comps, inverse, coefs, *refs):
    stage = len(plan.widths) - 1
    sources, out = refs[:-1], refs[-1]
    frames = plan.frames
    basis = coefs[...]
    lane = lax.broadcasted_iota(jnp.int32, basis.shape, 1)
    row = lax.broadcasted_iota(jnp.int32, basis.shape, 0)
    basis = jnp.where((lane < frames) & (row < comps), basis, 0.0)
    unit = jnp.zeros_like(basis)
    for i in range(comps):
        line = basis[i : i + 1, :]
        line = line * lax.rsqrt(jnp.sum(line * line, axis=1, keepdims=True))
        unit = jnp.where(row == i, line, unit)
        basis = basis - jnp.sum(basis * line, axis=1, keepdims=True) * line
    unit = unit[:, 0:frames]
    for slot in range(plan.owned):
        value = add_tiles(plan, stage, inverse, sources, 0, slot)
        along = jnp.dot(unit, value, precision=HIGHEST, preferred_element_type=jnp.float32)
        out[slot] = value - lax.dot_general(
            unit,
            along,
            (((0,), (0,)), ((), ())),
            precision=HIGHEST,
            preferred_element_type=jnp.float32,
        )


def finish(plan, comps, inverse, coefs, sources):
    vmem = pl.BlockSpec(memory_space=pltpu.VMEM)
    return pl.pallas_call(
        functools.partial(finish_kernel, plan, comps),
        name="finish",
        in_specs=[pl.BlockSpec(memory_space=pltpu.SMEM)] + [vmem] * (1 + len(sources)),
        out_specs=vmem,
        out_shape=jax.ShapeDtypeStruct((plan.owned, plan.frames, plan.tile_width), jnp.float32),
    )(inverse, coefs, *sources)


def exchange(plan, stage, blocks):
    received = [blocks[0]]
    for digit in range(1, len(blocks)):
        pairs = [(i, i ^ (digit << plan.done[stage])) for i in range(plan.devices)]
        received.append(lax.ppermute(blocks[digit], AXIS, pairs))
    return received


def body(series, noise_mask, probes, sample_weights, block_ids, tile_ids, tile_owner):
    frames, voxels = series.shape
    entries, block_width, tile_width = sample_weights.shape
    plan = Plan(
        lax.axis_size(AXIS), tile_owner.shape[0], entries, frames, block_width, tile_width
    )
    keep, send, inverse = sample(
        plan, series, sample_weights, block_ids, tile_ids, tile_owner
    )
    blocks = exchange(plan, 0, [keep, send])
    blocks = merge(plan, 0, inverse, blocks)
    coefs = local_coefs(series, noise_mask, probes)
    for stage in range(len(plan.widths)):
        coefs = sum(exchange(plan, stage, [coefs] * (1 << plan.widths[stage])))
    for stage in range(1, len(plan.widths)):
        blocks = exchange(plan, stage, blocks)
        if stage + 1 < len(plan.widths):
            blocks = merge(plan, stage, inverse, blocks)
    return finish(plan, probes.shape[1], inverse, coefs, blocks)


def solution(mesh):
    return jax.shard_map(
        body,
        mesh=mesh,
        in_specs=(
            P(None, AXIS),
            P(AXIS),
            P(),
            P(AXIS, None, None),
            P(AXIS),
            P(AXIS),
            P(),
        ),
        out_specs=P(AXIS, None, None),
        check_vma=False,
    )
```

time: 71 us -> 56.9 us (0.80)
  waiting for transfers between devices: 27.2 us -> 15.3 us
  Pallas kernels: 26 us -> 18.7 us
  starting transfers between devices: 12.7 us -> 18.7 us
  local copies, waits for them, and re-layouts: 4.6 us -> 3.34 us
    ppermute x7 -> x14, waiting for transfers between devices: 27.2 us -> 15.3 us  [exchange(): received.append(lax.ppermute(blocks[digit], AXIS, pairs))]
    pallas_call x1 -> x2, Pallas kernels: 20.9 us -> 13.7 us  [the longest x1 7.45 us: local_coefs(): pl.pallas_call(functools.partial(coef_kernel, COEF_STEPS), name='coefs',...]
    ppermute x7 -> x14, starting transfers between devices: 12.7 us -> 18.7 us  [exchange(): received.append(lax.ppermute(blocks[digit], AXIS, pairs))]
    pad x1 -> x0, local copies, waits for them, and re-layouts: 1.28 us -> none  [body(): rows = jnp.pad(probes.T, ((0, COEF_ROWS - comps), (0, 0)))]
    unnamed x12 -> x14, local copies, waits for them, and re-layouts: 3.32 us -> 3.34 us
  transfers between devices with their start and end apart: 7 -> 14, of which waited for: 5 -> 6; matrix products, arithmetic and copies ran while one was open for 0% -> 1% of each run, Pallas kernels for 0% -> 14%
where the time goes in v2:
time: 56.9 us; the launch traced here: 56.7 us
  Pallas kernels  18.7 us (33%)
  starting transfers between devices  18.7 us (33%)
  waiting for transfers between devices  15.3 us (27%)
  local copies, waits for them, and re-layouts  3.34 us (6%)
  other arithmetic  0.6 us (1%)
    ppermute x14, starting transfers between devices, exchange(): received.append(lax.ppermute(blocks[digit], AXIS, pairs))  18.7 us
    ppermute x14, waiting for transfers between devices, exchange(): received.append(lax.ppermute(blocks[digit], AXIS, pairs))  15.3 us
    pallas_call x1, Pallas kernels, local_coefs(): pl.pallas_call(functools.partial(coef_kernel, COEF_STEPS), name='coefs',...  7.45 us
    pallas_call x1, Pallas kernels, sample(): pl.pallas_call(functools.partial(sample_kernel, plan), name='sample', in_...  6.22 us
    pallas_call x1, Pallas kernels, finish(): pl.pallas_call(functools.partial(finish_kernel, plan, comps), name='finis...  3.45 us
    unnamed x14, local copies, waits for them, and re-layouts  3.34 us
    pallas_call x2, Pallas kernels, merge(): pl.pallas_call(functools.partial(merge_kernel, plan, stage), name='merge'...  1.57 us
  transfers between devices with their start and end apart: 14, of which 6 were waited for; matrix products, arithmetic and copies ran while one was open for 1% of the time, Pallas kernels for 14%

profile of v2, /device:TPU:0, one launch (start us, length us, event | category | flops | bytes accessed | tf_op | source)
XLA Modules:
  0.0 56.7 jit_solution(3091830797857158946)
XLA Ops:
  0.0 6.2 %sample.1 = (f32[2640,128]{1,0:T(8,128)}, f32[2640,128]{1,0:T(8,128)}, s32[32]{0:T(128)}) custom-call(s32[48]{0:T(128)} %block_ids.1, s32[48]{0:T(128)} %tile_ids.1, s32[128]{0:T(128)} %tile_owner.1, f32[80,32768]{1,0:T(8,128)} %series.3, bf16[48,256,128]{2,1,0:T(8,128)(2,1)} %weights.1), custom_call_target="tpu_custom_call" | custom-call | tf_op jit(solution)/shard_map/sample/pallas_call | solution.py:141
  6.2 0.5 collective-permute-start.7
  6.7 2.9 %collective-permute-done.7.refs_1_ = f32[2640,128]{1,0:T(8,128)S(1)} collective-permute-done((f32[2640,128]{1,0:T(8,128)}, f32[2640,128]{1,0:T(8,128)S(1)}, u32[]{:S(2)}, u32[]{:S(2)}) %collective-permute-start.7) | collective-permute-done | bytes 1351712 | tf_op jit(solution)/shard_map/ppermute | solution.py:336
  9.7 1.3 %copy-done = f32[2640,128]{1,0:T(8,128)S(1)} copy-done((f32[2640,128]{1,0:T(8,128)S(1)}, f32[2640,128]{1,0:T(8,128)}, u32[]{:S(2)}) %copy-start) | copy-done | bytes 1351704
  11.0 0.7 %copy-done.2 = s32[32]{0:T(128)S(1)} copy-done((s32[32]{0:T(128)S(1)}, s32[32]{0:T(128)}, u32[]{:S(2)}) %copy-start.2) | copy-done | bytes 152
  11.7 0.8 %merge.2 = (f32[640,128]{1,0:T(8,128)S(1)}, f32[640,128]{1,0:T(8,128)S(1)}, f32[640,128]{1,0:T(8,128)S(1)}, f32[640,128]{1,0:T(8,128)S(1)}) custom-call(s32[32]{0:T(128)S(1)} %copy-done.2, f32[2640,128]{1,0:T(8,128)S(1)} %copy-done, f32[2640,128]{1,0:T(8,128)S(1)} %collective-permute-done.7.refs_1_), custom_call_target="tpu_custom_call" | custom-call | tf_op jit(solution)/shard_map/merge/pallas_call | solution.py:284
  12.5 2.9 %collective-permute-start.8 = (f32[640,128]{1,0:T(8,128)S(1)}, f32[640,128]{1,0:T(8,128)S(1)}, u32[]{:S(2)}, u32[]{:S(2)}) collective-permute-start(f32[640,128]{1,0:T(8,128)S(1)} %get-tuple-element.20), channel_id=1, source_target_pairs={{0,2},{1,3},{2,0},{3,1},{4,6},{5,7},{6,4},{7,5},{8,10},{9,11},{10,... | collective-permute-start | bytes 983048 | tf_op jit(solution)/shard_map/ppermute | solution.py:336
  15.5 1.5 %collective-permute-start.9 = (f32[640,128]{1,0:T(8,128)S(1)}, f32[640,128]{1,0:T(8,128)S(1)}, u32[]{:S(2)}, u32[]{:S(2)}) collective-permute-start(f32[640,128]{1,0:T(8,128)S(1)} %get-tuple-element.21), channel_id=1, source_target_pairs={{0,4},{1,5},{2,6},{3,7},{4,0},{5,1},{6,2},{7,3},{8,12},{9,13},{10,... | collective-permute-start | bytes 983048 | tf_op jit(solution)/shard_map/ppermute | solution.py:336
  17.0 0.0 collective-permute-start.10
  17.0 7.5 %coefs.1 = f32[8,128]{1,0:T(8,128)S(1)} custom-call(f32[80,32768]{1,0:T(8,128)} %series.3, s32[1,32768]{1,0:T(1,128)} %bitcast.3, f32[5,80]{1,0:T(8,128)S(1)} %bitcast.2), custom_call_target="tpu_custom_call" | custom-call | flops 1677721600 | bytes 10485760 | tf_op jit(solution)/shard_map/coefs/pallas_call | solution.py:212
  24.5 0.1 collective-permute-start
  24.5 1.2 %collective-permute-done = f32[8,128]{1,0:T(8,128)S(1)} collective-permute-done((f32[8,128]{1,0:T(8,128)S(1)}, f32[8,128]{1,0:T(8,128)S(1)}, u32[]{:S(2)}, u32[]{:S(2)}) %collective-permute-start) | collective-permute-done | bytes 4128 | tf_op jit(solution)/shard_map/ppermute | solution.py:336
  25.7 2.9 %collective-permute-start.3 = (f32[8,128]{1,0:T(8,128)S(1)}, f32[8,128]{1,0:T(8,128)S(1)}, u32[]{:S(2)}, u32[]{:S(2)}) collective-permute-start(f32[8,128]{1,0:T(8,128)S(1)} %add.21), channel_id=1, source_target_pairs={{0,6},{1,7},{2,4},{3,5},{4,2},{5,3},{6,0},{7,1},{8,14},{9,15},{10,... | collective-permute-start | bytes 12296 | tf_op jit(solution)/shard_map/ppermute | solution.py:336
  28.6 0.5 collective-permute-start.2
  29.1 2.8 %collective-permute-done.3 = f32[8,128]{1,0:T(8,128)S(1)} collective-permute-done((f32[8,128]{1,0:T(8,128)S(1)}, f32[8,128]{1,0:T(8,128)S(1)}, u32[]{:S(2)}, u32[]{:S(2)}) %collective-permute-start.3) | collective-permute-done | bytes 4128 | tf_op jit(solution)/shard_map/ppermute | solution.py:336
  31.9 1.5 %collective-permute-start.1 = (f32[8,128]{1,0:T(8,128)S(1)}, f32[8,128]{1,0:T(8,128)S(1)}, u32[]{:S(2)}, u32[]{:S(2)}) collective-permute-start(f32[8,128]{1,0:T(8,128)S(1)} %add.21), channel_id=1, source_target_pairs={{0,2},{1,3},{2,0},{3,1},{4,6},{5,7},{6,4},{7,5},{8,10},{9,11},{10,... | collective-permute-start | bytes 12296 | tf_op jit(solution)/shard_map/ppermute | solution.py:336
  33.4 2.1 %collective-permute-done.1 = f32[8,128]{1,0:T(8,128)S(1)} collective-permute-done((f32[8,128]{1,0:T(8,128)S(1)}, f32[8,128]{1,0:T(8,128)S(1)}, u32[]{:S(2)}, u32[]{:S(2)}) %collective-permute-start.1) | collective-permute-done | bytes 4128 | tf_op jit(solution)/shard_map/ppermute | solution.py:336
  35.5 3.6 %collective-permute-start.6 = (f32[8,128]{1,0:T(8,128)S(1)}, f32[8,128]{1,0:T(8,128)S(1)}, u32[]{:S(2)}, u32[]{:S(2)}) collective-permute-start(f32[8,128]{1,0:T(8,128)S(1)} %add_add_fusion.1), channel_id=1, source_target_pairs={{0,24},{1,25},{2,26},{3,27},{4,28},{5,29},{6,30},{7,31},{8,16},{9,... | collective-permute-start | bytes 12296 | tf_op jit(solution)/shard_map/ppermute | solution.py:336
  39.1 0.8 %collective-permute-start.4 = (f32[8,128]{1,0:T(8,128)S(1)}, f32[8,128]{1,0:T(8,128)S(1)}, u32[]{:S(2)}, u32[]{:S(2)}) collective-permute-start(f32[8,128]{1,0:T(8,128)S(1)} %add_add_fusion.1), channel_id=1, source_target_pairs={{0,8},{1,9},{2,10},{3,11},{4,12},{5,13},{6,14},{7,15},{8,0},{9,1},... | collective-permute-start | bytes 12296 | tf_op jit(solution)/shard_map/ppermute | solution.py:336
  39.9 0.0 collective-permute-done.9.refs_2_
  39.9 0.0 collective-permute-done.10.refs_3_
  39.9 0.7 %merge.3 = (f32[240,128]{1,0:T(8,128)S(1)}, f32[240,128]{1,0:T(8,128)S(1)}, f32[240,128]{1,0:T(8,128)S(1)}, f32[240,128]{1,0:T(8,128)S(1)}) custom-call(s32[32]{0:T(128)S(1)} %copy-done.2, f32[640,128]{1,0:T(8,128)S(1)} %get-tuple-element.19.refs_0_, f32[640,128]{1,0:T(8,128)S(1)} %collective-permute-done.8.refs_1_, ...), custom_call_target="tpu_custom_call" | custom-call | tf_op jit(solution)/shard_map/merge/pallas_call | solution.py:284
  40.7 0.6 %copy-done.1 = f32[240,128]{1,0:T(8,128)} copy-done((f32[240,128]{1,0:T(8,128)}, f32[240,128]{1,0:T(8,128)S(1)}, u32[]{:S(2)}) %copy-start.1) | copy-done | bytes 122904
  41.3 1.2 %collective-permute-start.11 = (f32[240,128]{1,0:T(8,128)S(1)}, f32[240,128]{1,0:T(8,128)S(1)}, u32[]{:S(2)}, u32[]{:S(2)}) collective-permute-start(f32[240,128]{1,0:T(8,128)S(1)} %get-tuple-element.24), channel_id=1, source_target_pairs={{0,8},{1,9},{2,10},{3,11},{4,12},{5,13},{6,14},{7,15},{8,0},{9,1},... | collective-permute-start | bytes 368648 | tf_op jit(solution)/shard_map/ppermute | solution.py:336
  42.5 2.9 %collective-permute-start.12 = (f32[240,128]{1,0:T(8,128)S(1)}, f32[240,128]{1,0:T(8,128)S(1)}, u32[]{:S(2)}, u32[]{:S(2)}) collective-permute-start(f32[240,128]{1,0:T(8,128)S(1)} %get-tuple-element.25), channel_id=1, source_target_pairs={{0,16},{1,17},{2,18},{3,19},{4,20},{5,21},{6,22},{7,23},{8,24},{9,... | collective-permute-start | bytes 368648 | tf_op jit(solution)/shard_map/ppermute | solution.py:336
  45.5 0.2 collective-permute-start.13
  45.7 0.6 %add_add_fusion.coefs = f32[8,128]{1,0:T(8,128)} fusion(f32[8,128]{1,0:T(8,128)S(1)} %collective-permute-done.6, f32[8,128]{1,0:T(8,128)S(1)} %collective-permute-done.5, f32[8,128]{1,0:T(8,128)S(1)} %add_add_fusion.1, f32[8,128]{1,0:T(8,128)S(1)} %collective-permute-done.4), kind=kLoop, calls=%fused_computation | loop fusion | flops 3072 | bytes 20480 | tf_op jit(solution)/shard_map/add | solution.py:353
  46.3 0.1 collective-permute-done.11.refs_1_
  46.4 6.2 %collective-permute-done.12.refs_2_ = f32[240,128]{1,0:T(8,128)S(1)} collective-permute-done((f32[240,128]{1,0:T(8,128)S(1)}, f32[240,128]{1,0:T(8,128)S(1)}, u32[]{:S(2)}, u32[]{:S(2)}) %collective-permute-start.12) | collective-permute-done | bytes 122912 | tf_op jit(solution)/shard_map/ppermute | solution.py:336
  52.6 0.6 %copy-done.5 = f32[240,128]{1,0:T(8,128)} copy-done((f32[240,128]{1,0:T(8,128)}, f32[240,128]{1,0:T(8,128)S(1)}, u32[]{:S(2)}) %copy-start.5) | copy-done | bytes 122904
  53.2 0.1 copy-done.6
  53.3 3.4 %finish.1 = f32[4,80,128]{2,1,0:T(8,128)} custom-call(s32[32]{0:T(128)} %get-tuple-element.16.inverse, f32[8,128]{1,0:T(8,128)} %add_add_fusion.coefs, f32[240,128]{1,0:T(8,128)} %copy-done.1, f32[240,128]{1,0:T(8,128)} %copy-done.4, f32[240,128]{1,0:T(8,128)} %copy-done.5, f32[240,128]{1,0:T(8,128)} %copy-done.6), custom_call_target="tpu_custom_call" | custom-call | tf_op jit(solution)/shard_map/finish/pallas_call | solution.py:323
  (18 shorter events, 0.0 us)
Async XLA Ops:
  6.2 3.4 %collective-permute-start.7 = (f32[2640,128]{1,0:T(8,128)}, f32[2640,128]{1,0:T(8,128)S(1)}, u32[]{:S(2)}, u32[]{:S(2)}) collective-permute-start(f32[2640,128]{1,0:T(8,128)} %get-tuple-element.18), channel_id=1, source_target_pairs={{0,1},{1,0},{2,3},{3,2},{4,5},{5,4},{6,7},{7,6},{8,9},{9,8},{10,11... | collective-permute-start | bytes 4055048 | tf_op jit(solution)/shard_map/ppermute | solution.py:336
  9.7 1.3 %copy-start = (f32[2640,128]{1,0:T(8,128)S(1)}, f32[2640,128]{1,0:T(8,128)}, u32[]{:S(2)}) copy-start(f32[2640,128]{1,0:T(8,128)} %get-tuple-element.17.refs_0_) | copy-start | bytes 4055044
  11.0 0.7 %copy-start.2 = (s32[32]{0:T(128)S(1)}, s32[32]{0:T(128)}, u32[]{:S(2)}) copy-start(s32[32]{0:T(128)} %get-tuple-element.16.inverse) | copy-start | bytes 388
  11.7 5.3 %copy-start.3 = (f32[80,5]{0,1:T(8,128)S(1)}, f32[80,5]{0,1:T(8,128)}, u32[]{:S(2)}) copy-start(f32[80,5]{0,1:T(8,128)} %param.9) | copy-start | bytes 4804
  12.5 26.6 %collective-permute-start.8 = (f32[640,128]{1,0:T(8,128)S(1)}, f32[640,128]{1,0:T(8,128)S(1)}, u32[]{:S(2)}, u32[]{:S(2)}) collective-permute-start(f32[640,128]{1,0:T(8,128)S(1)} %get-tuple-element.20), channel_id=1, source_target_pairs={{0,2},{1,3},{2,0},{3,1},{4,6},{5,7},{6,4},{7,5},{8,10},{9,11},{10,... | collective-permute-start | bytes 983048 | tf_op jit(solution)/shard_map/ppermute | solution.py:336
  15.5 24.4 %collective-permute-start.9 = (f32[640,128]{1,0:T(8,128)S(1)}, f32[640,128]{1,0:T(8,128)S(1)}, u32[]{:S(2)}, u32[]{:S(2)}) collective-permute-start(f32[640,128]{1,0:T(8,128)S(1)} %get-tuple-element.21), channel_id=1, source_target_pairs={{0,4},{1,5},{2,6},{3,7},{4,0},{5,1},{6,2},{7,3},{8,12},{9,13},{10,... | collective-permute-start | bytes 983048 | tf_op jit(solution)/shard_map/ppermute | solution.py:336
  17.0 22.9 %collective-permute-start.10 = (f32[640,128]{1,0:T(8,128)S(1)}, f32[640,128]{1,0:T(8,128)S(1)}, u32[]{:S(2)}, u32[]{:S(2)}) collective-permute-start(f32[640,128]{1,0:T(8,128)S(1)} %get-tuple-element.22), channel_id=1, source_target_pairs={{0,6},{1,7},{2,4},{3,5},{4,2},{5,3},{6,0},{7,1},{8,14},{9,15},{10,... | collective-permute-start | bytes 983048 | tf_op jit(solution)/shard_map/ppermute | solution.py:336
  24.5 1.2 %collective-permute-start = (f32[8,128]{1,0:T(8,128)S(1)}, f32[8,128]{1,0:T(8,128)S(1)}, u32[]{:S(2)}, u32[]{:S(2)}) collective-permute-start(f32[8,128]{1,0:T(8,128)S(1)} %coefs.1), channel_id=1, source_target_pairs={{0,1},{1,0},{2,3},{3,2},{4,5},{5,4},{6,7},{7,6},{8,9},{9,8},{10,11... | collective-permute-start | bytes 12296 | tf_op jit(solution)/shard_map/ppermute | solution.py:336
  25.7 6.2 %collective-permute-start.3 = (f32[8,128]{1,0:T(8,128)S(1)}, f32[8,128]{1,0:T(8,128)S(1)}, u32[]{:S(2)}, u32[]{:S(2)}) collective-permute-start(f32[8,128]{1,0:T(8,128)S(1)} %add.21), channel_id=1, source_target_pairs={{0,6},{1,7},{2,4},{3,5},{4,2},{5,3},{6,0},{7,1},{8,14},{9,15},{10,... | collective-permute-start | bytes 12296 | tf_op jit(solution)/shard_map/ppermute | solution.py:336
  28.6 4.8 %collective-permute-start.2 = (f32[8,128]{1,0:T(8,128)S(1)}, f32[8,128]{1,0:T(8,128)S(1)}, u32[]{:S(2)}, u32[]{:S(2)}) collective-permute-start(f32[8,128]{1,0:T(8,128)S(1)} %add.21), channel_id=1, source_target_pairs={{0,4},{1,5},{2,6},{3,7},{4,0},{5,1},{6,2},{7,3},{8,12},{9,13},{10,... | collective-permute-start | bytes 12296 | tf_op jit(solution)/shard_map/ppermute | solution.py:336
  31.9 3.6 %collective-permute-start.1 = (f32[8,128]{1,0:T(8,128)S(1)}, f32[8,128]{1,0:T(8,128)S(1)}, u32[]{:S(2)}, u32[]{:S(2)}) collective-permute-start(f32[8,128]{1,0:T(8,128)S(1)} %add.21), channel_id=1, source_target_pairs={{0,2},{1,3},{2,0},{3,1},{4,6},{5,7},{6,4},{7,5},{8,10},{9,11},{10,... | collective-permute-start | bytes 12296 | tf_op jit(solution)/shard_map/ppermute | solution.py:336
  35.5 10.0 %collective-permute-start.6 = (f32[8,128]{1,0:T(8,128)S(1)}, f32[8,128]{1,0:T(8,128)S(1)}, u32[]{:S(2)}, u32[]{:S(2)}) collective-permute-start(f32[8,128]{1,0:T(8,128)S(1)} %add_add_fusion.1), channel_id=1, source_target_pairs={{0,24},{1,25},{2,26},{3,27},{4,28},{5,29},{6,30},{7,31},{8,16},{9,... | collective-permute-start | bytes 12296 | tf_op jit(solution)/shard_map/ppermute | solution.py:336
  39.1 6.6 %collective-permute-start.5 = (f32[8,128]{1,0:T(8,128)S(1)}, f32[8,128]{1,0:T(8,128)S(1)}, u32[]{:S(2)}, u32[]{:S(2)}) collective-permute-start(f32[8,128]{1,0:T(8,128)S(1)} %add_add_fusion.1), channel_id=1, source_target_pairs={{0,16},{1,17},{2,18},{3,19},{4,20},{5,21},{6,22},{7,23},{8,24},{9,... | collective-permute-start | bytes 12296 | tf_op jit(solution)/shard_map/ppermute | solution.py:336
  39.1 6.6 %collective-permute-start.4 = (f32[8,128]{1,0:T(8,128)S(1)}, f32[8,128]{1,0:T(8,128)S(1)}, u32[]{:S(2)}, u32[]{:S(2)}) collective-permute-start(f32[8,128]{1,0:T(8,128)S(1)} %add_add_fusion.1), channel_id=1, source_target_pairs={{0,8},{1,9},{2,10},{3,11},{4,12},{5,13},{6,14},{7,15},{8,0},{9,1},... | collective-permute-start | bytes 12296 | tf_op jit(solution)/shard_map/ppermute | solution.py:336
  40.6 0.6 %copy-start.1 = (f32[240,128]{1,0:T(8,128)}, f32[240,128]{1,0:T(8,128)S(1)}, u32[]{:S(2)}) copy-start(f32[240,128]{1,0:T(8,128)S(1)} %get-tuple-element.23.refs_0_) | copy-start | bytes 368644
  41.3 5.1 %collective-permute-start.11 = (f32[240,128]{1,0:T(8,128)S(1)}, f32[240,128]{1,0:T(8,128)S(1)}, u32[]{:S(2)}, u32[]{:S(2)}) collective-permute-start(f32[240,128]{1,0:T(8,128)S(1)} %get-tuple-element.24), channel_id=1, source_target_pairs={{0,8},{1,9},{2,10},{3,11},{4,12},{5,13},{6,14},{7,15},{8,0},{9,1},... | collective-permute-start | bytes 368648 | tf_op jit(solution)/shard_map/ppermute | solution.py:336
  42.5 10.0 %collective-permute-start.12 = (f32[240,128]{1,0:T(8,128)S(1)}, f32[240,128]{1,0:T(8,128)S(1)}, u32[]{:S(2)}, u32[]{:S(2)}) collective-permute-start(f32[240,128]{1,0:T(8,128)S(1)} %get-tuple-element.25), channel_id=1, source_target_pairs={{0,16},{1,17},{2,18},{3,19},{4,20},{5,21},{6,22},{7,23},{8,24},{9,... | collective-permute-start | bytes 368648 | tf_op jit(solution)/shard_map/ppermute | solution.py:336
  45.5 7.1 %collective-permute-start.13 = (f32[240,128]{1,0:T(8,128)S(1)}, f32[240,128]{1,0:T(8,128)S(1)}, u32[]{:S(2)}, u32[]{:S(2)}) collective-permute-start(f32[240,128]{1,0:T(8,128)S(1)} %get-tuple-element.26), channel_id=1, source_target_pairs={{0,24},{1,25},{2,26},{3,27},{4,28},{5,29},{6,30},{7,31},{8,16},{9,... | collective-permute-start | bytes 368648 | tf_op jit(solution)/shard_map/ppermute | solution.py:336
  46.4 6.2 %copy-start.4 = (f32[240,128]{1,0:T(8,128)}, f32[240,128]{1,0:T(8,128)S(1)}, u32[]{:S(2)}) copy-start(f32[240,128]{1,0:T(8,128)S(1)} %collective-permute-done.11.refs_1_) | copy-start | bytes 368644
  52.6 0.6 %copy-start.5 = (f32[240,128]{1,0:T(8,128)}, f32[240,128]{1,0:T(8,128)S(1)}, u32[]{:S(2)}) copy-start(f32[240,128]{1,0:T(8,128)S(1)} %collective-permute-done.12.refs_2_) | copy-start | bytes 368644
  52.6 0.7 %copy-start.6 = (f32[240,128]{1,0:T(8,128)}, f32[240,128]{1,0:T(8,128)S(1)}, u32[]{:S(2)}) copy-start(f32[240,128]{1,0:T(8,128)S(1)} %collective-permute-done.13.refs_3_) | copy-start | bytes 368644

commit v3 on v2

v3 whole, which is shorter than its diff:
```python
import functools

import jax
import jax.numpy as jnp
from jax import lax
from jax.experimental import pallas as pl
from jax.experimental.pallas import tpu as pltpu
from jax.sharding import PartitionSpec as P

AXIS = "slab"
HIGHEST = lax.Precision.HIGHEST
LANES = 128
COEF_ROWS = 8
GROUP = 8
WIDE = 256
COEF_STEP = 4096
EARLY = 3
CHUNKS = 2


class Plan:
    def __init__(self, devices, tiles, entries, frames, block_width, tile_width):
        self.devices = devices
        self.tiles = tiles
        self.entries = entries
        self.frames = frames
        self.block_width = block_width
        self.tile_width = tile_width
        self.owned = tiles // devices
        self.log = devices.bit_length() - 1
        assert 1 << self.log == devices and self.owned * devices == tiles
        widths = [1]
        while sum(widths) < self.log:
            widths.append(min(2, self.log - sum(widths)))
        self.widths = widths
        self.done = [sum(widths[:i]) for i in range(len(widths) + 1)]
        self.slots = [
            min(self.owned, -(-(self.owned * (1 << b) + entries - 1) // devices))
            for b in self.done
        ]
        self.slots[-1] = self.owned
        self.owners = [devices >> self.done[i + 1] for i in range(len(widths))]

    def tiles_in(self, stage):
        return self.owners[stage] * self.slots[stage]

    def position(self, rel, stage):
        place = 0
        for i in range(stage, len(self.widths)):
            digit = (rel >> self.done[i]) & ((1 << self.widths[i]) - 1)
            place = (place << self.widths[i]) | digit
        return place

    def relative(self, place, stage):
        rel = 0
        for i in reversed(range(stage, len(self.widths))):
            rel = rel | ((place & ((1 << self.widths[i]) - 1)) << self.done[i])
            place = place >> self.widths[i]
        return rel


def tile_rows(index, frames):
    return pl.ds(pl.multiple_of(index * frames, 8), frames)


def split(values):
    high = values.astype(jnp.bfloat16)
    low = (values - high.astype(jnp.float32)).astype(jnp.bfloat16)
    return high, low


def demean(values):
    return values - jnp.sum(values, axis=0, keepdims=True) * (1.0 / values.shape[0])


def in_hbm(array):
    return pltpu.with_memory_space_constraint(array, pltpu.HBM)


def sample_kernel(
    plan, block_ids, tile_ids, tile_owner, series, weights,
    keep, send, picked, held, pick_sems, weight_sems,
):
    frames, width = plan.frames, plan.block_width
    groups = plan.entries // GROUP

    def pick(k):
        start = pl.multiple_of(block_ids[k] * width, width)
        return pltpu.make_async_copy(
            series.at[:, pl.ds(start, width)], picked.at[k], pick_sems.at[k]
        )

    def fetch(g):
        span = pl.ds(g * GROUP, GROUP)
        return pltpu.make_async_copy(weights.at[span], held.at[span], weight_sems.at[g])

    def begin(g, carry):
        fetch(g).start()
        for i in range(GROUP):
            pick(g * GROUP + i).start()
        return carry

    lax.fori_loop(0, groups, begin, 0)
    keep[...] = jnp.zeros_like(keep)
    send[...] = jnp.zeros_like(send)
    device = lax.axis_index(AXIS)
    spare = plan.owners[0] * plan.slots[0]

    def group(g, carry):
        fetch(g).wait()
        for i in range(GROUP):
            pick(g * GROUP + i).wait()
        for i in range(GROUP):
            k = g * GROUP + i
            tile = tile_ids[k]
            high, low = split(demean(picked[k]))
            both = jnp.dot(
                jnp.concatenate([high, low], axis=0),
                held[k],
                preferred_element_type=jnp.float32,
            )
            total = both[0:frames] + both[frames:]
            rel = tile_owner[tile & (plan.devices - 1)] ^ device
            offset = (tile - device * plan.owned) & (plan.tiles - 1)
            slot = plan.position(rel, 1) * plan.slots[0] + (offset >> plan.log)
            mine = (rel & 1) == 0
            used = tile >= 0
            to_keep = jnp.where(used & mine, slot, spare)
            to_send = jnp.where(used & jnp.logical_not(mine), slot, spare)
            keep[tile_rows(to_keep, frames), :] = total
            send[tile_rows(to_send, frames), :] = total
        return carry

    lax.fori_loop(0, groups, group, 0)


def sample(plan, series, weights, block_ids, tile_ids, tile_owner):
    frames, width = plan.frames, plan.block_width
    smem = pl.BlockSpec(memory_space=pltpu.SMEM)
    vmem = pl.BlockSpec(memory_space=pltpu.VMEM)
    hbm = pl.BlockSpec(memory_space=pl.ANY)
    block = jax.ShapeDtypeStruct(((plan.tiles_in(0) + 1) * frames, LANES), jnp.float32)
    held_bytes = plan.entries * width * (4 * frames + 2 * plan.tile_width)
    return pl.pallas_call(
        functools.partial(sample_kernel, plan),
        name="sample",
        in_specs=[smem, smem, smem, hbm, hbm],
        out_specs=[vmem, vmem],
        out_shape=[block, block],
        scratch_shapes=[
            pltpu.VMEM((plan.entries, frames, width), jnp.float32),
            pltpu.VMEM(weights.shape, weights.dtype),
            pltpu.SemaphoreType.DMA((plan.entries,)),
            pltpu.SemaphoreType.DMA((plan.entries // GROUP,)),
        ],
        compiler_params=pltpu.CompilerParams(
            vmem_limit_bytes=held_bytes + 8 * block.shape[0] * LANES + (6 << 20)
        ),
    )(*[in_hbm(x) for x in (block_ids, tile_ids, tile_owner, series, weights)])


def coef_kernel(
    first, steps, series, mask, probes, before, coefs,
    held, marks, halves, masked, gram, sems, mark_sem,
):
    frames = series.shape[0]
    columns = COEF_STEP

    def fetch(step):
        span = pl.ds(pl.multiple_of(step * columns, columns), columns)
        there = pl.ds(pl.multiple_of((first + step) * columns, columns), columns)
        return pltpu.make_async_copy(series.at[:, there], held.at[:, span], sems.at[step])

    mark_copy = pltpu.make_async_copy(
        mask.at[:, pl.ds(first * columns, steps * columns)], marks, mark_sem
    )
    mark_copy.start()
    for step in range(steps):
        fetch(step).start()
    gram[...] = jnp.zeros_like(gram)
    mark_copy.wait()

    def chunk(step, carry):
        fetch(step).wait()
        start = step * columns
        for at in range(0, columns, WIDE):
            span = pl.ds(pl.multiple_of(start + at, WIDE), WIDE)
            place = pl.ds(at, WIDE)
            high, low = split(demean(held[:, span]))
            halves[0:frames, place] = high
            halves[frames:, place] = low
            masked[:, place] = high * marks[:, span].astype(jnp.float32).astype(jnp.bfloat16)
        gram[...] += lax.dot_general(
            halves[...],
            masked[...],
            (((1,), (1,)), ((), ())),
            preferred_element_type=jnp.float32,
        )
        return carry

    lax.fori_loop(0, steps, chunk, 0)
    low = gram[frames:, :]
    start = probes[...]
    made = jnp.dot(
        start, gram[0:frames, :] + low, precision=HIGHEST, preferred_element_type=jnp.float32
    ) + lax.dot_general(
        start,
        low,
        (((1,), (1,)), ((), ())),
        precision=HIGHEST,
        preferred_element_type=jnp.float32,
    )
    coefs[...] = before[...]
    coefs[0 : start.shape[0], 0:frames] += made


def local_coefs(series, noise_mask, probes, before, first, steps):
    frames, voxels = series.shape
    held = steps * COEF_STEP
    vmem = pl.BlockSpec(memory_space=pltpu.VMEM)
    hbm = pl.BlockSpec(memory_space=pl.ANY)
    return pl.pallas_call(
        functools.partial(coef_kernel, first, steps),
        name="coefs",
        in_specs=[hbm, hbm, vmem, vmem],
        out_specs=vmem,
        out_shape=jax.ShapeDtypeStruct(before.shape, before.dtype),
        scratch_shapes=[
            pltpu.VMEM((frames, held), series.dtype),
            pltpu.VMEM((1, held), noise_mask.dtype),
            pltpu.VMEM((2 * frames, COEF_STEP), jnp.bfloat16),
            pltpu.VMEM((frames, COEF_STEP), jnp.bfloat16),
            pltpu.VMEM((2 * frames, frames), jnp.float32),
            pltpu.SemaphoreType.DMA((steps,)),
            pltpu.SemaphoreType.DMA,
        ],
        compiler_params=pltpu.CompilerParams(vmem_limit_bytes=24 << 20),
        cost_estimate=pl.CostEstimate(
            flops=4 * frames * frames * held,
            bytes_accessed=4 * frames * held,
            transcendentals=0,
        ),
    )(in_hbm(series), in_hbm(noise_mask.reshape(1, voxels)), probes.T, before)


def note_owners(plan, tile_owner, inverse):
    for residue in range(plan.devices):
        inverse[tile_owner[residue]] = residue


def add_tiles(plan, stage, inverse, sources, place, slot, height, skip=0, rows=None):
    rows = height if rows is None else rows
    device = lax.axis_index(AXIS)
    done, after = plan.done[stage], plan.done[stage + 1]
    slots, devices, tiles = plan.slots[stage], plan.devices, plan.tiles
    residue = inverse[device ^ plan.relative(place, stage + 1)]
    last = stage + 1 == len(plan.widths)
    base = 0 if last else ((device >> after) << after) * plan.owned
    tile = (base + ((residue - base) & (devices - 1)) + slot * devices) & (tiles - 1)
    total = None
    for digit, source in enumerate(sources):
        sender = device ^ (digit << done)
        first = ((sender >> done) << done) * plan.owned
        offset = (tile - first) & (tiles - 1)
        there = offset < slots * devices
        at = place * slots + jnp.minimum(offset >> plan.log, slots - 1)
        value = source[pl.ds(pl.multiple_of(at * height + skip, 8), rows), :]
        value = jnp.where(there, value, 0.0)
        total = value if total is None else total + value
    return total


def add_coefs(sources):
    total = None
    for source in sources:
        value = source[pl.ds(source.shape[0] - COEF_ROWS, COEF_ROWS), :]
        total = value if total is None else total + value
    return total


def merge_kernel(plan, stage, span, fresh, tile_owner, *refs):
    fan = 1 << plan.widths[stage]
    sources, refs = refs[:fan], refs[fan:]
    coefs = None
    if fresh:
        coefs, refs = refs[0][...] + refs[1][...], refs[2:]
    outs, inverse = refs[:-1], refs[-1]
    begin, rows = span
    slots, count = plan.slots[stage + 1], plan.owners[stage + 1]
    size = count * slots * rows
    note_owners(plan, tile_owner, inverse)
    if outs[0].shape[0] > size:
        if not fresh:
            coefs = add_coefs(sources)
        for out in outs:
            out[pl.ds(size, COEF_ROWS), :] = coefs
    height, skip = (plan.frames, begin) if stage == 0 else (rows, 0)
    for digit, out in enumerate(outs):

        def owner(rest, carry):
            for slot in range(slots):
                value = add_tiles(
                    plan, stage, inverse, sources, digit * count + rest, slot,
                    height, skip, rows,
                )
                target = pl.ds(pl.multiple_of((rest * slots + slot) * rows, 8), rows)
                out[target, :] = value
            return carry

        if count <= 4:
            for rest in range(count):
                owner(rest, 0)
        else:
            lax.fori_loop(0, count, owner, 0)


def merge(plan, stage, span, riding, tile_owner, sources, coefs=()):
    fan = 1 << plan.widths[stage + 1]
    rows = plan.tiles_in(stage + 1) * span[1] + (COEF_ROWS if riding else 0)
    block = jax.ShapeDtypeStruct((rows, LANES), jnp.float32)
    vmem = pl.BlockSpec(memory_space=pltpu.VMEM)
    arrays = list(sources) + list(coefs)
    return pl.pallas_call(
        functools.partial(merge_kernel, plan, stage, span, len(coefs) > 0),
        name="merge",
        in_specs=[pl.BlockSpec(memory_space=pltpu.SMEM)] + [vmem] * len(arrays),
        out_specs=[vmem] * fan,
        out_shape=[block] * fan,
        scratch_shapes=[pltpu.SMEM((plan.devices,), jnp.int32)],
        compiler_params=pltpu.CompilerParams(vmem_limit_bytes=32 << 20),
    )(in_hbm(tile_owner), *arrays)


def finish_kernel(plan, comps, spans, tile_owner, *refs):
    stage = len(plan.widths) - 1
    fan = 1 << plan.widths[stage]
    parts = [refs[i * fan : (i + 1) * fan] for i in range(len(spans))]
    out, inverse = refs[-2:]
    frames = plan.frames
    note_owners(plan, tile_owner, inverse)
    basis = add_coefs(parts[-1])
    lane = lax.broadcasted_iota(jnp.int32, basis.shape, 1)
    row = lax.broadcasted_iota(jnp.int32, basis.shape, 0)
    basis = jnp.where((lane < frames) & (row < comps), basis, 0.0)
    unit = jnp.zeros_like(basis)
    for i in range(comps):
        line = basis[i : i + 1, :]
        line = line * lax.rsqrt(jnp.sum(line * line, axis=1, keepdims=True))
        unit = jnp.where(row == i, line, unit)
        basis = basis - jnp.sum(basis * line, axis=1, keepdims=True) * line
    unit = unit[:, 0:frames]
    values = []
    for slot in range(plan.owned):
        pieces = [
            add_tiles(plan, stage, inverse, sources, 0, slot, rows)
            for (begin, rows), sources in zip(spans, parts)
        ]
        values.append(jnp.concatenate(pieces, axis=0))
    value = jnp.concatenate(values, axis=1)
    along = jnp.dot(unit, value, precision=HIGHEST, preferred_element_type=jnp.float32)
    value = value - lax.dot_general(
        unit,
        along,
        (((0,), (0,)), ((), ())),
        precision=HIGHEST,
        preferred_element_type=jnp.float32,
    )
    for slot in range(plan.owned):
        out[slot] = value[:, slot * plan.tile_width : (slot + 1) * plan.tile_width]


def finish(plan, comps, spans, tile_owner, parts):
    vmem = pl.BlockSpec(memory_space=pltpu.VMEM)
    arrays = [block for part in parts for block in part]
    return pl.pallas_call(
        functools.partial(finish_kernel, plan, comps, spans),
        name="finish",
        in_specs=[pl.BlockSpec(memory_space=pltpu.SMEM)] + [vmem] * len(arrays),
        out_specs=vmem,
        out_shape=jax.ShapeDtypeStruct((plan.owned, plan.frames, plan.tile_width), jnp.float32),
        scratch_shapes=[pltpu.SMEM((plan.devices,), jnp.int32)],
        compiler_params=pltpu.CompilerParams(vmem_limit_bytes=32 << 20),
    )(in_hbm(tile_owner), *arrays)


def exchange(plan, stage, blocks):
    received = [blocks[0]]
    for digit in range(1, len(blocks)):
        pairs = [(i, i ^ (digit << plan.done[stage])) for i in range(plan.devices)]
        received.append(lax.ppermute(blocks[digit], AXIS, pairs))
    return received


def body(series, noise_mask, probes, sample_weights, block_ids, tile_ids, tile_owner):
    frames, voxels = series.shape
    entries, block_width, tile_width = sample_weights.shape
    plan = Plan(
        lax.axis_size(AXIS), tile_owner.shape[0], entries, frames, block_width, tile_width
    )
    stages = len(plan.widths)
    rows = frames // CHUNKS
    spans = [(i * rows, rows) for i in range(CHUNKS)]
    steps = voxels // COEF_STEP
    keep, send = sample(plan, series, sample_weights, block_ids, tile_ids, tile_owner)
    keep, send, probes = lax.optimization_barrier((keep, send, probes))
    pair = exchange(plan, 0, [keep, send])
    coefs = jnp.zeros((COEF_ROWS, LANES), jnp.float32)
    coefs = local_coefs(series, noise_mask, probes, coefs, 0, EARLY)
    chunks = [merge(plan, 0, span, False, tile_owner, pair) for span in spans[:-1]]
    chunks[-1], coefs = lax.optimization_barrier((chunks[-1], coefs))
    coefs = local_coefs(series, noise_mask, probes, coefs, EARLY, steps - EARLY)
    coefs = exchange(plan, 0, [coefs, coefs])
    chunks.append(merge(plan, 0, spans[-1], True, tile_owner, pair, coefs))
    for stage in range(1, stages):
        for i, span in enumerate(spans):
            chunks[i] = exchange(plan, stage, chunks[i])
            if stage + 1 < stages:
                riding = i + 1 == len(spans)
                chunks[i] = merge(plan, stage, span, riding, tile_owner, chunks[i])
    return finish(plan, probes.shape[1], spans, tile_owner, chunks)


def solution(mesh):
    return jax.shard_map(
        body,
        mesh=mesh,
        in_specs=(
            P(None, AXIS),
            P(AXIS),
            P(),
            P(AXIS, None, None),
            P(AXIS),
            P(AXIS),
            P(),
        ),
        out_specs=P(AXIS, None, None),
        check_vma=False,
    )
```

time: 56.9 us -> 52.1 us (0.916)
  local copies, waits for them, and re-layouts: 3.34 us -> 0.01 us
  waiting for transfers between devices: 15.3 us -> 13.1 us
  Pallas kernels: 18.7 us -> 20.3 us
  other arithmetic: 0.6 us -> 0 us
    unnamed x14 -> x2, local copies, waits for them, and re-layouts: 3.34 us -> 0.01 us
    pallas_call x4 -> x7, Pallas kernels: 12.5 us -> 15.5 us  [the longest x2 9.32 us: local_coefs(): pl.pallas_call(functools.partial(coef_kernel, first, steps), name='coefs'...]
    ppermute x14, waiting for transfers between devices: 15.3 us -> 13.1 us  [exchange(): received.append(lax.ppermute(blocks[digit], AXIS, pairs))]
    pallas_call x1, Pallas kernels: 6.22 us -> 4.82 us  [sample(): pl.pallas_call(functools.partial(sample_kernel, plan), name='sample', in_...]
    add x3 -> x0, other arithmetic: 0.6 us -> none  [body(): coefs = sum(exchange(plan, stage, [coefs] * (1 << plan.widths[stage])))]
  transfers between devices with their start and end apart: 14 -> 14, of which waited for: 6 -> 4; matrix products, arithmetic and copies ran while one was open for 1% -> 0% of each run, Pallas kernels for 14% -> 23%
where the time goes in v3:
time: 52.1 us; the launch traced here: 51.9 us
  Pallas kernels  20.3 us (39%)
  starting transfers between devices  18.4 us (35%)
  waiting for transfers between devices  13.1 us (25%)
    ppermute x14, starting transfers between devices, exchange(): received.append(lax.ppermute(blocks[digit], AXIS, pairs))  18.4 us
    ppermute x14, waiting for transfers between devices, exchange(): received.append(lax.ppermute(blocks[digit], AXIS, pairs))  13.1 us
    pallas_call x2, Pallas kernels, local_coefs(): pl.pallas_call(functools.partial(coef_kernel, first, steps), name='coefs'...  9.32 us
    pallas_call x1, Pallas kernels, sample(): pl.pallas_call(functools.partial(sample_kernel, plan), name='sample', in_...  4.82 us
    pallas_call x4, Pallas kernels, merge(): pl.pallas_call(functools.partial(merge_kernel, plan, stage, span, len(coe...  3.59 us
    pallas_call x1, Pallas kernels, finish(): pl.pallas_call(functools.partial(finish_kernel, plan, comps, spans), name...  2.56 us
  transfers between devices with their start and end apart: 14, of which 4 were waited for; matrix products, arithmetic and copies ran while one was open for 0% of the time, Pallas kernels for 23%

profile of v3, /device:TPU:0, one launch (start us, length us, event | category | flops | bytes accessed | tf_op | source)
XLA Modules:
  0.0 51.9 jit_solution(14938985363509096080)
XLA Ops:
  0.0 4.8 %sample.1 = (f32[2640,128]{1,0:T(8,128)S(1)}, f32[2640,128]{1,0:T(8,128)S(1)}) custom-call(s32[48]{0:T(128)} %block_ids.1, s32[48]{0:T(128)} %tile_ids.1, s32[128]{0:T(128)} %tile_owner.11, f32[80,32768]{1,0:T(8,128)} %series.5, bf16[48,256,128]{2,1,0:T(8,128)(2,1)} %weights.1), custom_call_target="tpu_custom_call" | custom-call | tf_op jit(solution)/shard_map/sample/pallas_call | solution.py:144
  4.8 0.5 collective-permute-start
  5.3 3.6 %coefs.2.before = f32[8,128]{1,0:T(8,128)S(1)} custom-call(f32[80,32768]{1,0:T(8,128)} %series.5, s32[1,32768]{1,0:T(1,128)} %bitcast.4, f32[5,80]{1,0:T(8,128)S(1)} %bitcast.2, f32[8,128]{1,0:T(8,128)S(1)} %broadcast_in_dim.3.before), custom_call_target="tpu_custom_call" | custom-call | flops 314572800 | bytes 3932160 | tf_op jit(solution)/shard_map/coefs/pallas_call | solution.py:222
  9.0 0.0 collective-permute-done.refs_1_
  9.0 0.9 %merge.4 = (f32[320,128]{1,0:T(8,128)S(1)}, f32[320,128]{1,0:T(8,128)S(1)}, f32[320,128]{1,0:T(8,128)S(1)}, f32[320,128]{1,0:T(8,128)S(1)}) custom-call(s32[128]{0:T(128)} %tile_owner.11, f32[2640,128]{1,0:T(8,128)S(1)} %get-tuple-element.33.refs_0_, f32[2640,128]{1,0:T(8,128)S(1)} %collective-permute-done.refs_1_), custom_call_target="tpu_custom_call" | custom-call | tf_op jit(solution)/shard_map/merge/pallas_call | solution.py:323
  9.9 2.6 %collective-permute-start.1 = (f32[320,128]{1,0:T(8,128)S(1)}, f32[320,128]{1,0:T(8,128)S(1)}, u32[]{:S(2)}, u32[]{:S(2)}) collective-permute-start(f32[320,128]{1,0:T(8,128)S(1)} %get-tuple-element.41), channel_id=1, source_target_pairs={{0,2},{1,3},{2,0},{3,1},{4,6},{5,7},{6,4},{7,5},{8,10},{9,11},{10,... | collective-permute-start | bytes 491528 | tf_op jit(solution)/shard_map/ppermute | solution.py:390
  12.5 1.5 %collective-permute-start.2 = (f32[320,128]{1,0:T(8,128)S(1)}, f32[320,128]{1,0:T(8,128)S(1)}, u32[]{:S(2)}, u32[]{:S(2)}) collective-permute-start(f32[320,128]{1,0:T(8,128)S(1)} %get-tuple-element.42), channel_id=1, source_target_pairs={{0,4},{1,5},{2,6},{3,7},{4,0},{5,1},{6,2},{7,3},{8,12},{9,13},{10,... | collective-permute-start | bytes 491528 | tf_op jit(solution)/shard_map/ppermute | solution.py:390
  14.0 0.0 collective-permute-start.3
  14.1 5.7 %coefs.3.refs_2_ = f32[8,128]{1,0:T(8,128)S(1)} custom-call(f32[80,32768]{1,0:T(8,128)} %series.5, s32[1,32768]{1,0:T(1,128)} %bitcast.5, f32[5,80]{1,0:T(8,128)S(1)} %bitcast.3, f32[8,128]{1,0:T(8,128)S(1)} %coefs.2.before), custom_call_target="tpu_custom_call" | custom-call | flops 524288000 | bytes 6553600 | tf_op jit(solution)/shard_map/coefs/pallas_call | solution.py:222
  19.8 0.1 collective-permute-start.7
  19.8 1.2 %collective-permute-done.7.refs_3_ = f32[8,128]{1,0:T(8,128)S(1)} collective-permute-done((f32[8,128]{1,0:T(8,128)S(1)}, f32[8,128]{1,0:T(8,128)S(1)}, u32[]{:S(2)}, u32[]{:S(2)}) %collective-permute-start.7) | collective-permute-done | bytes 4128 | tf_op jit(solution)/shard_map/ppermute | solution.py:390
  21.0 0.9 %merge.6 = (f32[328,128]{1,0:T(8,128)S(1)}, f32[328,128]{1,0:T(8,128)S(1)}, f32[328,128]{1,0:T(8,128)S(1)}, f32[328,128]{1,0:T(8,128)S(1)}) custom-call(s32[128]{0:T(128)} %tile_owner.11, f32[2640,128]{1,0:T(8,128)S(1)} %get-tuple-element.33.refs_0_, f32[2640,128]{1,0:T(8,128)S(1)} %collective-permute-done.refs_1_, f32[8,128]{1,0:T(8,128)S(1)} %coefs.3.refs_2_, ...), custom_call_target="tpu_custom_call" | custom-call | tf_op jit(solution)/shard_map/merge/pallas_call | solution.py:323
  21.9 3.0 %collective-permute-start.10 = (f32[328,128]{1,0:T(8,128)S(1)}, f32[328,128]{1,0:T(8,128)S(1)}, u32[]{:S(2)}, u32[]{:S(2)}) collective-permute-start(f32[328,128]{1,0:T(8,128)S(1)} %get-tuple-element.52), channel_id=1, source_target_pairs={{0,6},{1,7},{2,4},{3,5},{4,2},{5,3},{6,0},{7,1},{8,14},{9,15},{10,... | collective-permute-start | bytes 503816 | tf_op jit(solution)/shard_map/ppermute | solution.py:390
  24.9 0.5 %collective-permute-start.8 = (f32[328,128]{1,0:T(8,128)S(1)}, f32[328,128]{1,0:T(8,128)S(1)}, u32[]{:S(2)}, u32[]{:S(2)}) collective-permute-start(f32[328,128]{1,0:T(8,128)S(1)} %get-tuple-element.50), channel_id=1, source_target_pairs={{0,2},{1,3},{2,0},{3,1},{4,6},{5,7},{6,4},{7,5},{8,10},{9,11},{10,... | collective-permute-start | bytes 503816 | tf_op jit(solution)/shard_map/ppermute | solution.py:390
  25.4 0.0 collective-permute-done.1.refs_1_
  25.4 0.1 collective-permute-start.9
  25.6 0.9 %merge.5 = (f32[120,128]{1,0:T(8,128)S(1)}, f32[120,128]{1,0:T(8,128)S(1)}, f32[120,128]{1,0:T(8,128)S(1)}, f32[120,128]{1,0:T(8,128)S(1)}) custom-call(s32[128]{0:T(128)} %tile_owner.11, f32[320,128]{1,0:T(8,128)S(1)} %get-tuple-element.40.refs_0_, f32[320,128]{1,0:T(8,128)S(1)} %collective-permute-done.1.refs_1_, ...), custom_call_target="tpu_custom_call" | custom-call | tf_op jit(solution)/shard_map/merge/pallas_call | solution.py:323
  26.4 2.0 %collective-permute-start.4 = (f32[120,128]{1,0:T(8,128)S(1)}, f32[120,128]{1,0:T(8,128)S(1)}, u32[]{:S(2)}, u32[]{:S(2)}) collective-permute-start(f32[120,128]{1,0:T(8,128)S(1)} %get-tuple-element.45), channel_id=1, source_target_pairs={{0,8},{1,9},{2,10},{3,11},{4,12},{5,13},{6,14},{7,15},{8,0},{9,1},... | collective-permute-start | bytes 184328 | tf_op jit(solution)/shard_map/ppermute | solution.py:390
  28.5 1.5 %collective-permute-done.10.refs_3_ = f32[328,128]{1,0:T(8,128)S(1)} collective-permute-done((f32[328,128]{1,0:T(8,128)S(1)}, f32[328,128]{1,0:T(8,128)S(1)}, u32[]{:S(2)}, u32[]{:S(2)}) %collective-permute-start.10) | collective-permute-done | bytes 167968 | tf_op jit(solution)/shard_map/ppermute | solution.py:390
  30.0 3.4 %collective-permute-done.8.refs_1_ = f32[328,128]{1,0:T(8,128)S(1)} collective-permute-done((f32[328,128]{1,0:T(8,128)S(1)}, f32[328,128]{1,0:T(8,128)S(1)}, u32[]{:S(2)}, u32[]{:S(2)}) %collective-permute-start.8) | collective-permute-done | bytes 167968 | tf_op jit(solution)/shard_map/ppermute | solution.py:390
  33.4 0.9 %merge.7 = (f32[128,128]{1,0:T(8,128)S(1)}, f32[128,128]{1,0:T(8,128)S(1)}, f32[128,128]{1,0:T(8,128)S(1)}, f32[128,128]{1,0:T(8,128)S(1)}) custom-call(s32[128]{0:T(128)} %tile_owner.11, f32[328,128]{1,0:T(8,128)S(1)} %get-tuple-element.49.refs_0_, f32[328,128]{1,0:T(8,128)S(1)} %collective-permute-done.8.refs_1_, ...), custom_call_target="tpu_custom_call" | custom-call | tf_op jit(solution)/shard_map/merge/pallas_call | solution.py:323
  34.3 1.6 %collective-permute-start.11 = (f32[128,128]{1,0:T(8,128)S(1)}, f32[128,128]{1,0:T(8,128)S(1)}, u32[]{:S(2)}, u32[]{:S(2)}) collective-permute-start(f32[128,128]{1,0:T(8,128)S(1)} %get-tuple-element.54), channel_id=1, source_target_pairs={{0,8},{1,9},{2,10},{3,11},{4,12},{5,13},{6,14},{7,15},{8,0},{9,1},... | collective-permute-start | bytes 196616 | tf_op jit(solution)/shard_map/ppermute | solution.py:390
  35.9 2.6 %collective-permute-start.12 = (f32[128,128]{1,0:T(8,128)S(1)}, f32[128,128]{1,0:T(8,128)S(1)}, u32[]{:S(2)}, u32[]{:S(2)}) collective-permute-start(f32[128,128]{1,0:T(8,128)S(1)} %get-tuple-element.55), channel_id=1, source_target_pairs={{0,16},{1,17},{2,18},{3,19},{4,20},{5,21},{6,22},{7,23},{8,24},{9,... | collective-permute-start | bytes 196616 | tf_op jit(solution)/shard_map/ppermute | solution.py:390
  38.5 0.2 collective-permute-start.13
  38.7 1.7 %collective-permute-start.5 = (f32[120,128]{1,0:T(8,128)S(1)}, f32[120,128]{1,0:T(8,128)S(1)}, u32[]{:S(2)}, u32[]{:S(2)}) collective-permute-start(f32[120,128]{1,0:T(8,128)S(1)} %get-tuple-element.46), channel_id=1, source_target_pairs={{0,16},{1,17},{2,18},{3,19},{4,20},{5,21},{6,22},{7,23},{8,24},{9,... | collective-permute-start | bytes 184328 | tf_op jit(solution)/shard_map/ppermute | solution.py:390
  40.4 1.9 %collective-permute-start.6 = (f32[120,128]{1,0:T(8,128)S(1)}, f32[120,128]{1,0:T(8,128)S(1)}, u32[]{:S(2)}, u32[]{:S(2)}) collective-permute-start(f32[120,128]{1,0:T(8,128)S(1)} %get-tuple-element.47), channel_id=1, source_target_pairs={{0,24},{1,25},{2,26},{3,27},{4,28},{5,29},{6,30},{7,31},{8,16},{9,... | collective-permute-start | bytes 184328 | tf_op jit(solution)/shard_map/ppermute | solution.py:390
  42.4 7.0 %collective-permute-done.5.refs_2_ = f32[120,128]{1,0:T(8,128)S(1)} collective-permute-done((f32[120,128]{1,0:T(8,128)S(1)}, f32[120,128]{1,0:T(8,128)S(1)}, u32[]{:S(2)}, u32[]{:S(2)}) %collective-permute-start.5) | collective-permute-done | bytes 61472 | tf_op jit(solution)/shard_map/ppermute | solution.py:390
  49.3 0.0 collective-permute-done.6.refs_3_
  49.3 0.0 collective-permute-done.11.refs_5_
  49.3 0.0 collective-permute-done.12.refs_6_
  49.3 0.0 collective-permute-done.13.refs_7_
  49.3 2.6 %finish.1 = f32[4,80,128]{2,1,0:T(8,128)} custom-call(s32[128]{0:T(128)} %tile_owner.11, f32[120,128]{1,0:T(8,128)S(1)} %get-tuple-element.44.refs_0_, f32[120,128]{1,0:T(8,128)S(1)} %collective-permute-done.4.refs_1_, f32[120,128]{1,0:T(8,128)S(1)} %collective-permute-done.5.refs_2_, f32[120,128]{1,0:T(8,128)S(1)} %collective-permute-done.6.refs_3_, ...), custom_call_target="tpu_custom_call" | custom-call | tf_op jit(solution)/shard_map/finish/pallas_call | solution.py:375
  (7 shorter events, 0.0 us)
Async XLA Ops:
  0.0 5.3 %copy-start = (f32[80,5]{0,1:T(8,128)S(1)}, f32[80,5]{0,1:T(8,128)}, u32[]{:S(2)}) copy-start(f32[80,5]{0,1:T(8,128)} %param.9) | copy-start | bytes 4804
  4.8 4.2 %collective-permute-start = (f32[2640,128]{1,0:T(8,128)S(1)}, f32[2640,128]{1,0:T(8,128)S(1)}, u32[]{:S(2)}, u32[]{:S(2)}) collective-permute-start(f32[2640,128]{1,0:T(8,128)S(1)} %get-tuple-element.34), channel_id=1, source_target_pairs={{0,1},{1,0},{2,3},{3,2},{4,5},{5,4},{6,7},{7,6},{8,9},{9,8},{10,11... | collective-permute-start | bytes 4055048 | tf_op jit(solution)/shard_map/ppermute | solution.py:390
  9.9 15.5 %collective-permute-start.1 = (f32[320,128]{1,0:T(8,128)S(1)}, f32[320,128]{1,0:T(8,128)S(1)}, u32[]{:S(2)}, u32[]{:S(2)}) collective-permute-start(f32[320,128]{1,0:T(8,128)S(1)} %get-tuple-element.41), channel_id=1, source_target_pairs={{0,2},{1,3},{2,0},{3,1},{4,6},{5,7},{6,4},{7,5},{8,10},{9,11},{10,... | collective-permute-start | bytes 491528 | tf_op jit(solution)/shard_map/ppermute | solution.py:390
  12.5 13.0 %collective-permute-start.2 = (f32[320,128]{1,0:T(8,128)S(1)}, f32[320,128]{1,0:T(8,128)S(1)}, u32[]{:S(2)}, u32[]{:S(2)}) collective-permute-start(f32[320,128]{1,0:T(8,128)S(1)} %get-tuple-element.42), channel_id=1, source_target_pairs={{0,4},{1,5},{2,6},{3,7},{4,0},{5,1},{6,2},{7,3},{8,12},{9,13},{10,... | collective-permute-start | bytes 491528 | tf_op jit(solution)/shard_map/ppermute | solution.py:390
  14.0 11.5 %collective-permute-start.3 = (f32[320,128]{1,0:T(8,128)S(1)}, f32[320,128]{1,0:T(8,128)S(1)}, u32[]{:S(2)}, u32[]{:S(2)}) collective-permute-start(f32[320,128]{1,0:T(8,128)S(1)} %get-tuple-element.43), channel_id=1, source_target_pairs={{0,6},{1,7},{2,4},{3,5},{4,2},{5,3},{6,0},{7,1},{8,14},{9,15},{10,... | collective-permute-start | bytes 491528 | tf_op jit(solution)/shard_map/ppermute | solution.py:390
  19.8 1.2 %collective-permute-start.7 = (f32[8,128]{1,0:T(8,128)S(1)}, f32[8,128]{1,0:T(8,128)S(1)}, u32[]{:S(2)}, u32[]{:S(2)}) collective-permute-start(f32[8,128]{1,0:T(8,128)S(1)} %coefs.3.refs_2_), channel_id=1, source_target_pairs={{0,1},{1,0},{2,3},{3,2},{4,5},{5,4},{6,7},{7,6},{8,9},{9,8},{10,11... | collective-permute-start | bytes 12296 | tf_op jit(solution)/shard_map/ppermute | solution.py:390
  21.9 8.1 %collective-permute-start.10 = (f32[328,128]{1,0:T(8,128)S(1)}, f32[328,128]{1,0:T(8,128)S(1)}, u32[]{:S(2)}, u32[]{:S(2)}) collective-permute-start(f32[328,128]{1,0:T(8,128)S(1)} %get-tuple-element.52), channel_id=1, source_target_pairs={{0,6},{1,7},{2,4},{3,5},{4,2},{5,3},{6,0},{7,1},{8,14},{9,15},{10,... | collective-permute-start | bytes 503816 | tf_op jit(solution)/shard_map/ppermute | solution.py:390
  24.9 8.5 %collective-permute-start.8 = (f32[328,128]{1,0:T(8,128)S(1)}, f32[328,128]{1,0:T(8,128)S(1)}, u32[]{:S(2)}, u32[]{:S(2)}) collective-permute-start(f32[328,128]{1,0:T(8,128)S(1)} %get-tuple-element.50), channel_id=1, source_target_pairs={{0,2},{1,3},{2,0},{3,1},{4,6},{5,7},{6,4},{7,5},{8,10},{9,11},{10,... | collective-permute-start | bytes 503816 | tf_op jit(solution)/shard_map/ppermute | solution.py:390
  25.4 8.0 %collective-permute-start.9 = (f32[328,128]{1,0:T(8,128)S(1)}, f32[328,128]{1,0:T(8,128)S(1)}, u32[]{:S(2)}, u32[]{:S(2)}) collective-permute-start(f32[328,128]{1,0:T(8,128)S(1)} %get-tuple-element.51), channel_id=1, source_target_pairs={{0,4},{1,5},{2,6},{3,7},{4,0},{5,1},{6,2},{7,3},{8,12},{9,13},{10,... | collective-permute-start | bytes 503816 | tf_op jit(solution)/shard_map/ppermute | solution.py:390
  26.4 14.0 %collective-permute-start.4 = (f32[120,128]{1,0:T(8,128)S(1)}, f32[120,128]{1,0:T(8,128)S(1)}, u32[]{:S(2)}, u32[]{:S(2)}) collective-permute-start(f32[120,128]{1,0:T(8,128)S(1)} %get-tuple-element.45), channel_id=1, source_target_pairs={{0,8},{1,9},{2,10},{3,11},{4,12},{5,13},{6,14},{7,15},{8,0},{9,1},... | collective-permute-start | bytes 184328 | tf_op jit(solution)/shard_map/ppermute | solution.py:390
  34.3 15.0 %collective-permute-start.11 = (f32[128,128]{1,0:T(8,128)S(1)}, f32[128,128]{1,0:T(8,128)S(1)}, u32[]{:S(2)}, u32[]{:S(2)}) collective-permute-start(f32[128,128]{1,0:T(8,128)S(1)} %get-tuple-element.54), channel_id=1, source_target_pairs={{0,8},{1,9},{2,10},{3,11},{4,12},{5,13},{6,14},{7,15},{8,0},{9,1},... | collective-permute-start | bytes 196616 | tf_op jit(solution)/shard_map/ppermute | solution.py:390
  35.9 13.4 %collective-permute-start.12 = (f32[128,128]{1,0:T(8,128)S(1)}, f32[128,128]{1,0:T(8,128)S(1)}, u32[]{:S(2)}, u32[]{:S(2)}) collective-permute-start(f32[128,128]{1,0:T(8,128)S(1)} %get-tuple-element.55), channel_id=1, source_target_pairs={{0,16},{1,17},{2,18},{3,19},{4,20},{5,21},{6,22},{7,23},{8,24},{9,... | collective-permute-start | bytes 196616 | tf_op jit(solution)/shard_map/ppermute | solution.py:390
  38.5 10.8 %collective-permute-start.13 = (f32[128,128]{1,0:T(8,128)S(1)}, f32[128,128]{1,0:T(8,128)S(1)}, u32[]{:S(2)}, u32[]{:S(2)}) collective-permute-start(f32[128,128]{1,0:T(8,128)S(1)} %get-tuple-element.56), channel_id=1, source_target_pairs={{0,24},{1,25},{2,26},{3,27},{4,28},{5,29},{6,30},{7,31},{8,16},{9,... | collective-permute-start | bytes 196616 | tf_op jit(solution)/shard_map/ppermute | solution.py:390
  38.7 10.6 %collective-permute-start.5 = (f32[120,128]{1,0:T(8,128)S(1)}, f32[120,128]{1,0:T(8,128)S(1)}, u32[]{:S(2)}, u32[]{:S(2)}) collective-permute-start(f32[120,128]{1,0:T(8,128)S(1)} %get-tuple-element.46), channel_id=1, source_target_pairs={{0,16},{1,17},{2,18},{3,19},{4,20},{5,21},{6,22},{7,23},{8,24},{9,... | collective-permute-start | bytes 184328 | tf_op jit(solution)/shard_map/ppermute | solution.py:390
  40.4 8.9 %collective-permute-start.6 = (f32[120,128]{1,0:T(8,128)S(1)}, f32[120,128]{1,0:T(8,128)S(1)}, u32[]{:S(2)}, u32[]{:S(2)}) collective-permute-start(f32[120,128]{1,0:T(8,128)S(1)} %get-tuple-element.47), channel_id=1, source_target_pairs={{0,24},{1,25},{2,26},{3,27},{4,28},{5,29},{6,30},{7,31},{8,16},{9,... | collective-permute-start | bytes 184328 | tf_op jit(solution)/shard_map/ppermute | solution.py:390

commit v4 on v3

--- a/solution.py
+++ b/solution.py
@@ -413,6 +413,9 @@
     chunks.append(merge(plan, 0, spans[-1], True, tile_owner, pair, coefs))
     for stage in range(1, stages):
         for i, span in enumerate(spans):
+            if stage + 1 == stages and i > 0:
+                far, chunks[i] = lax.optimization_barrier((chunks[i - 1][2:], chunks[i]))
+                chunks[i - 1] = chunks[i - 1][:2] + far
             chunks[i] = exchange(plan, stage, chunks[i])
             if stage + 1 < stages:
                 riding = i + 1 == len(spans)

time: 52.1 us -> 47.6 us (0.914)
  waiting for transfers between devices: 13.1 us -> 9.88 us
  starting transfers between devices: 18.4 us -> 17.1 us
    ppermute x14, waiting for transfers between devices: 13.1 us -> 9.88 us  [exchange(): received.append(lax.ppermute(blocks[digit], AXIS, pairs))]
    ppermute x14, starting transfers between devices: 18.4 us -> 17.1 us  [exchange(): received.append(lax.ppermute(blocks[digit], AXIS, pairs))]
  transfers between devices with their start and end apart: 14 -> 14, of which waited for: 4 -> 4; matrix products, arithmetic and copies ran while one was open for 0% -> 0% of each run, Pallas kernels for 23% -> 25%
where the time goes in v4:
time: 47.6 us; the launch traced here: 47.4 us
  Pallas kernels  20.3 us (43%)
  starting transfers between devices  17.1 us (36%)
  waiting for transfers between devices  9.88 us (21%)
    ppermute x14, starting transfers between devices, exchange(): received.append(lax.ppermute(blocks[digit], AXIS, pairs))  17.1 us
    ppermute x14, waiting for transfers between devices, exchange(): received.append(lax.ppermute(blocks[digit], AXIS, pairs))  9.88 us
    pallas_call x2, Pallas kernels, local_coefs(): pl.pallas_call(functools.partial(coef_kernel, first, steps), name='coefs'...  9.32 us
    pallas_call x1, Pallas kernels, sample(): pl.pallas_call(functools.partial(sample_kernel, plan), name='sample', in_...  4.82 us
    pallas_call x4, Pallas kernels, merge(): pl.pallas_call(functools.partial(merge_kernel, plan, stage, span, len(coe...  3.59 us
    pallas_call x1, Pallas kernels, finish(): pl.pallas_call(functools.partial(finish_kernel, plan, comps, spans), name...  2.57 us
  transfers between devices with their start and end apart: 14, of which 4 were waited for; matrix products, arithmetic and copies ran while one was open for 0% of the time, Pallas kernels for 25%

profile of v4, /device:TPU:0, one launch (start us, length us, event | category | flops | bytes accessed | tf_op | source)
XLA Modules:
  0.0 47.4 jit_solution(11244214841108001284)
XLA Ops:
  0.0 4.8 %sample.1 = (f32[2640,128]{1,0:T(8,128)S(1)}, f32[2640,128]{1,0:T(8,128)S(1)}) custom-call(s32[48]{0:T(128)} %block_ids.1, s32[48]{0:T(128)} %tile_ids.1, s32[128]{0:T(128)} %tile_owner.11, f32[80,32768]{1,0:T(8,128)} %series.5, bf16[48,256,128]{2,1,0:T(8,128)(2,1)} %weights.1), custom_call_target="tpu_custom_call" | custom-call | tf_op jit(solution)/shard_map/sample/pallas_call | solution.py:144
  4.8 0.5 %collective-permute-start = (f32[2640,128]{1,0:T(8,128)S(1)}, f32[2640,128]{1,0:T(8,128)S(1)}, u32[]{:S(2)}, u32[]{:S(2)}) collective-permute-start(f32[2640,128]{1,0:T(8,128)S(1)} %get-tuple-element.40), channel_id=1, source_target_pairs={{0,1},{1,0},{2,3},{3,2},{4,5},{5,4},{6,7},{7,6},{8,9},{9,8},{10,11... | collective-permute-start | bytes 4055048 | tf_op jit(solution)/shard_map/ppermute | solution.py:390
  5.3 3.6 %coefs.2.before = f32[8,128]{1,0:T(8,128)S(1)} custom-call(f32[80,32768]{1,0:T(8,128)} %series.5, s32[1,32768]{1,0:T(1,128)} %bitcast.4, f32[5,80]{1,0:T(8,128)S(1)} %bitcast.2, f32[8,128]{1,0:T(8,128)S(1)} %broadcast_in_dim.3.before), custom_call_target="tpu_custom_call" | custom-call | flops 314572800 | bytes 3932160 | tf_op jit(solution)/shard_map/coefs/pallas_call | solution.py:222
  9.0 0.0 collective-permute-done.refs_1_
  9.0 0.9 %merge.4 = (f32[320,128]{1,0:T(8,128)S(1)}, f32[320,128]{1,0:T(8,128)S(1)}, f32[320,128]{1,0:T(8,128)S(1)}, f32[320,128]{1,0:T(8,128)S(1)}) custom-call(s32[128]{0:T(128)} %tile_owner.11, f32[2640,128]{1,0:T(8,128)S(1)} %get-tuple-element.39.refs_0_, f32[2640,128]{1,0:T(8,128)S(1)} %collective-permute-done.refs_1_), custom_call_target="tpu_custom_call" | custom-call | tf_op jit(solution)/shard_map/merge/pallas_call | solution.py:323
  9.9 2.6 %collective-permute-start.1 = (f32[320,128]{1,0:T(8,128)S(1)}, f32[320,128]{1,0:T(8,128)S(1)}, u32[]{:S(2)}, u32[]{:S(2)}) collective-permute-start(f32[320,128]{1,0:T(8,128)S(1)} %get-tuple-element.47), channel_id=1, source_target_pairs={{0,2},{1,3},{2,0},{3,1},{4,6},{5,7},{6,4},{7,5},{8,10},{9,11},{10,... | collective-permute-start | bytes 491528 | tf_op jit(solution)/shard_map/ppermute | solution.py:390
  12.5 1.5 %collective-permute-start.2 = (f32[320,128]{1,0:T(8,128)S(1)}, f32[320,128]{1,0:T(8,128)S(1)}, u32[]{:S(2)}, u32[]{:S(2)}) collective-permute-start(f32[320,128]{1,0:T(8,128)S(1)} %get-tuple-element.48), channel_id=1, source_target_pairs={{0,4},{1,5},{2,6},{3,7},{4,0},{5,1},{6,2},{7,3},{8,12},{9,13},{10,... | collective-permute-start | bytes 491528 | tf_op jit(solution)/shard_map/ppermute | solution.py:390
  14.0 0.0 collective-permute-start.3
  14.1 5.7 %coefs.3.refs_2_ = f32[8,128]{1,0:T(8,128)S(1)} custom-call(f32[80,32768]{1,0:T(8,128)} %series.5, s32[1,32768]{1,0:T(1,128)} %bitcast.5, f32[5,80]{1,0:T(8,128)S(1)} %bitcast.3, f32[8,128]{1,0:T(8,128)S(1)} %coefs.2.before), custom_call_target="tpu_custom_call" | custom-call | flops 524288000 | bytes 6553600 | tf_op jit(solution)/shard_map/coefs/pallas_call | solution.py:222
  19.8 0.1 collective-permute-start.7
  19.8 1.2 %collective-permute-done.7.refs_3_ = f32[8,128]{1,0:T(8,128)S(1)} collective-permute-done((f32[8,128]{1,0:T(8,128)S(1)}, f32[8,128]{1,0:T(8,128)S(1)}, u32[]{:S(2)}, u32[]{:S(2)}) %collective-permute-start.7) | collective-permute-done | bytes 4128 | tf_op jit(solution)/shard_map/ppermute | solution.py:390
  21.0 0.9 %merge.6 = (f32[328,128]{1,0:T(8,128)S(1)}, f32[328,128]{1,0:T(8,128)S(1)}, f32[328,128]{1,0:T(8,128)S(1)}, f32[328,128]{1,0:T(8,128)S(1)}) custom-call(s32[128]{0:T(128)} %tile_owner.11, f32[2640,128]{1,0:T(8,128)S(1)} %get-tuple-element.39.refs_0_, f32[2640,128]{1,0:T(8,128)S(1)} %collective-permute-done.refs_1_, f32[8,128]{1,0:T(8,128)S(1)} %coefs.3.refs_2_, ...), custom_call_target="tpu_custom_call" | custom-call | tf_op jit(solution)/shard_map/merge/pallas_call | solution.py:323
  21.9 3.0 %collective-permute-start.10 = (f32[328,128]{1,0:T(8,128)S(1)}, f32[328,128]{1,0:T(8,128)S(1)}, u32[]{:S(2)}, u32[]{:S(2)}) collective-permute-start(f32[328,128]{1,0:T(8,128)S(1)} %get-tuple-element.58), channel_id=1, source_target_pairs={{0,6},{1,7},{2,4},{3,5},{4,2},{5,3},{6,0},{7,1},{8,14},{9,15},{10,... | collective-permute-start | bytes 503816 | tf_op jit(solution)/shard_map/ppermute | solution.py:390
  24.9 0.5 %collective-permute-start.8 = (f32[328,128]{1,0:T(8,128)S(1)}, f32[328,128]{1,0:T(8,128)S(1)}, u32[]{:S(2)}, u32[]{:S(2)}) collective-permute-start(f32[328,128]{1,0:T(8,128)S(1)} %get-tuple-element.56), channel_id=1, source_target_pairs={{0,2},{1,3},{2,0},{3,1},{4,6},{5,7},{6,4},{7,5},{8,10},{9,11},{10,... | collective-permute-start | bytes 503816 | tf_op jit(solution)/shard_map/ppermute | solution.py:390
  25.4 0.0 collective-permute-done.1.refs_1_
  25.4 0.1 collective-permute-start.9
  25.6 0.0 collective-permute-done.2.refs_2_
  25.6 0.0 collective-permute-done.3.refs_3_
  25.6 0.9 %merge.5 = (f32[120,128]{1,0:T(8,128)S(1)}, f32[120,128]{1,0:T(8,128)S(1)}, f32[120,128]{1,0:T(8,128)S(1)}, f32[120,128]{1,0:T(8,128)S(1)}) custom-call(s32[128]{0:T(128)} %tile_owner.11, f32[320,128]{1,0:T(8,128)S(1)} %get-tuple-element.46.refs_0_, f32[320,128]{1,0:T(8,128)S(1)} %collective-permute-done.1.refs_1_, ...), custom_call_target="tpu_custom_call" | custom-call | tf_op jit(solution)/shard_map/merge/pallas_call | solution.py:323
  26.4 3.1 %collective-permute-start.5 = (f32[120,128]{1,0:T(8,128)S(1)}, f32[120,128]{1,0:T(8,128)S(1)}, u32[]{:S(2)}, u32[]{:S(2)}) collective-permute-start(f32[120,128]{1,0:T(8,128)S(1)} %get-tuple-element.52), channel_id=1, source_target_pairs={{0,16},{1,17},{2,18},{3,19},{4,20},{5,21},{6,22},{7,23},{8,24},{9,... | collective-permute-start | bytes 184328 | tf_op jit(solution)/shard_map/ppermute | solution.py:390
  29.5 1.3 %collective-permute-start.6 = (f32[120,128]{1,0:T(8,128)S(1)}, f32[120,128]{1,0:T(8,128)S(1)}, u32[]{:S(2)}, u32[]{:S(2)}) collective-permute-start(f32[120,128]{1,0:T(8,128)S(1)} %get-tuple-element.53), channel_id=1, source_target_pairs={{0,24},{1,25},{2,26},{3,27},{4,28},{5,29},{6,30},{7,31},{8,16},{9,... | collective-permute-start | bytes 184328 | tf_op jit(solution)/shard_map/ppermute | solution.py:390
  30.8 0.0 collective-permute-done.10.refs_3_
  30.8 2.6 %collective-permute-done.8.refs_1_ = f32[328,128]{1,0:T(8,128)S(1)} collective-permute-done((f32[328,128]{1,0:T(8,128)S(1)}, f32[328,128]{1,0:T(8,128)S(1)}, u32[]{:S(2)}, u32[]{:S(2)}) %collective-permute-start.8) | collective-permute-done | bytes 167968 | tf_op jit(solution)/shard_map/ppermute | solution.py:390
  33.4 0.0 collective-permute-done.9.refs_2_
  33.4 0.9 %merge.7 = (f32[128,128]{1,0:T(8,128)S(1)}, f32[128,128]{1,0:T(8,128)S(1)}, f32[128,128]{1,0:T(8,128)S(1)}, f32[128,128]{1,0:T(8,128)S(1)}) custom-call(s32[128]{0:T(128)} %tile_owner.11, f32[328,128]{1,0:T(8,128)S(1)} %get-tuple-element.55.refs_0_, f32[328,128]{1,0:T(8,128)S(1)} %collective-permute-done.8.refs_1_, ...), custom_call_target="tpu_custom_call" | custom-call | tf_op jit(solution)/shard_map/merge/pallas_call | solution.py:323
  34.3 1.2 %collective-permute-done.6.refs_3_ = f32[120,128]{1,0:T(8,128)S(1)} collective-permute-done((f32[120,128]{1,0:T(8,128)S(1)}, f32[120,128]{1,0:T(8,128)S(1)}, u32[]{:S(2)}, u32[]{:S(2)}) %collective-permute-start.6) | collective-permute-done | bytes 61472 | tf_op jit(solution)/shard_map/ppermute | solution.py:390
  35.5 0.4 collective-permute-start.11
  36.0 2.6 %collective-permute-start.12 = (f32[128,128]{1,0:T(8,128)S(1)}, f32[128,128]{1,0:T(8,128)S(1)}, u32[]{:S(2)}, u32[]{:S(2)}) collective-permute-start(f32[128,128]{1,0:T(8,128)S(1)} %get-tuple-element.67), channel_id=1, source_target_pairs={{0,16},{1,17},{2,18},{3,19},{4,20},{5,21},{6,22},{7,23},{8,24},{9,... | collective-permute-start | bytes 196616 | tf_op jit(solution)/shard_map/ppermute | solution.py:390
  38.5 1.3 %collective-permute-start.13 = (f32[128,128]{1,0:T(8,128)S(1)}, f32[128,128]{1,0:T(8,128)S(1)}, u32[]{:S(2)}, u32[]{:S(2)}) collective-permute-start(f32[128,128]{1,0:T(8,128)S(1)} %get-tuple-element.68), channel_id=1, source_target_pairs={{0,24},{1,25},{2,26},{3,27},{4,28},{5,29},{6,30},{7,31},{8,16},{9,... | collective-permute-start | bytes 196616 | tf_op jit(solution)/shard_map/ppermute | solution.py:390
  39.9 4.9 %collective-permute-done.4.refs_1_ = f32[120,128]{1,0:T(8,128)S(1)} collective-permute-done((f32[120,128]{1,0:T(8,128)S(1)}, f32[120,128]{1,0:T(8,128)S(1)}, u32[]{:S(2)}, u32[]{:S(2)}) %collective-permute-start.4) | collective-permute-done | bytes 61472 | tf_op jit(solution)/shard_map/ppermute | solution.py:390
  44.8 0.0 collective-permute-done.13.refs_7_
  44.8 2.6 %finish.1 = f32[4,80,128]{2,1,0:T(8,128)} custom-call(s32[128]{0:T(128)} %tile_owner.11, f32[120,128]{1,0:T(8,128)S(1)} %get-tuple-element.50.refs_0_, f32[120,128]{1,0:T(8,128)S(1)} %collective-permute-done.4.refs_1_, f32[120,128]{1,0:T(8,128)S(1)} %collective-permute-done.5.refs_2_, f32[120,128]{1,0:T(8,128)S(1)} %collective-permute-done.6.refs_3_, ...), custom_call_target="tpu_custom_call" | custom-call | tf_op jit(solution)/shard_map/finish/pallas_call | solution.py:375
  (7 shorter events, 0.0 us)
Async XLA Ops:
  0.0 5.3 %copy-start = (f32[80,5]{0,1:T(8,128)S(1)}, f32[80,5]{0,1:T(8,128)}, u32[]{:S(2)}) copy-start(f32[80,5]{0,1:T(8,128)} %param.9) | copy-start | bytes 4804
  4.8 4.2 %collective-permute-start = (f32[2640,128]{1,0:T(8,128)S(1)}, f32[2640,128]{1,0:T(8,128)S(1)}, u32[]{:S(2)}, u32[]{:S(2)}) collective-permute-start(f32[2640,128]{1,0:T(8,128)S(1)} %get-tuple-element.40), channel_id=1, source_target_pairs={{0,1},{1,0},{2,3},{3,2},{4,5},{5,4},{6,7},{7,6},{8,9},{9,8},{10,11... | collective-permute-start | bytes 4055048 | tf_op jit(solution)/shard_map/ppermute | solution.py:390
  9.9 15.5 %collective-permute-start.1 = (f32[320,128]{1,0:T(8,128)S(1)}, f32[320,128]{1,0:T(8,128)S(1)}, u32[]{:S(2)}, u32[]{:S(2)}) collective-permute-start(f32[320,128]{1,0:T(8,128)S(1)} %get-tuple-element.47), channel_id=1, source_target_pairs={{0,2},{1,3},{2,0},{3,1},{4,6},{5,7},{6,4},{7,5},{8,10},{9,11},{10,... | collective-permute-start | bytes 491528 | tf_op jit(solution)/shard_map/ppermute | solution.py:390
  12.5 13.0 %collective-permute-start.2 = (f32[320,128]{1,0:T(8,128)S(1)}, f32[320,128]{1,0:T(8,128)S(1)}, u32[]{:S(2)}, u32[]{:S(2)}) collective-permute-start(f32[320,128]{1,0:T(8,128)S(1)} %get-tuple-element.48), channel_id=1, source_target_pairs={{0,4},{1,5},{2,6},{3,7},{4,0},{5,1},{6,2},{7,3},{8,12},{9,13},{10,... | collective-permute-start | bytes 491528 | tf_op jit(solution)/shard_map/ppermute | solution.py:390
  14.0 11.5 %collective-permute-start.3 = (f32[320,128]{1,0:T(8,128)S(1)}, f32[320,128]{1,0:T(8,128)S(1)}, u32[]{:S(2)}, u32[]{:S(2)}) collective-permute-start(f32[320,128]{1,0:T(8,128)S(1)} %get-tuple-element.49), channel_id=1, source_target_pairs={{0,6},{1,7},{2,4},{3,5},{4,2},{5,3},{6,0},{7,1},{8,14},{9,15},{10,... | collective-permute-start | bytes 491528 | tf_op jit(solution)/shard_map/ppermute | solution.py:390
  19.8 1.2 %collective-permute-start.7 = (f32[8,128]{1,0:T(8,128)S(1)}, f32[8,128]{1,0:T(8,128)S(1)}, u32[]{:S(2)}, u32[]{:S(2)}) collective-permute-start(f32[8,128]{1,0:T(8,128)S(1)} %coefs.3.refs_2_), channel_id=1, source_target_pairs={{0,1},{1,0},{2,3},{3,2},{4,5},{5,4},{6,7},{7,6},{8,9},{9,8},{10,11... | collective-permute-start | bytes 12296 | tf_op jit(solution)/shard_map/ppermute | solution.py:390
  21.9 8.9 %collective-permute-start.10 = (f32[328,128]{1,0:T(8,128)S(1)}, f32[328,128]{1,0:T(8,128)S(1)}, u32[]{:S(2)}, u32[]{:S(2)}) collective-permute-start(f32[328,128]{1,0:T(8,128)S(1)} %get-tuple-element.58), channel_id=1, source_target_pairs={{0,6},{1,7},{2,4},{3,5},{4,2},{5,3},{6,0},{7,1},{8,14},{9,15},{10,... | collective-permute-start | bytes 503816 | tf_op jit(solution)/shard_map/ppermute | solution.py:390
  24.9 8.5 %collective-permute-start.8 = (f32[328,128]{1,0:T(8,128)S(1)}, f32[328,128]{1,0:T(8,128)S(1)}, u32[]{:S(2)}, u32[]{:S(2)}) collective-permute-start(f32[328,128]{1,0:T(8,128)S(1)} %get-tuple-element.56), channel_id=1, source_target_pairs={{0,2},{1,3},{2,0},{3,1},{4,6},{5,7},{6,4},{7,5},{8,10},{9,11},{10,... | collective-permute-start | bytes 503816 | tf_op jit(solution)/shard_map/ppermute | solution.py:390
  25.4 8.0 %collective-permute-start.9 = (f32[328,128]{1,0:T(8,128)S(1)}, f32[328,128]{1,0:T(8,128)S(1)}, u32[]{:S(2)}, u32[]{:S(2)}) collective-permute-start(f32[328,128]{1,0:T(8,128)S(1)} %get-tuple-element.57), channel_id=1, source_target_pairs={{0,4},{1,5},{2,6},{3,7},{4,0},{5,1},{6,2},{7,3},{8,12},{9,13},{10,... | collective-permute-start | bytes 503816 | tf_op jit(solution)/shard_map/ppermute | solution.py:390
  26.4 7.9 %collective-permute-start.5 = (f32[120,128]{1,0:T(8,128)S(1)}, f32[120,128]{1,0:T(8,128)S(1)}, u32[]{:S(2)}, u32[]{:S(2)}) collective-permute-start(f32[120,128]{1,0:T(8,128)S(1)} %get-tuple-element.52), channel_id=1, source_target_pairs={{0,16},{1,17},{2,18},{3,19},{4,20},{5,21},{6,22},{7,23},{8,24},{9,... | collective-permute-start | bytes 184328 | tf_op jit(solution)/shard_map/ppermute | solution.py:390
  29.5 6.0 %collective-permute-start.6 = (f32[120,128]{1,0:T(8,128)S(1)}, f32[120,128]{1,0:T(8,128)S(1)}, u32[]{:S(2)}, u32[]{:S(2)}) collective-permute-start(f32[120,128]{1,0:T(8,128)S(1)} %get-tuple-element.53), channel_id=1, source_target_pairs={{0,24},{1,25},{2,26},{3,27},{4,28},{5,29},{6,30},{7,31},{8,16},{9,... | collective-permute-start | bytes 184328 | tf_op jit(solution)/shard_map/ppermute | solution.py:390
  35.5 9.3 %collective-permute-start.11 = (f32[128,128]{1,0:T(8,128)S(1)}, f32[128,128]{1,0:T(8,128)S(1)}, u32[]{:S(2)}, u32[]{:S(2)}) collective-permute-start(f32[128,128]{1,0:T(8,128)S(1)} %get-tuple-element.66), channel_id=1, source_target_pairs={{0,8},{1,9},{2,10},{3,11},{4,12},{5,13},{6,14},{7,15},{8,0},{9,1},... | collective-permute-start | bytes 196616 | tf_op jit(solution)/shard_map/ppermute | solution.py:390
  36.0 8.9 %collective-permute-start.12 = (f32[128,128]{1,0:T(8,128)S(1)}, f32[128,128]{1,0:T(8,128)S(1)}, u32[]{:S(2)}, u32[]{:S(2)}) collective-permute-start(f32[128,128]{1,0:T(8,128)S(1)} %get-tuple-element.67), channel_id=1, source_target_pairs={{0,16},{1,17},{2,18},{3,19},{4,20},{5,21},{6,22},{7,23},{8,24},{9,... | collective-permute-start | bytes 196616 | tf_op jit(solution)/shard_map/ppermute | solution.py:390
  38.5 6.3 %collective-permute-start.13 = (f32[128,128]{1,0:T(8,128)S(1)}, f32[128,128]{1,0:T(8,128)S(1)}, u32[]{:S(2)}, u32[]{:S(2)}) collective-permute-start(f32[128,128]{1,0:T(8,128)S(1)} %get-tuple-element.68), channel_id=1, source_target_pairs={{0,24},{1,25},{2,26},{3,27},{4,28},{5,29},{6,30},{7,31},{8,16},{9,... | collective-permute-start | bytes 196616 | tf_op jit(solution)/shard_map/ppermute | solution.py:390
  39.9 4.9 %collective-permute-start.4 = (f32[120,128]{1,0:T(8,128)S(1)}, f32[120,128]{1,0:T(8,128)S(1)}, u32[]{:S(2)}, u32[]{:S(2)}) collective-permute-start(f32[120,128]{1,0:T(8,128)S(1)} %get-tuple-element.51), channel_id=1, source_target_pairs={{0,8},{1,9},{2,10},{3,11},{4,12},{5,13},{6,14},{7,15},{8,0},{9,1},... | collective-permute-start | bytes 184328 | tf_op jit(solution)/shard_map/ppermute | solution.py:390

commit v5 on v4

--- a/solution.py
+++ b/solution.py
@@ -11,7 +11,8 @@
 HIGHEST = lax.Precision.HIGHEST
 LANES = 128
 COEF_ROWS = 8
-GROUP = 8
+GROUP = 16
+AHEAD = 3
 WIDE = 256
 COEF_STEP = 4096
 EARLY = 3
@@ -175,13 +176,18 @@
         mask.at[:, pl.ds(first * columns, steps * columns)], marks, mark_sem
     )
     mark_copy.start()
-    for step in range(steps):
+    for step in range(min(AHEAD, steps)):
         fetch(step).start()
     gram[...] = jnp.zeros_like(gram)
     mark_copy.wait()
 
     def chunk(step, carry):
         fetch(step).wait()
+
+        @pl.when(step + AHEAD < steps)
+        def _():
+            fetch(step + AHEAD).start()
+
         start = step * columns
         for at in range(0, columns, WIDE):
             span = pl.ds(pl.multiple_of(start + at, WIDE), WIDE)
@@ -328,7 +334,7 @@
         out_shape=[block] * fan,
         scratch_shapes=[pltpu.SMEM((plan.devices,), jnp.int32)],
         compiler_params=pltpu.CompilerParams(vmem_limit_bytes=32 << 20),
-    )(in_hbm(tile_owner), *arrays)
+    )(tile_owner, *arrays)
 
 
 def finish_kernel(plan, comps, spans, tile_owner, *refs):
@@ -345,9 +351,10 @@
     unit = jnp.zeros_like(basis)
     for i in range(comps):
         line = basis[i : i + 1, :]
-        line = line * lax.rsqrt(jnp.sum(line * line, axis=1, keepdims=True))
-        unit = jnp.where(row == i, line, unit)
-        basis = basis - jnp.sum(basis * line, axis=1, keepdims=True) * line
+        dots = jnp.sum(basis * line, axis=1, keepdims=True)
+        square = dots[i : i + 1, :]
+        unit = jnp.where(row == i, line * lax.rsqrt(square), unit)
+        basis = basis - dots * (line / square)
     unit = unit[:, 0:frames]
     values = []
     for slot in range(plan.owned):
@@ -380,7 +387,7 @@
         out_shape=jax.ShapeDtypeStruct((plan.owned, plan.frames, plan.tile_width), jnp.float32),
         scratch_shapes=[pltpu.SMEM((plan.devices,), jnp.int32)],
         compiler_params=pltpu.CompilerParams(vmem_limit_bytes=32 << 20),
-    )(in_hbm(tile_owner), *arrays)
+    )(tile_owner, *arrays)
 
 
 def exchange(plan, stage, blocks):

time: 47.6 us -> 46.1 us (0.968)
  Pallas kernels: 20.3 us -> 18.7 us
    pallas_call x2, Pallas kernels: 9.32 us -> 8.47 us  [local_coefs(): pl.pallas_call(functools.partial(coef_kernel, first, steps), name='coefs'...]
    pallas_call x4, Pallas kernels: 3.59 us -> 3.1 us  [merge(): pl.pallas_call(functools.partial(merge_kernel, plan, stage, span, len(coe...]
  transfers between devices with their start and end apart: 14 -> 14, of which waited for: 4 -> 4; matrix products, arithmetic and copies ran while one was open for 0% -> 0% of each run, Pallas kernels for 25% -> 23%
where the time goes in v5:
time: 46.1 us; the launch traced here: 46 us
  Pallas kernels  18.7 us (41%)
  starting transfers between devices  17.1 us (37%)
  waiting for transfers between devices  10 us (22%)
    ppermute x14, starting transfers between devices, exchange(): received.append(lax.ppermute(blocks[digit], AXIS, pairs))  17.1 us
    ppermute x14, waiting for transfers between devices, exchange(): received.append(lax.ppermute(blocks[digit], AXIS, pairs))  10 us
    pallas_call x2, Pallas kernels, local_coefs(): pl.pallas_call(functools.partial(coef_kernel, first, steps), name='coefs'...  8.47 us
    pallas_call x1, Pallas kernels, sample(): pl.pallas_call(functools.partial(sample_kernel, plan), name='sample', in_...  5.03 us
    pallas_call x4, Pallas kernels, merge(): pl.pallas_call(functools.partial(merge_kernel, plan, stage, span, len(coe...  3.1 us
    pallas_call x1, Pallas kernels, finish(): pl.pallas_call(functools.partial(finish_kernel, plan, comps, spans), name...  2.14 us
  transfers between devices with their start and end apart: 14, of which 4 were waited for; matrix products, arithmetic and copies ran while one was open for 0% of the time, Pallas kernels for 23%

profile of v5, /device:TPU:0, one launch (start us, length us, event | category | flops | bytes accessed | tf_op | source)
XLA Modules:
  0.0 46.0 jit_solution(11268529601643051500)
XLA Ops:
  0.0 5.0 %sample.1 = (f32[2640,128]{1,0:T(8,128)S(1)}, f32[2640,128]{1,0:T(8,128)S(1)}) custom-call(s32[48]{0:T(128)} %block_ids.1, s32[48]{0:T(128)} %tile_ids.1, s32[128]{0:T(128)} %tile_owner.11, f32[80,32768]{1,0:T(8,128)} %series.5, bf16[48,256,128]{2,1,0:T(8,128)(2,1)} %weights.1), custom_call_target="tpu_custom_call" | custom-call | tf_op jit(solution)/shard_map/sample/pallas_call | solution.py:145
  5.0 0.5 %collective-permute-start = (f32[2640,128]{1,0:T(8,128)S(1)}, f32[2640,128]{1,0:T(8,128)S(1)}, u32[]{:S(2)}, u32[]{:S(2)}) collective-permute-start(f32[2640,128]{1,0:T(8,128)S(1)} %get-tuple-element.40), channel_id=1, source_target_pairs={{0,1},{1,0},{2,3},{3,2},{4,5},{5,4},{6,7},{7,6},{8,9},{9,8},{10,11... | collective-permute-start | bytes 4055048 | tf_op jit(solution)/shard_map/ppermute | solution.py:397
  5.6 3.6 %coefs.2.before = f32[8,128]{1,0:T(8,128)S(1)} custom-call(f32[80,32768]{1,0:T(8,128)} %series.5, s32[1,32768]{1,0:T(1,128)} %bitcast.4, f32[5,80]{1,0:T(8,128)S(1)} %bitcast.2, f32[8,128]{1,0:T(8,128)S(1)} %broadcast_in_dim.3.before), custom_call_target="tpu_custom_call" | custom-call | flops 314572800 | bytes 3932160 | tf_op jit(solution)/shard_map/coefs/pallas_call | solution.py:228
  9.2 0.0 collective-permute-done.refs_1_
  9.2 0.8 %merge.4 = (f32[320,128]{1,0:T(8,128)S(1)}, f32[320,128]{1,0:T(8,128)S(1)}, f32[320,128]{1,0:T(8,128)S(1)}, f32[320,128]{1,0:T(8,128)S(1)}) custom-call(s32[128]{0:T(128)S(1)} %copy-done, f32[2640,128]{1,0:T(8,128)S(1)} %get-tuple-element.39.refs_0_, f32[2640,128]{1,0:T(8,128)S(1)} %collective-permute-done.refs_1_), custom_call_target="tpu_custom_call" | custom-call | tf_op jit(solution)/shard_map/merge/pallas_call | solution.py:329
  10.0 2.6 %collective-permute-start.1 = (f32[320,128]{1,0:T(8,128)S(1)}, f32[320,128]{1,0:T(8,128)S(1)}, u32[]{:S(2)}, u32[]{:S(2)}) collective-permute-start(f32[320,128]{1,0:T(8,128)S(1)} %get-tuple-element.47), channel_id=1, source_target_pairs={{0,2},{1,3},{2,0},{3,1},{4,6},{5,7},{6,4},{7,5},{8,10},{9,11},{10,... | collective-permute-start | bytes 491528 | tf_op jit(solution)/shard_map/ppermute | solution.py:397
  12.6 1.5 %collective-permute-start.2 = (f32[320,128]{1,0:T(8,128)S(1)}, f32[320,128]{1,0:T(8,128)S(1)}, u32[]{:S(2)}, u32[]{:S(2)}) collective-permute-start(f32[320,128]{1,0:T(8,128)S(1)} %get-tuple-element.48), channel_id=1, source_target_pairs={{0,4},{1,5},{2,6},{3,7},{4,0},{5,1},{6,2},{7,3},{8,12},{9,13},{10,... | collective-permute-start | bytes 491528 | tf_op jit(solution)/shard_map/ppermute | solution.py:397
  14.1 0.0 collective-permute-start.3
  14.1 4.9 %coefs.3.refs_2_ = f32[8,128]{1,0:T(8,128)S(1)} custom-call(f32[80,32768]{1,0:T(8,128)} %series.5, s32[1,32768]{1,0:T(1,128)} %bitcast.5, f32[5,80]{1,0:T(8,128)S(1)} %bitcast.3, f32[8,128]{1,0:T(8,128)S(1)} %coefs.2.before), custom_call_target="tpu_custom_call" | custom-call | flops 524288000 | bytes 6553600 | tf_op jit(solution)/shard_map/coefs/pallas_call | solution.py:228
  19.0 0.1 collective-permute-start.7
  19.1 1.2 %collective-permute-done.7.refs_3_ = f32[8,128]{1,0:T(8,128)S(1)} collective-permute-done((f32[8,128]{1,0:T(8,128)S(1)}, f32[8,128]{1,0:T(8,128)S(1)}, u32[]{:S(2)}, u32[]{:S(2)}) %collective-permute-start.7) | collective-permute-done | bytes 4128 | tf_op jit(solution)/shard_map/ppermute | solution.py:397
  20.2 0.8 %merge.6 = (f32[328,128]{1,0:T(8,128)S(1)}, f32[328,128]{1,0:T(8,128)S(1)}, f32[328,128]{1,0:T(8,128)S(1)}, f32[328,128]{1,0:T(8,128)S(1)}) custom-call(s32[128]{0:T(128)S(1)} %copy-done, f32[2640,128]{1,0:T(8,128)S(1)} %get-tuple-element.39.refs_0_, f32[2640,128]{1,0:T(8,128)S(1)} %collective-permute-done.refs_1_, f32[8,128]{1,0:T(8,128)S(1)} %coefs.3.refs_2_, ...), custom_call_target="tpu_custom_call" | custom-call | tf_op jit(solution)/shard_map/merge/pallas_call | solution.py:329
  21.1 3.0 %collective-permute-start.10 = (f32[328,128]{1,0:T(8,128)S(1)}, f32[328,128]{1,0:T(8,128)S(1)}, u32[]{:S(2)}, u32[]{:S(2)}) collective-permute-start(f32[328,128]{1,0:T(8,128)S(1)} %get-tuple-element.58), channel_id=1, source_target_pairs={{0,6},{1,7},{2,4},{3,5},{4,2},{5,3},{6,0},{7,1},{8,14},{9,15},{10,... | collective-permute-start | bytes 503816 | tf_op jit(solution)/shard_map/ppermute | solution.py:397
  24.0 0.5 %collective-permute-start.8 = (f32[328,128]{1,0:T(8,128)S(1)}, f32[328,128]{1,0:T(8,128)S(1)}, u32[]{:S(2)}, u32[]{:S(2)}) collective-permute-start(f32[328,128]{1,0:T(8,128)S(1)} %get-tuple-element.56), channel_id=1, source_target_pairs={{0,2},{1,3},{2,0},{3,1},{4,6},{5,7},{6,4},{7,5},{8,10},{9,11},{10,... | collective-permute-start | bytes 503816 | tf_op jit(solution)/shard_map/ppermute | solution.py:397
  24.6 0.0 collective-permute-done.1.refs_1_
  24.6 0.1 collective-permute-start.9
  24.7 0.0 collective-permute-done.2.refs_2_
  24.7 0.0 collective-permute-done.3.refs_3_
  24.7 0.7 %merge.5 = (f32[120,128]{1,0:T(8,128)S(1)}, f32[120,128]{1,0:T(8,128)S(1)}, f32[120,128]{1,0:T(8,128)S(1)}, f32[120,128]{1,0:T(8,128)S(1)}) custom-call(s32[128]{0:T(128)S(1)} %copy-done, f32[320,128]{1,0:T(8,128)S(1)} %get-tuple-element.46.refs_0_, f32[320,128]{1,0:T(8,128)S(1)} %collective-permute-done.1.refs_1_, ...), custom_call_target="tpu_custom_call" | custom-call | tf_op jit(solution)/shard_map/merge/pallas_call | solution.py:329
  25.4 3.1 %collective-permute-start.5 = (f32[120,128]{1,0:T(8,128)S(1)}, f32[120,128]{1,0:T(8,128)S(1)}, u32[]{:S(2)}, u32[]{:S(2)}) collective-permute-start(f32[120,128]{1,0:T(8,128)S(1)} %get-tuple-element.52), channel_id=1, source_target_pairs={{0,16},{1,17},{2,18},{3,19},{4,20},{5,21},{6,22},{7,23},{8,24},{9,... | collective-permute-start | bytes 184328 | tf_op jit(solution)/shard_map/ppermute | solution.py:397
  28.5 1.3 %collective-permute-start.6 = (f32[120,128]{1,0:T(8,128)S(1)}, f32[120,128]{1,0:T(8,128)S(1)}, u32[]{:S(2)}, u32[]{:S(2)}) collective-permute-start(f32[120,128]{1,0:T(8,128)S(1)} %get-tuple-element.53), channel_id=1, source_target_pairs={{0,24},{1,25},{2,26},{3,27},{4,28},{5,29},{6,30},{7,31},{8,16},{9,... | collective-permute-start | bytes 184328 | tf_op jit(solution)/shard_map/ppermute | solution.py:397
  29.8 0.0 collective-permute-done.10.refs_3_
  29.8 2.7 %collective-permute-done.8.refs_1_ = f32[328,128]{1,0:T(8,128)S(1)} collective-permute-done((f32[328,128]{1,0:T(8,128)S(1)}, f32[328,128]{1,0:T(8,128)S(1)}, u32[]{:S(2)}, u32[]{:S(2)}) %collective-permute-start.8) | collective-permute-done | bytes 167968 | tf_op jit(solution)/shard_map/ppermute | solution.py:397
  32.5 0.0 collective-permute-done.9.refs_2_
  32.5 0.7 %merge.7 = (f32[128,128]{1,0:T(8,128)S(1)}, f32[128,128]{1,0:T(8,128)S(1)}, f32[128,128]{1,0:T(8,128)S(1)}, f32[128,128]{1,0:T(8,128)S(1)}) custom-call(s32[128]{0:T(128)S(1)} %copy-done, f32[328,128]{1,0:T(8,128)S(1)} %get-tuple-element.55.refs_0_, f32[328,128]{1,0:T(8,128)S(1)} %collective-permute-done.8.refs_1_, ...), custom_call_target="tpu_custom_call" | custom-call | tf_op jit(solution)/shard_map/merge/pallas_call | solution.py:329
  33.3 1.2 %collective-permute-done.6.refs_3_ = f32[120,128]{1,0:T(8,128)S(1)} collective-permute-done((f32[120,128]{1,0:T(8,128)S(1)}, f32[120,128]{1,0:T(8,128)S(1)}, u32[]{:S(2)}, u32[]{:S(2)}) %collective-permute-start.6) | collective-permute-done | bytes 61472 | tf_op jit(solution)/shard_map/ppermute | solution.py:397
  34.5 0.4 collective-permute-start.11
  35.0 2.6 %collective-permute-start.12 = (f32[128,128]{1,0:T(8,128)S(1)}, f32[128,128]{1,0:T(8,128)S(1)}, u32[]{:S(2)}, u32[]{:S(2)}) collective-permute-start(f32[128,128]{1,0:T(8,128)S(1)} %get-tuple-element.67), channel_id=1, source_target_pairs={{0,16},{1,17},{2,18},{3,19},{4,20},{5,21},{6,22},{7,23},{8,24},{9,... | collective-permute-start | bytes 196616 | tf_op jit(solution)/shard_map/ppermute | solution.py:397
  37.5 1.3 %collective-permute-start.13 = (f32[128,128]{1,0:T(8,128)S(1)}, f32[128,128]{1,0:T(8,128)S(1)}, u32[]{:S(2)}, u32[]{:S(2)}) collective-permute-start(f32[128,128]{1,0:T(8,128)S(1)} %get-tuple-element.68), channel_id=1, source_target_pairs={{0,24},{1,25},{2,26},{3,27},{4,28},{5,29},{6,30},{7,31},{8,16},{9,... | collective-permute-start | bytes 196616 | tf_op jit(solution)/shard_map/ppermute | solution.py:397
  38.9 0.0 collective-permute-start.4
  38.9 4.9 %collective-permute-done.4.refs_1_ = f32[120,128]{1,0:T(8,128)S(1)} collective-permute-done((f32[120,128]{1,0:T(8,128)S(1)}, f32[120,128]{1,0:T(8,128)S(1)}, u32[]{:S(2)}, u32[]{:S(2)}) %collective-permute-start.4) | collective-permute-done | bytes 61472 | tf_op jit(solution)/shard_map/ppermute | solution.py:397
  43.8 2.1 %finish.1 = f32[4,80,128]{2,1,0:T(8,128)} custom-call(s32[128]{0:T(128)S(1)} %copy-done, f32[120,128]{1,0:T(8,128)S(1)} %get-tuple-element.50.refs_0_, f32[120,128]{1,0:T(8,128)S(1)} %collective-permute-done.4.refs_1_, f32[120,128]{1,0:T(8,128)S(1)} %collective-permute-done.5.refs_2_, f32[120,128]{1,0:T(8,128)S(1)} %collective-permute-done.6.refs_3_, ...), custom_call_target="tpu_custom_call" | custom-call | tf_op jit(solution)/shard_map/finish/pallas_call | solution.py:382
  (9 shorter events, 0.0 us)
Async XLA Ops:
  0.0 5.6 %copy-start.1 = (f32[80,5]{0,1:T(8,128)S(1)}, f32[80,5]{0,1:T(8,128)}, u32[]{:S(2)}) copy-start(f32[80,5]{0,1:T(8,128)} %param.9) | copy-start | bytes 4804
  5.0 4.1 %collective-permute-start = (f32[2640,128]{1,0:T(8,128)S(1)}, f32[2640,128]{1,0:T(8,128)S(1)}, u32[]{:S(2)}, u32[]{:S(2)}) collective-permute-start(f32[2640,128]{1,0:T(8,128)S(1)} %get-tuple-element.40), channel_id=1, source_target_pairs={{0,1},{1,0},{2,3},{3,2},{4,5},{5,4},{6,7},{7,6},{8,9},{9,8},{10,11... | collective-permute-start | bytes 4055048 | tf_op jit(solution)/shard_map/ppermute | solution.py:397
  5.6 3.6 %copy-start = (s32[128]{0:T(128)S(1)}, s32[128]{0:T(128)}, u32[]{:S(2)}) copy-start(s32[128]{0:T(128)} %tile_owner.11) | copy-start | bytes 1540
  10.0 14.6 %collective-permute-start.1 = (f32[320,128]{1,0:T(8,128)S(1)}, f32[320,128]{1,0:T(8,128)S(1)}, u32[]{:S(2)}, u32[]{:S(2)}) collective-permute-start(f32[320,128]{1,0:T(8,128)S(1)} %get-tuple-element.47), channel_id=1, source_target_pairs={{0,2},{1,3},{2,0},{3,1},{4,6},{5,7},{6,4},{7,5},{8,10},{9,11},{10,... | collective-permute-start | bytes 491528 | tf_op jit(solution)/shard_map/ppermute | solution.py:397
  12.6 12.1 %collective-permute-start.2 = (f32[320,128]{1,0:T(8,128)S(1)}, f32[320,128]{1,0:T(8,128)S(1)}, u32[]{:S(2)}, u32[]{:S(2)}) collective-permute-start(f32[320,128]{1,0:T(8,128)S(1)} %get-tuple-element.48), channel_id=1, source_target_pairs={{0,4},{1,5},{2,6},{3,7},{4,0},{5,1},{6,2},{7,3},{8,12},{9,13},{10,... | collective-permute-start | bytes 491528 | tf_op jit(solution)/shard_map/ppermute | solution.py:397
  14.1 10.6 %collective-permute-start.3 = (f32[320,128]{1,0:T(8,128)S(1)}, f32[320,128]{1,0:T(8,128)S(1)}, u32[]{:S(2)}, u32[]{:S(2)}) collective-permute-start(f32[320,128]{1,0:T(8,128)S(1)} %get-tuple-element.49), channel_id=1, source_target_pairs={{0,6},{1,7},{2,4},{3,5},{4,2},{5,3},{6,0},{7,1},{8,14},{9,15},{10,... | collective-permute-start | bytes 491528 | tf_op jit(solution)/shard_map/ppermute | solution.py:397
  19.0 1.2 %collective-permute-start.7 = (f32[8,128]{1,0:T(8,128)S(1)}, f32[8,128]{1,0:T(8,128)S(1)}, u32[]{:S(2)}, u32[]{:S(2)}) collective-permute-start(f32[8,128]{1,0:T(8,128)S(1)} %coefs.3.refs_2_), channel_id=1, source_target_pairs={{0,1},{1,0},{2,3},{3,2},{4,5},{5,4},{6,7},{7,6},{8,9},{9,8},{10,11... | collective-permute-start | bytes 12296 | tf_op jit(solution)/shard_map/ppermute | solution.py:397
  21.1 8.8 %collective-permute-start.10 = (f32[328,128]{1,0:T(8,128)S(1)}, f32[328,128]{1,0:T(8,128)S(1)}, u32[]{:S(2)}, u32[]{:S(2)}) collective-permute-start(f32[328,128]{1,0:T(8,128)S(1)} %get-tuple-element.58), channel_id=1, source_target_pairs={{0,6},{1,7},{2,4},{3,5},{4,2},{5,3},{6,0},{7,1},{8,14},{9,15},{10,... | collective-permute-start | bytes 503816 | tf_op jit(solution)/shard_map/ppermute | solution.py:397
  24.0 8.5 %collective-permute-start.8 = (f32[328,128]{1,0:T(8,128)S(1)}, f32[328,128]{1,0:T(8,128)S(1)}, u32[]{:S(2)}, u32[]{:S(2)}) collective-permute-start(f32[328,128]{1,0:T(8,128)S(1)} %get-tuple-element.56), channel_id=1, source_target_pairs={{0,2},{1,3},{2,0},{3,1},{4,6},{5,7},{6,4},{7,5},{8,10},{9,11},{10,... | collective-permute-start | bytes 503816 | tf_op jit(solution)/shard_map/ppermute | solution.py:397
  24.6 8.0 %collective-permute-start.9 = (f32[328,128]{1,0:T(8,128)S(1)}, f32[328,128]{1,0:T(8,128)S(1)}, u32[]{:S(2)}, u32[]{:S(2)}) collective-permute-start(f32[328,128]{1,0:T(8,128)S(1)} %get-tuple-element.57), channel_id=1, source_target_pairs={{0,4},{1,5},{2,6},{3,7},{4,0},{5,1},{6,2},{7,3},{8,12},{9,13},{10,... | collective-permute-start | bytes 503816 | tf_op jit(solution)/shard_map/ppermute | solution.py:397
  25.4 7.9 %collective-permute-start.5 = (f32[120,128]{1,0:T(8,128)S(1)}, f32[120,128]{1,0:T(8,128)S(1)}, u32[]{:S(2)}, u32[]{:S(2)}) collective-permute-start(f32[120,128]{1,0:T(8,128)S(1)} %get-tuple-element.52), channel_id=1, source_target_pairs={{0,16},{1,17},{2,18},{3,19},{4,20},{5,21},{6,22},{7,23},{8,24},{9,... | collective-permute-start | bytes 184328 | tf_op jit(solution)/shard_map/ppermute | solution.py:397
  28.5 6.0 %collective-permute-start.6 = (f32[120,128]{1,0:T(8,128)S(1)}, f32[120,128]{1,0:T(8,128)S(1)}, u32[]{:S(2)}, u32[]{:S(2)}) collective-permute-start(f32[120,128]{1,0:T(8,128)S(1)} %get-tuple-element.53), channel_id=1, source_target_pairs={{0,24},{1,25},{2,26},{3,27},{4,28},{5,29},{6,30},{7,31},{8,16},{9,... | collective-permute-start | bytes 184328 | tf_op jit(solution)/shard_map/ppermute | solution.py:397
  34.5 9.3 %collective-permute-start.11 = (f32[128,128]{1,0:T(8,128)S(1)}, f32[128,128]{1,0:T(8,128)S(1)}, u32[]{:S(2)}, u32[]{:S(2)}) collective-permute-start(f32[128,128]{1,0:T(8,128)S(1)} %get-tuple-element.66), channel_id=1, source_target_pairs={{0,8},{1,9},{2,10},{3,11},{4,12},{5,13},{6,14},{7,15},{8,0},{9,1},... | collective-permute-start | bytes 196616 | tf_op jit(solution)/shard_map/ppermute | solution.py:397
  35.0 8.9 %collective-permute-start.12 = (f32[128,128]{1,0:T(8,128)S(1)}, f32[128,128]{1,0:T(8,128)S(1)}, u32[]{:S(2)}, u32[]{:S(2)}) collective-permute-start(f32[128,128]{1,0:T(8,128)S(1)} %get-tuple-element.67), channel_id=1, source_target_pairs={{0,16},{1,17},{2,18},{3,19},{4,20},{5,21},{6,22},{7,23},{8,24},{9,... | collective-permute-start | bytes 196616 | tf_op jit(solution)/shard_map/ppermute | solution.py:397
  37.5 6.3 %collective-permute-start.13 = (f32[128,128]{1,0:T(8,128)S(1)}, f32[128,128]{1,0:T(8,128)S(1)}, u32[]{:S(2)}, u32[]{:S(2)}) collective-permute-start(f32[128,128]{1,0:T(8,128)S(1)} %get-tuple-element.68), channel_id=1, source_target_pairs={{0,24},{1,25},{2,26},{3,27},{4,28},{5,29},{6,30},{7,31},{8,16},{9,... | collective-permute-start | bytes 196616 | tf_op jit(solution)/shard_map/ppermute | solution.py:397
  38.9 4.9 %collective-permute-start.4 = (f32[120,128]{1,0:T(8,128)S(1)}, f32[120,128]{1,0:T(8,128)S(1)}, u32[]{:S(2)}, u32[]{:S(2)}) collective-permute-start(f32[120,128]{1,0:T(8,128)S(1)} %get-tuple-element.51), channel_id=1, source_target_pairs={{0,8},{1,9},{2,10},{3,11},{4,12},{5,13},{6,14},{7,15},{8,0},{9,1},... | collective-permute-start | bytes 184328 | tf_op jit(solution)/shard_map/ppermute | solution.py:397

commit v6 on v5

--- a/solution.py
+++ b/solution.py
@@ -11,12 +11,11 @@
 HIGHEST = lax.Precision.HIGHEST
 LANES = 128
 COEF_ROWS = 8
-GROUP = 16
+GROUP = 8
 AHEAD = 3
 WIDE = 256
 COEF_STEP = 4096
 EARLY = 3
-CHUNKS = 2
 
 
 class Plan:
@@ -405,8 +404,8 @@
         lax.axis_size(AXIS), tile_owner.shape[0], entries, frames, block_width, tile_width
     )
     stages = len(plan.widths)
-    rows = frames // CHUNKS
-    spans = [(i * rows, rows) for i in range(CHUNKS)]
+    cut = frames * 3 // 5 // 8 * 8
+    spans = [(0, cut), (cut, frames - cut)]
     steps = voxels // COEF_STEP
     keep, send = sample(plan, series, sample_weights, block_ids, tile_ids, tile_owner)
     keep, send, probes = lax.optimization_barrier((keep, send, probes))
@@ -421,8 +420,9 @@
     for stage in range(1, stages):
         for i, span in enumerate(spans):
             if stage + 1 == stages and i > 0:
-                far, chunks[i] = lax.optimization_barrier((chunks[i - 1][2:], chunks[i]))
+                far, near = lax.optimization_barrier((chunks[i - 1][2:], chunks[i][1]))
                 chunks[i - 1] = chunks[i - 1][:2] + far
+                chunks[i] = [chunks[i][0], near] + list(chunks[i][2:])
             chunks[i] = exchange(plan, stage, chunks[i])
             if stage + 1 < stages:
                 riding = i + 1 == len(spans)

time: 46.1 us -> 42.7 us (0.926)
  waiting for transfers between devices: 10 us -> 6.25 us
  starting transfers between devices: 17.1 us -> 17.7 us
    ppermute x14, waiting for transfers between devices: 10 us -> 6.25 us  [exchange(): received.append(lax.ppermute(blocks[digit], AXIS, pairs))]
    ppermute x14, starting transfers between devices: 17.1 us -> 17.7 us  [exchange(): received.append(lax.ppermute(blocks[digit], AXIS, pairs))]
  transfers between devices with their start and end apart: 14 -> 14, of which waited for: 4 -> 4; matrix products, arithmetic and copies ran while one was open for 0% -> 0% of each run, Pallas kernels for 23% -> 25%
where the time goes in v6:
time: 42.7 us; the launch traced here: 42.5 us
  Pallas kernels  18.5 us (43%)
  starting transfers between devices  17.7 us (41%)
  waiting for transfers between devices  6.25 us (15%)
    ppermute x14, starting transfers between devices, exchange(): received.append(lax.ppermute(blocks[digit], AXIS, pairs))  17.7 us
    pallas_call x2, Pallas kernels, local_coefs(): pl.pallas_call(functools.partial(coef_kernel, first, steps), name='coefs'...  8.47 us
    ppermute x14, waiting for transfers between devices, exchange(): received.append(lax.ppermute(blocks[digit], AXIS, pairs))  6.25 us
    pallas_call x1, Pallas kernels, sample(): pl.pallas_call(functools.partial(sample_kernel, plan), name='sample', in_...  4.82 us
    pallas_call x4, Pallas kernels, merge(): pl.pallas_call(functools.partial(merge_kernel, plan, stage, span, len(coe...  3.08 us
    pallas_call x1, Pallas kernels, finish(): pl.pallas_call(functools.partial(finish_kernel, plan, comps, spans), name...  2.14 us
  transfers between devices with their start and end apart: 14, of which 4 were waited for; matrix products, arithmetic and copies ran while one was open for 0% of the time, Pallas kernels for 25%

profile of v6, /device:TPU:0, one launch (start us, length us, event | category | flops | bytes accessed | tf_op | source)
XLA Modules:
  0.0 42.5 jit_solution(7466130424820067451)
XLA Ops:
  0.0 4.8 %sample.1 = (f32[2640,128]{1,0:T(8,128)S(1)}, f32[2640,128]{1,0:T(8,128)S(1)}) custom-call(s32[48]{0:T(128)} %block_ids.1, s32[48]{0:T(128)} %tile_ids.1, s32[128]{0:T(128)} %tile_owner.11, f32[80,32768]{1,0:T(8,128)} %series.5, bf16[48,256,128]{2,1,0:T(8,128)(2,1)} %weights.1), custom_call_target="tpu_custom_call" | custom-call | tf_op jit(solution)/shard_map/sample/pallas_call | solution.py:144
  4.8 0.5 %collective-permute-start = (f32[2640,128]{1,0:T(8,128)S(1)}, f32[2640,128]{1,0:T(8,128)S(1)}, u32[]{:S(2)}, u32[]{:S(2)}) collective-permute-start(f32[2640,128]{1,0:T(8,128)S(1)} %get-tuple-element.37), channel_id=1, source_target_pairs={{0,1},{1,0},{2,3},{3,2},{4,5},{5,4},{6,7},{7,6},{8,9},{9,8},{10,11... | collective-permute-start | bytes 4055048 | tf_op jit(solution)/shard_map/ppermute | solution.py:396
  5.4 3.6 %coefs.2.before = f32[8,128]{1,0:T(8,128)S(1)} custom-call(f32[80,32768]{1,0:T(8,128)} %series.5, s32[1,32768]{1,0:T(1,128)} %bitcast.4, f32[5,80]{1,0:T(8,128)S(1)} %bitcast.2, f32[8,128]{1,0:T(8,128)S(1)} %broadcast_in_dim.3.before), custom_call_target="tpu_custom_call" | custom-call | flops 314572800 | bytes 3932160 | tf_op jit(solution)/shard_map/coefs/pallas_call | solution.py:227
  9.0 0.0 collective-permute-done.refs_1_
  9.0 0.8 %merge.4 = (f32[384,128]{1,0:T(8,128)S(1)}, f32[384,128]{1,0:T(8,128)S(1)}, f32[384,128]{1,0:T(8,128)S(1)}, f32[384,128]{1,0:T(8,128)S(1)}) custom-call(s32[128]{0:T(128)S(1)} %copy-done, f32[2640,128]{1,0:T(8,128)S(1)} %get-tuple-element.36.refs_0_, f32[2640,128]{1,0:T(8,128)S(1)} %collective-permute-done.refs_1_), custom_call_target="tpu_custom_call" | custom-call | tf_op jit(solution)/shard_map/merge/pallas_call | solution.py:328
  9.8 2.6 %collective-permute-start.1 = (f32[384,128]{1,0:T(8,128)S(1)}, f32[384,128]{1,0:T(8,128)S(1)}, u32[]{:S(2)}, u32[]{:S(2)}) collective-permute-start(f32[384,128]{1,0:T(8,128)S(1)} %get-tuple-element.44), channel_id=1, source_target_pairs={{0,2},{1,3},{2,0},{3,1},{4,6},{5,7},{6,4},{7,5},{8,10},{9,11},{10,... | collective-permute-start | bytes 589832 | tf_op jit(solution)/shard_map/ppermute | solution.py:396
  12.4 1.5 %collective-permute-start.2 = (f32[384,128]{1,0:T(8,128)S(1)}, f32[384,128]{1,0:T(8,128)S(1)}, u32[]{:S(2)}, u32[]{:S(2)}) collective-permute-start(f32[384,128]{1,0:T(8,128)S(1)} %get-tuple-element.45), channel_id=1, source_target_pairs={{0,4},{1,5},{2,6},{3,7},{4,0},{5,1},{6,2},{7,3},{8,12},{9,13},{10,... | collective-permute-start | bytes 589832 | tf_op jit(solution)/shard_map/ppermute | solution.py:396
  13.9 0.0 collective-permute-start.3
  13.9 4.9 %coefs.3.refs_2_ = f32[8,128]{1,0:T(8,128)S(1)} custom-call(f32[80,32768]{1,0:T(8,128)} %series.5, s32[1,32768]{1,0:T(1,128)} %bitcast.5, f32[5,80]{1,0:T(8,128)S(1)} %bitcast.3, f32[8,128]{1,0:T(8,128)S(1)} %coefs.2.before), custom_call_target="tpu_custom_call" | custom-call | flops 524288000 | bytes 6553600 | tf_op jit(solution)/shard_map/coefs/pallas_call | solution.py:227
  18.8 0.1 collective-permute-start.7
  18.9 1.2 %collective-permute-done.7.refs_3_ = f32[8,128]{1,0:T(8,128)S(1)} collective-permute-done((f32[8,128]{1,0:T(8,128)S(1)}, f32[8,128]{1,0:T(8,128)S(1)}, u32[]{:S(2)}, u32[]{:S(2)}) %collective-permute-start.7) | collective-permute-done | bytes 4128 | tf_op jit(solution)/shard_map/ppermute | solution.py:396
  20.0 0.8 %merge.6 = (f32[264,128]{1,0:T(8,128)S(1)}, f32[264,128]{1,0:T(8,128)S(1)}, f32[264,128]{1,0:T(8,128)S(1)}, f32[264,128]{1,0:T(8,128)S(1)}) custom-call(s32[128]{0:T(128)S(1)} %copy-done, f32[2640,128]{1,0:T(8,128)S(1)} %get-tuple-element.36.refs_0_, f32[2640,128]{1,0:T(8,128)S(1)} %collective-permute-done.refs_1_, f32[8,128]{1,0:T(8,128)S(1)} %coefs.3.refs_2_, ...), custom_call_target="tpu_custom_call" | custom-call | tf_op jit(solution)/shard_map/merge/pallas_call | solution.py:328
  20.8 3.0 %collective-permute-start.10 = (f32[264,128]{1,0:T(8,128)S(1)}, f32[264,128]{1,0:T(8,128)S(1)}, u32[]{:S(2)}, u32[]{:S(2)}) collective-permute-start(f32[264,128]{1,0:T(8,128)S(1)} %get-tuple-element.55), channel_id=1, source_target_pairs={{0,6},{1,7},{2,4},{3,5},{4,2},{5,3},{6,0},{7,1},{8,14},{9,15},{10,... | collective-permute-start | bytes 405512 | tf_op jit(solution)/shard_map/ppermute | solution.py:396
  23.8 0.5 %collective-permute-start.8 = (f32[264,128]{1,0:T(8,128)S(1)}, f32[264,128]{1,0:T(8,128)S(1)}, u32[]{:S(2)}, u32[]{:S(2)}) collective-permute-start(f32[264,128]{1,0:T(8,128)S(1)} %get-tuple-element.53), channel_id=1, source_target_pairs={{0,2},{1,3},{2,0},{3,1},{4,6},{5,7},{6,4},{7,5},{8,10},{9,11},{10,... | collective-permute-start | bytes 405512 | tf_op jit(solution)/shard_map/ppermute | solution.py:396
  24.4 0.0 collective-permute-done.1.refs_1_
  24.4 0.1 collective-permute-start.9
  24.5 0.7 %merge.5 = (f32[144,128]{1,0:T(8,128)S(1)}, f32[144,128]{1,0:T(8,128)S(1)}, f32[144,128]{1,0:T(8,128)S(1)}, f32[144,128]{1,0:T(8,128)S(1)}) custom-call(s32[128]{0:T(128)S(1)} %copy-done, f32[384,128]{1,0:T(8,128)S(1)} %get-tuple-element.43.refs_0_, f32[384,128]{1,0:T(8,128)S(1)} %collective-permute-done.1.refs_1_, ...), custom_call_target="tpu_custom_call" | custom-call | tf_op jit(solution)/shard_map/merge/pallas_call | solution.py:328
  25.2 3.1 %collective-permute-start.5 = (f32[144,128]{1,0:T(8,128)S(1)}, f32[144,128]{1,0:T(8,128)S(1)}, u32[]{:S(2)}, u32[]{:S(2)}) collective-permute-start(f32[144,128]{1,0:T(8,128)S(1)} %get-tuple-element.49), channel_id=1, source_target_pairs={{0,16},{1,17},{2,18},{3,19},{4,20},{5,21},{6,22},{7,23},{8,24},{9,... | collective-permute-start | bytes 221192 | tf_op jit(solution)/shard_map/ppermute | solution.py:396
  28.3 1.3 %collective-permute-start.6 = (f32[144,128]{1,0:T(8,128)S(1)}, f32[144,128]{1,0:T(8,128)S(1)}, u32[]{:S(2)}, u32[]{:S(2)}) collective-permute-start(f32[144,128]{1,0:T(8,128)S(1)} %get-tuple-element.50), channel_id=1, source_target_pairs={{0,24},{1,25},{2,26},{3,27},{4,28},{5,29},{6,30},{7,31},{8,16},{9,... | collective-permute-start | bytes 221192 | tf_op jit(solution)/shard_map/ppermute | solution.py:396
  29.6 0.0 collective-permute-done.10.refs_3_
  29.6 0.7 %collective-permute-start.4 = (f32[144,128]{1,0:T(8,128)S(1)}, f32[144,128]{1,0:T(8,128)S(1)}, u32[]{:S(2)}, u32[]{:S(2)}) collective-permute-start(f32[144,128]{1,0:T(8,128)S(1)} %get-tuple-element.48), channel_id=1, source_target_pairs={{0,8},{1,9},{2,10},{3,11},{4,12},{5,13},{6,14},{7,15},{8,0},{9,1},... | collective-permute-start | bytes 221192 | tf_op jit(solution)/shard_map/ppermute | solution.py:396
  30.3 0.6 %collective-permute-done.8.refs_1_ = f32[264,128]{1,0:T(8,128)S(1)} collective-permute-done((f32[264,128]{1,0:T(8,128)S(1)}, f32[264,128]{1,0:T(8,128)S(1)}, u32[]{:S(2)}, u32[]{:S(2)}) %collective-permute-start.8) | collective-permute-done | bytes 135200 | tf_op jit(solution)/shard_map/ppermute | solution.py:396
  30.9 0.7 %merge.7 = (f32[104,128]{1,0:T(8,128)S(1)}, f32[104,128]{1,0:T(8,128)S(1)}, f32[104,128]{1,0:T(8,128)S(1)}, f32[104,128]{1,0:T(8,128)S(1)}) custom-call(s32[128]{0:T(128)S(1)} %copy-done, f32[264,128]{1,0:T(8,128)S(1)} %get-tuple-element.52.refs_0_, f32[264,128]{1,0:T(8,128)S(1)} %collective-permute-done.8.refs_1_, ...), custom_call_target="tpu_custom_call" | custom-call | tf_op jit(solution)/shard_map/merge/pallas_call | solution.py:328
  31.7 2.6 %collective-permute-start.12 = (f32[104,128]{1,0:T(8,128)S(1)}, f32[104,128]{1,0:T(8,128)S(1)}, u32[]{:S(2)}, u32[]{:S(2)}) collective-permute-start(f32[104,128]{1,0:T(8,128)S(1)} %get-tuple-element.61), channel_id=1, source_target_pairs={{0,16},{1,17},{2,18},{3,19},{4,20},{5,21},{6,22},{7,23},{8,24},{9,... | collective-permute-start | bytes 159752 | tf_op jit(solution)/shard_map/ppermute | solution.py:396
  34.3 1.3 %collective-permute-start.13 = (f32[104,128]{1,0:T(8,128)S(1)}, f32[104,128]{1,0:T(8,128)S(1)}, u32[]{:S(2)}, u32[]{:S(2)}) collective-permute-start(f32[104,128]{1,0:T(8,128)S(1)} %get-tuple-element.62), channel_id=1, source_target_pairs={{0,24},{1,25},{2,26},{3,27},{4,28},{5,29},{6,30},{7,31},{8,16},{9,... | collective-permute-start | bytes 159752 | tf_op jit(solution)/shard_map/ppermute | solution.py:396
  35.6 0.0 collective-permute-done.6.refs_3_
  35.6 0.3 collective-permute-start.11
  35.9 1.0 %collective-permute-done.12.refs_6_ = f32[104,128]{1,0:T(8,128)S(1)} collective-permute-done((f32[104,128]{1,0:T(8,128)S(1)}, f32[104,128]{1,0:T(8,128)S(1)}, u32[]{:S(2)}, u32[]{:S(2)}) %collective-permute-start.12) | collective-permute-done | bytes 53280 | tf_op jit(solution)/shard_map/ppermute | solution.py:396
  37.0 3.4 %collective-permute-done.13.refs_7_ = f32[104,128]{1,0:T(8,128)S(1)} collective-permute-done((f32[104,128]{1,0:T(8,128)S(1)}, f32[104,128]{1,0:T(8,128)S(1)}, u32[]{:S(2)}, u32[]{:S(2)}) %collective-permute-start.13) | collective-permute-done | bytes 53280 | tf_op jit(solution)/shard_map/ppermute | solution.py:396
  40.4 0.0 collective-permute-done.4.refs_1_
  40.4 0.0 collective-permute-done.11.refs_5_
  40.4 2.1 %finish.1 = f32[4,80,128]{2,1,0:T(8,128)} custom-call(s32[128]{0:T(128)S(1)} %copy-done, f32[144,128]{1,0:T(8,128)S(1)} %get-tuple-element.47.refs_0_, f32[144,128]{1,0:T(8,128)S(1)} %collective-permute-done.4.refs_1_, f32[144,128]{1,0:T(8,128)S(1)} %collective-permute-done.5.refs_2_, f32[144,128]{1,0:T(8,128)S(1)} %collective-permute-done.6.refs_3_, ...), custom_call_target="tpu_custom_call" | custom-call | tf_op jit(solution)/shard_map/finish/pallas_call | solution.py:381
  (9 shorter events, 0.0 us)
Async XLA Ops:
  0.0 5.3 %copy-start.1 = (f32[80,5]{0,1:T(8,128)S(1)}, f32[80,5]{0,1:T(8,128)}, u32[]{:S(2)}) copy-start(f32[80,5]{0,1:T(8,128)} %param.9) | copy-start | bytes 4804
  4.8 4.1 %collective-permute-start = (f32[2640,128]{1,0:T(8,128)S(1)}, f32[2640,128]{1,0:T(8,128)S(1)}, u32[]{:S(2)}, u32[]{:S(2)}) collective-permute-start(f32[2640,128]{1,0:T(8,128)S(1)} %get-tuple-element.37), channel_id=1, source_target_pairs={{0,1},{1,0},{2,3},{3,2},{4,5},{5,4},{6,7},{7,6},{8,9},{9,8},{10,11... | collective-permute-start | bytes 4055048 | tf_op jit(solution)/shard_map/ppermute | solution.py:396
  5.3 3.6 %copy-start = (s32[128]{0:T(128)S(1)}, s32[128]{0:T(128)}, u32[]{:S(2)}) copy-start(s32[128]{0:T(128)} %tile_owner.11) | copy-start | bytes 1540
  9.8 14.6 %collective-permute-start.1 = (f32[384,128]{1,0:T(8,128)S(1)}, f32[384,128]{1,0:T(8,128)S(1)}, u32[]{:S(2)}, u32[]{:S(2)}) collective-permute-start(f32[384,128]{1,0:T(8,128)S(1)} %get-tuple-element.44), channel_id=1, source_target_pairs={{0,2},{1,3},{2,0},{3,1},{4,6},{5,7},{6,4},{7,5},{8,10},{9,11},{10,... | collective-permute-start | bytes 589832 | tf_op jit(solution)/shard_map/ppermute | solution.py:396
  12.4 12.1 %collective-permute-start.2 = (f32[384,128]{1,0:T(8,128)S(1)}, f32[384,128]{1,0:T(8,128)S(1)}, u32[]{:S(2)}, u32[]{:S(2)}) collective-permute-start(f32[384,128]{1,0:T(8,128)S(1)} %get-tuple-element.45), channel_id=1, source_target_pairs={{0,4},{1,5},{2,6},{3,7},{4,0},{5,1},{6,2},{7,3},{8,12},{9,13},{10,... | collective-permute-start | bytes 589832 | tf_op jit(solution)/shard_map/ppermute | solution.py:396
  13.9 10.6 %collective-permute-start.3 = (f32[384,128]{1,0:T(8,128)S(1)}, f32[384,128]{1,0:T(8,128)S(1)}, u32[]{:S(2)}, u32[]{:S(2)}) collective-permute-start(f32[384,128]{1,0:T(8,128)S(1)} %get-tuple-element.46), channel_id=1, source_target_pairs={{0,6},{1,7},{2,4},{3,5},{4,2},{5,3},{6,0},{7,1},{8,14},{9,15},{10,... | collective-permute-start | bytes 589832 | tf_op jit(solution)/shard_map/ppermute | solution.py:396
  18.8 1.2 %collective-permute-start.7 = (f32[8,128]{1,0:T(8,128)S(1)}, f32[8,128]{1,0:T(8,128)S(1)}, u32[]{:S(2)}, u32[]{:S(2)}) collective-permute-start(f32[8,128]{1,0:T(8,128)S(1)} %coefs.3.refs_2_), channel_id=1, source_target_pairs={{0,1},{1,0},{2,3},{3,2},{4,5},{5,4},{6,7},{7,6},{8,9},{9,8},{10,11... | collective-permute-start | bytes 12296 | tf_op jit(solution)/shard_map/ppermute | solution.py:396
  20.8 8.8 %collective-permute-start.10 = (f32[264,128]{1,0:T(8,128)S(1)}, f32[264,128]{1,0:T(8,128)S(1)}, u32[]{:S(2)}, u32[]{:S(2)}) collective-permute-start(f32[264,128]{1,0:T(8,128)S(1)} %get-tuple-element.55), channel_id=1, source_target_pairs={{0,6},{1,7},{2,4},{3,5},{4,2},{5,3},{6,0},{7,1},{8,14},{9,15},{10,... | collective-permute-start | bytes 405512 | tf_op jit(solution)/shard_map/ppermute | solution.py:396
  23.8 7.1 %collective-permute-start.8 = (f32[264,128]{1,0:T(8,128)S(1)}, f32[264,128]{1,0:T(8,128)S(1)}, u32[]{:S(2)}, u32[]{:S(2)}) collective-permute-start(f32[264,128]{1,0:T(8,128)S(1)} %get-tuple-element.53), channel_id=1, source_target_pairs={{0,2},{1,3},{2,0},{3,1},{4,6},{5,7},{6,4},{7,5},{8,10},{9,11},{10,... | collective-permute-start | bytes 405512 | tf_op jit(solution)/shard_map/ppermute | solution.py:396
  24.4 6.6 %collective-permute-start.9 = (f32[264,128]{1,0:T(8,128)S(1)}, f32[264,128]{1,0:T(8,128)S(1)}, u32[]{:S(2)}, u32[]{:S(2)}) collective-permute-start(f32[264,128]{1,0:T(8,128)S(1)} %get-tuple-element.54), channel_id=1, source_target_pairs={{0,4},{1,5},{2,6},{3,7},{4,0},{5,1},{6,2},{7,3},{8,12},{9,13},{10,... | collective-permute-start | bytes 405512 | tf_op jit(solution)/shard_map/ppermute | solution.py:396
  25.2 10.4 %collective-permute-start.5 = (f32[144,128]{1,0:T(8,128)S(1)}, f32[144,128]{1,0:T(8,128)S(1)}, u32[]{:S(2)}, u32[]{:S(2)}) collective-permute-start(f32[144,128]{1,0:T(8,128)S(1)} %get-tuple-element.49), channel_id=1, source_target_pairs={{0,16},{1,17},{2,18},{3,19},{4,20},{5,21},{6,22},{7,23},{8,24},{9,... | collective-permute-start | bytes 221192 | tf_op jit(solution)/shard_map/ppermute | solution.py:396
  28.3 7.4 %collective-permute-start.6 = (f32[144,128]{1,0:T(8,128)S(1)}, f32[144,128]{1,0:T(8,128)S(1)}, u32[]{:S(2)}, u32[]{:S(2)}) collective-permute-start(f32[144,128]{1,0:T(8,128)S(1)} %get-tuple-element.50), channel_id=1, source_target_pairs={{0,24},{1,25},{2,26},{3,27},{4,28},{5,29},{6,30},{7,31},{8,16},{9,... | collective-permute-start | bytes 221192 | tf_op jit(solution)/shard_map/ppermute | solution.py:396
  29.6 10.8 %collective-permute-start.4 = (f32[144,128]{1,0:T(8,128)S(1)}, f32[144,128]{1,0:T(8,128)S(1)}, u32[]{:S(2)}, u32[]{:S(2)}) collective-permute-start(f32[144,128]{1,0:T(8,128)S(1)} %get-tuple-element.48), channel_id=1, source_target_pairs={{0,8},{1,9},{2,10},{3,11},{4,12},{5,13},{6,14},{7,15},{8,0},{9,1},... | collective-permute-start | bytes 221192 | tf_op jit(solution)/shard_map/ppermute | solution.py:396
  31.7 5.3 %collective-permute-start.12 = (f32[104,128]{1,0:T(8,128)S(1)}, f32[104,128]{1,0:T(8,128)S(1)}, u32[]{:S(2)}, u32[]{:S(2)}) collective-permute-start(f32[104,128]{1,0:T(8,128)S(1)} %get-tuple-element.61), channel_id=1, source_target_pairs={{0,16},{1,17},{2,18},{3,19},{4,20},{5,21},{6,22},{7,23},{8,24},{9,... | collective-permute-start | bytes 159752 | tf_op jit(solution)/shard_map/ppermute | solution.py:396
  34.3 6.1 %collective-permute-start.13 = (f32[104,128]{1,0:T(8,128)S(1)}, f32[104,128]{1,0:T(8,128)S(1)}, u32[]{:S(2)}, u32[]{:S(2)}) collective-permute-start(f32[104,128]{1,0:T(8,128)S(1)} %get-tuple-element.62), channel_id=1, source_target_pairs={{0,24},{1,25},{2,26},{3,27},{4,28},{5,29},{6,30},{7,31},{8,16},{9,... | collective-permute-start | bytes 159752 | tf_op jit(solution)/shard_map/ppermute | solution.py:396
  35.6 4.7 %collective-permute-start.11 = (f32[104,128]{1,0:T(8,128)S(1)}, f32[104,128]{1,0:T(8,128)S(1)}, u32[]{:S(2)}, u32[]{:S(2)}) collective-permute-start(f32[104,128]{1,0:T(8,128)S(1)} %get-tuple-element.60), channel_id=1, source_target_pairs={{0,8},{1,9},{2,10},{3,11},{4,12},{5,13},{6,14},{7,15},{8,0},{9,1},... | collective-permute-start | bytes 159752 | tf_op jit(solution)/shard_map/ppermute | solution.py:396

commit v7 on v6

--- a/solution.py
+++ b/solution.py
@@ -15,7 +15,7 @@
 AHEAD = 3
 WIDE = 256
 COEF_STEP = 4096
-EARLY = 3
+EARLY = 4
 
 
 class Plan:
@@ -44,6 +44,12 @@
     def tiles_in(self, stage):
         return self.owners[stage] * self.slots[stage]
 
+    def slot(self, stage, tile, offset):
+        return (tile >> self.log) & 1 if self.by_parity(stage) else offset >> self.log
+
+    def by_parity(self, stage):
+        return self.slots[stage] == 2 and self.owned % 2 == 0
+
     def position(self, rel, stage):
         place = 0
         for i in range(stage, len(self.widths)):
@@ -122,7 +128,7 @@
             total = both[0:frames] + both[frames:]
             rel = tile_owner[tile & (plan.devices - 1)] ^ device
             offset = (tile - device * plan.owned) & (plan.tiles - 1)
-            slot = plan.position(rel, 1) * plan.slots[0] + (offset >> plan.log)
+            slot = plan.position(rel, 1) * plan.slots[0] + plan.slot(0, tile, offset)
             mine = (rel & 1) == 0
             used = tile >= 0
             to_keep = jnp.where(used & mine, slot, spare)
@@ -159,93 +165,108 @@
     )(*[in_hbm(x) for x in (block_ids, tile_ids, tile_owner, series, weights)])
 
 
-def coef_kernel(
-    first, steps, series, mask, probes, before, coefs,
-    held, marks, halves, masked, gram, sems, mark_sem,
-):
-    frames = series.shape[0]
+def add_gram(values, marks, halves, masked, gram):
+    frames, columns = values.shape
+    for at in range(0, columns, WIDE):
+        place = pl.ds(at, WIDE)
+        high, low = split(demean(values[:, place]))
+        halves[0:frames, place] = high
+        halves[frames:, place] = low
+        masked[:, place] = high * marks[:, place].astype(jnp.float32).astype(jnp.bfloat16)
+    gram[...] += lax.dot_general(
+        halves[...],
+        masked[...],
+        (((1,), (1,)), ((), ())),
+        preferred_element_type=jnp.float32,
+    )
+
+
+def gram_kernel(first, steps, more, series, mask, *refs):
     columns = COEF_STEP
+    if more:
+        gram, following, held, marks, halves, masked, sems, mark_sem = refs
+        gram[...] = jnp.zeros_like(gram)
+    else:
+        probes, before, following, coefs = refs[:4]
+        held, marks, halves, masked, sems, mark_sem, gram = refs[4:]
+        gram[...] = before[...]
+        first, steps = first - 1, steps + 1
 
     def fetch(step):
-        span = pl.ds(pl.multiple_of(step * columns, columns), columns)
-        there = pl.ds(pl.multiple_of((first + step) * columns, columns), columns)
-        return pltpu.make_async_copy(series.at[:, there], held.at[:, span], sems.at[step])
-
+        span = pl.ds((first + step) * columns, columns)
+        target = following if more and step == steps else held.at[step - (not more)]
+        return pltpu.make_async_copy(series.at[:, span], target, sems.at[step])
+
+    start = 0 if more else 1
+    end = steps + 1 if more else steps
     mark_copy = pltpu.make_async_copy(
         mask.at[:, pl.ds(first * columns, steps * columns)], marks, mark_sem
     )
     mark_copy.start()
-    for step in range(min(AHEAD, steps)):
+    for step in range(start, min(start + AHEAD, end)):
         fetch(step).start()
-    gram[...] = jnp.zeros_like(gram)
     mark_copy.wait()
-
-    def chunk(step, carry):
-        fetch(step).wait()
-
-        @pl.when(step + AHEAD < steps)
-        def _():
-            fetch(step + AHEAD).start()
-
-        start = step * columns
-        for at in range(0, columns, WIDE):
-            span = pl.ds(pl.multiple_of(start + at, WIDE), WIDE)
-            place = pl.ds(at, WIDE)
-            high, low = split(demean(held[:, span]))
-            halves[0:frames, place] = high
-            halves[frames:, place] = low
-            masked[:, place] = high * marks[:, span].astype(jnp.float32).astype(jnp.bfloat16)
-        gram[...] += lax.dot_general(
-            halves[...],
-            masked[...],
-            (((1,), (1,)), ((), ())),
-            preferred_element_type=jnp.float32,
-        )
-        return carry
-
-    lax.fori_loop(0, steps, chunk, 0)
+    for step in range(steps):
+        values = following
+        if step >= start:
+            fetch(step).wait()
+            values = held.at[step - start]
+            if step + AHEAD < end:
+                fetch(step + AHEAD).start()
+        span = pl.ds(step * columns, columns)
+        add_gram(values, marks.at[:, span], halves, masked, gram)
+    if more:
+        for step in range(max(steps, start), end):
+            fetch(step).wait()
+        return
+    frames = series.shape[0]
     low = gram[frames:, :]
-    start = probes[...]
+    rows = probes[...]
     made = jnp.dot(
-        start, gram[0:frames, :] + low, precision=HIGHEST, preferred_element_type=jnp.float32
+        rows, gram[0:frames, :] + low, precision=HIGHEST, preferred_element_type=jnp.float32
     ) + lax.dot_general(
-        start,
+        rows,
         low,
         (((1,), (1,)), ((), ())),
         precision=HIGHEST,
         preferred_element_type=jnp.float32,
     )
-    coefs[...] = before[...]
-    coefs[0 : start.shape[0], 0:frames] += made
-
-
-def local_coefs(series, noise_mask, probes, before, first, steps):
+    coefs[...] = jnp.zeros_like(coefs)
+    coefs[0 : rows.shape[0], 0:frames] = made
+
+
+def local_coefs(series, noise_mask, first, steps, probes=None, before=()):
     frames, voxels = series.shape
-    held = steps * COEF_STEP
+    more = probes is None
     vmem = pl.BlockSpec(memory_space=pltpu.VMEM)
     hbm = pl.BlockSpec(memory_space=pl.ANY)
+    gram = jax.ShapeDtypeStruct((2 * frames, frames), jnp.float32)
+    step = jax.ShapeDtypeStruct((frames, COEF_STEP), series.dtype)
+    coefs = jax.ShapeDtypeStruct((COEF_ROWS, LANES), jnp.float32)
+    arrays = [] if more else [probes.T, *before]
+    total = steps if more else steps + 1
     return pl.pallas_call(
-        functools.partial(coef_kernel, first, steps),
-        name="coefs",
-        in_specs=[hbm, hbm, vmem, vmem],
-        out_specs=vmem,
-        out_shape=jax.ShapeDtypeStruct(before.shape, before.dtype),
+        functools.partial(gram_kernel, first, steps, more),
+        name="gram" if more else "coefs",
+        in_specs=[hbm, hbm] + [vmem] * len(arrays),
+        out_specs=[vmem, vmem] if more else vmem,
+        out_shape=[gram, step] if more else coefs,
         scratch_shapes=[
-            pltpu.VMEM((frames, held), series.dtype),
-            pltpu.VMEM((1, held), noise_mask.dtype),
+            pltpu.VMEM((steps, frames, COEF_STEP), series.dtype),
+            pltpu.VMEM((1, total * COEF_STEP), noise_mask.dtype),
             pltpu.VMEM((2 * frames, COEF_STEP), jnp.bfloat16),
             pltpu.VMEM((frames, COEF_STEP), jnp.bfloat16),
-            pltpu.VMEM((2 * frames, frames), jnp.float32),
-            pltpu.SemaphoreType.DMA((steps,)),
+            pltpu.SemaphoreType.DMA((steps + 1,)),
             pltpu.SemaphoreType.DMA,
-        ],
+        ]
+        + ([] if more else [pltpu.VMEM(gram.shape, gram.dtype)]),
         compiler_params=pltpu.CompilerParams(vmem_limit_bytes=24 << 20),
         cost_estimate=pl.CostEstimate(
-            flops=4 * frames * frames * held,
-            bytes_accessed=4 * frames * held,
+            flops=4 * frames * frames * total * COEF_STEP,
+            bytes_accessed=4 * frames * total * COEF_STEP,
             transcendentals=0,
         ),
-    )(in_hbm(series), in_hbm(noise_mask.reshape(1, voxels)), probes.T, before)
+    )(in_hbm(series), in_hbm(noise_mask.reshape(1, voxels)), *arrays)
 
 
 def note_owners(plan, tile_owner, inverse):
@@ -261,14 +282,17 @@
     residue = inverse[device ^ plan.relative(place, stage + 1)]
     last = stage + 1 == len(plan.widths)
     base = 0 if last else ((device >> after) << after) * plan.owned
-    tile = (base + ((residue - base) & (devices - 1)) + slot * devices) & (tiles - 1)
+    start = base + ((residue - base) & (devices - 1))
+    if not last and plan.by_parity(stage + 1):
+        slot = (start >> plan.log) + slot & 1
+    tile = (start + slot * devices) & (tiles - 1)
     total = None
     for digit, source in enumerate(sources):
         sender = device ^ (digit << done)
         first = ((sender >> done) << done) * plan.owned
         offset = (tile - first) & (tiles - 1)
         there = offset < slots * devices
-        at = place * slots + jnp.minimum(offset >> plan.log, slots - 1)
+        at = place * slots + jnp.minimum(plan.slot(stage, tile, offset), slots - 1)
         value = source[pl.ds(pl.multiple_of(at * height + skip, 8), rows), :]
         value = jnp.where(there, value, 0.0)
         total = value if total is None else total + value
@@ -283,17 +307,19 @@
     return total
 
 
-def merge_kernel(plan, stage, span, fresh, tile_owner, *refs):
+def merge_kernel(plan, stage, span, fresh, *refs):
     fan = 1 << plan.widths[stage]
-    sources, refs = refs[:fan], refs[fan:]
+    plain = plan.by_parity(stage) and plan.by_parity(stage + 1)
+    if not plain:
+        tile_owner, inverse, refs = refs[0], refs[-1], refs[1:-1]
+        note_owners(plan, tile_owner, inverse)
+    sources, outs = refs[:fan], refs[fan:]
     coefs = None
     if fresh:
-        coefs, refs = refs[0][...] + refs[1][...], refs[2:]
-    outs, inverse = refs[:-1], refs[-1]
+        coefs, outs = outs[0][...] + outs[1][...], outs[2:]
     begin, rows = span
     slots, count = plan.slots[stage + 1], plan.owners[stage + 1]
     size = count * slots * rows
-    note_owners(plan, tile_owner, inverse)
     if outs[0].shape[0] > size:
         if not fresh:
             coefs = add_coefs(sources)
@@ -302,21 +328,25 @@
     height, skip = (plan.frames, begin) if stage == 0 else (rows, 0)
     for digit, out in enumerate(outs):
 
-        def owner(rest, carry):
-            for slot in range(slots):
+        def add(i, carry):
+            place, slot = digit * count + i // slots, i % slots
+            if plain:
+                read = pl.ds(pl.multiple_of((place * slots + slot) * height + skip, 8), rows)
+                value = sources[0][read, :]
+                for source in sources[1:]:
+                    value = value + source[read, :]
+            else:
                 value = add_tiles(
-                    plan, stage, inverse, sources, digit * count + rest, slot,
-                    height, skip, rows,
+                    plan, stage, inverse, sources, place, slot, height, skip, rows
                 )
-                target = pl.ds(pl.multiple_of((rest * slots + slot) * rows, 8), rows)
-                out[target, :] = value
+            out[pl.ds(pl.multiple_of(i * rows, 8), rows), :] = value
             return carry
 
         if count <= 4:
-            for rest in range(count):
-                owner(rest, 0)
+            for i in range(count * slots):
+                add(i, 0)
         else:
-            lax.fori_loop(0, count, owner, 0)
+            lax.fori_loop(0, count * slots, add, 0)
 
 
 def merge(plan, stage, span, riding, tile_owner, sources, coefs=()):
@@ -325,15 +355,19 @@
     block = jax.ShapeDtypeStruct((rows, LANES), jnp.float32)
     vmem = pl.BlockSpec(memory_space=pltpu.VMEM)
     arrays = list(sources) + list(coefs)
+    specs, scratch = [vmem] * len(arrays), []
+    if not (plan.by_parity(stage) and plan.by_parity(stage + 1)):
+        arrays, specs = [tile_owner] + arrays, [pl.BlockSpec(memory_space=pltpu.SMEM)] + specs
+        scratch = [pltpu.SMEM((plan.devices,), jnp.int32)]
     return pl.pallas_call(
         functools.partial(merge_kernel, plan, stage, span, len(coefs) > 0),
         name="merge",
-        in_specs=[pl.BlockSpec(memory_space=pltpu.SMEM)] + [vmem] * len(arrays),
+        in_specs=specs,
         out_specs=[vmem] * fan,
         out_shape=[block] * fan,
-        scratch_shapes=[pltpu.SMEM((plan.devices,), jnp.int32)],
+        scratch_shapes=scratch,
         compiler_params=pltpu.CompilerParams(vmem_limit_bytes=32 << 20),
-    )(tile_owner, *arrays)
+    )(*arrays)
 
 
 def finish_kernel(plan, comps, spans, tile_owner, *refs):
@@ -363,12 +397,18 @@
         ]
         values.append(jnp.concatenate(pieces, axis=0))
     value = jnp.concatenate(values, axis=1)
-    along = jnp.dot(unit, value, precision=HIGHEST, preferred_element_type=jnp.float32)
+    unit_high, unit_low = split(unit)
+    high, low = split(value)
+    wide = jnp.concatenate([unit_high, unit_low, unit_high], axis=1)
+    along = jnp.dot(
+        wide, jnp.concatenate([high, high, low], axis=0), preferred_element_type=jnp.float32
+    )
+    high, low = split(along)
+    tall = jnp.concatenate([unit_high, unit_low, unit_high], axis=0)
     value = value - lax.dot_general(
-        unit,
-        along,
+        tall,
+        jnp.concatenate([high, high, low], axis=0),
         (((0,), (0,)), ((), ())),
-        precision=HIGHEST,
         preferred_element_type=jnp.float32,
     )
     for slot in range(plan.owned):
@@ -408,13 +448,12 @@
     spans = [(0, cut), (cut, frames - cut)]
     steps = voxels // COEF_STEP
     keep, send = sample(plan, series, sample_weights, block_ids, tile_ids, tile_owner)
-    keep, send, probes = lax.optimization_barrier((keep, send, probes))
+    keep, send, marks = lax.optimization_barrier((keep, send, noise_mask))
     pair = exchange(plan, 0, [keep, send])
-    coefs = jnp.zeros((COEF_ROWS, LANES), jnp.float32)
-    coefs = local_coefs(series, noise_mask, probes, coefs, 0, EARLY)
+    grams = local_coefs(series, marks, 0, EARLY)
     chunks = [merge(plan, 0, span, False, tile_owner, pair) for span in spans[:-1]]
-    chunks[-1], coefs = lax.optimization_barrier((chunks[-1], coefs))
-    coefs = local_coefs(series, noise_mask, probes, coefs, EARLY, steps - EARLY)
+    chunks[-1], grams = lax.optimization_barrier((chunks[-1], grams))
+    coefs = local_coefs(series, noise_mask, EARLY + 1, steps - EARLY - 1, probes, grams)
     coefs = exchange(plan, 0, [coefs, coefs])
     chunks.append(merge(plan, 0, spans[-1], True, tile_owner, pair, coefs))
     for stage in range(1, stages):

time: 42.7 us -> 40.3 us (0.944)
  Pallas kernels: 18.5 us -> 15.8 us
  starting transfers between devices: 17.7 us -> 18.6 us
  waiting for transfers between devices: 6.25 us -> 5.61 us
    pallas_call x4, Pallas kernels: 3.08 us -> 1.55 us  [merge(): pl.pallas_call(functools.partial(merge_kernel, plan, stage, span, len(coe...]
    pallas_call x2, Pallas kernels: 8.47 us -> 7.52 us  [local_coefs(): pl.pallas_call(functools.partial(gram_kernel, first, steps, more), name='...]
    ppermute x14, starting transfers between devices: 17.7 us -> 18.6 us  [exchange(): received.append(lax.ppermute(blocks[digit], AXIS, pairs))]
    ppermute x14, waiting for transfers between devices: 6.25 us -> 5.61 us  [exchange(): received.append(lax.ppermute(blocks[digit], AXIS, pairs))]
  transfers between devices with their start and end apart: 14 -> 14, of which waited for: 4 -> 6; matrix products, arithmetic and copies ran while one was open for 0% -> 0% of each run, Pallas kernels for 25% -> 22%
where the time goes in v7:
time: 40.3 us; the launch traced here: 40.1 us
  starting transfers between devices  18.6 us (46%)
  Pallas kernels  15.8 us (39%)
  waiting for transfers between devices  5.61 us (14%)
    ppermute x14, starting transfers between devices, exchange(): received.append(lax.ppermute(blocks[digit], AXIS, pairs))  18.6 us
    pallas_call x2, Pallas kernels, local_coefs(): pl.pallas_call(functools.partial(gram_kernel, first, steps, more), name='...  7.52 us
    ppermute x14, waiting for transfers between devices, exchange(): received.append(lax.ppermute(blocks[digit], AXIS, pairs))  5.61 us
    pallas_call x1, Pallas kernels, sample(): pl.pallas_call(functools.partial(sample_kernel, plan), name='sample', in_...  4.68 us
    pallas_call x1, Pallas kernels, finish(): pl.pallas_call(functools.partial(finish_kernel, plan, comps, spans), name...  2.02 us
    pallas_call x4, Pallas kernels, merge(): pl.pallas_call(functools.partial(merge_kernel, plan, stage, span, len(coe...  1.55 us
  transfers between devices with their start and end apart: 14, of which 6 were waited for; matrix products, arithmetic and copies ran while one was open for 0% of the time, Pallas kernels for 22%

profile of v7, /device:TPU:0, one launch (start us, length us, event | category | flops | bytes accessed | tf_op | source)
XLA Modules:
  0.0 40.1 jit_solution(228560299596829463)
XLA Ops:
  0.0 4.7 %sample.1 = (f32[2640,128]{1,0:T(8,128)S(1)}, f32[2640,128]{1,0:T(8,128)S(1)}) custom-call(s32[48]{0:T(128)} %block_ids.1, s32[48]{0:T(128)} %tile_ids.1, s32[128]{0:T(128)} %tile_owner.3, f32[80,32768]{1,0:T(8,128)} %series.5, bf16[48,256,128]{2,1,0:T(8,128)(2,1)} %weights.1), custom_call_target="tpu_custom_call" | custom-call | tf_op jit(solution)/shard_map/sample/pallas_call | solution.py:150
  4.7 0.5 %collective-permute-start = (f32[2640,128]{1,0:T(8,128)S(1)}, f32[2640,128]{1,0:T(8,128)S(1)}, u32[]{:S(2)}, u32[]{:S(2)}) collective-permute-start(f32[2640,128]{1,0:T(8,128)S(1)} %get-tuple-element.40), channel_id=1, source_target_pairs={{0,1},{1,0},{2,3},{3,2},{4,5},{5,4},{6,7},{7,6},{8,9},{9,8},{10,11... | collective-permute-start | bytes 4055048 | tf_op jit(solution)/shard_map/ppermute | solution.py:436
  5.2 3.6 %gram.1 = (f32[160,80]{1,0:T(8,128)S(1)}, f32[80,4096]{1,0:T(8,128)S(1)}) custom-call(f32[80,32768]{1,0:T(8,128)} %series.5, s32[1,32768]{1,0:T(1,128)} %bitcast.4), custom_call_target="tpu_custom_call" | custom-call | flops 419430400 | bytes 5242880 | tf_op jit(solution)/shard_map/gram/pallas_call | solution.py:248
  8.8 0.0 copy-start.1
  8.9 0.1 merge.4
  9.0 2.6 %collective-permute-start.1 = (f32[384,128]{1,0:T(8,128)S(1)}, f32[384,128]{1,0:T(8,128)S(1)}, u32[]{:S(2)}, u32[]{:S(2)}) collective-permute-start(f32[384,128]{1,0:T(8,128)S(1)} %get-tuple-element.49), channel_id=1, source_target_pairs={{0,2},{1,3},{2,0},{3,1},{4,6},{5,7},{6,4},{7,5},{8,10},{9,11},{10,... | collective-permute-start | bytes 589832 | tf_op jit(solution)/shard_map/ppermute | solution.py:436
  11.5 1.5 %collective-permute-start.2 = (f32[384,128]{1,0:T(8,128)S(1)}, f32[384,128]{1,0:T(8,128)S(1)}, u32[]{:S(2)}, u32[]{:S(2)}) collective-permute-start(f32[384,128]{1,0:T(8,128)S(1)} %get-tuple-element.50), channel_id=1, source_target_pairs={{0,4},{1,5},{2,6},{3,7},{4,0},{5,1},{6,2},{7,3},{8,12},{9,13},{10,... | collective-permute-start | bytes 589832 | tf_op jit(solution)/shard_map/ppermute | solution.py:436
  13.1 0.0 collective-permute-start.3
  13.1 3.9 %coefs.1.refs_2_ = f32[8,128]{1,0:T(8,128)S(1)} custom-call(f32[80,32768]{1,0:T(8,128)} %series.5, s32[1,32768]{1,0:T(1,128)} %bitcast.5, f32[5,80]{1,0:T(8,128)S(1)} %bitcast.3, f32[160,80]{1,0:T(8,128)S(1)} %get-tuple-element.56.refs_1_, f32[80,4096]{1,0:T(8,128)S(1)} %get-tuple-element.57.refs_2_), custom_call_target="tpu_custom_call" | custom-call | flops 419430400 | bytes 5242880 | tf_op jit(solution)/shard_map/coefs/pallas_call | solution.py:248
  17.0 0.0 copy-start
  17.0 0.1 collective-permute-start.7
  17.0 1.2 %collective-permute-done.7.refs_3_ = f32[8,128]{1,0:T(8,128)S(1)} collective-permute-done((f32[8,128]{1,0:T(8,128)S(1)}, f32[8,128]{1,0:T(8,128)S(1)}, u32[]{:S(2)}, u32[]{:S(2)}) %collective-permute-start.7) | collective-permute-done | bytes 4128 | tf_op jit(solution)/shard_map/ppermute | solution.py:436
  18.2 0.1 merge.6
  18.3 2.0 %collective-permute-start.8 = (f32[264,128]{1,0:T(8,128)S(1)}, f32[264,128]{1,0:T(8,128)S(1)}, u32[]{:S(2)}, u32[]{:S(2)}) collective-permute-start(f32[264,128]{1,0:T(8,128)S(1)} %get-tuple-element.59), channel_id=1, source_target_pairs={{0,2},{1,3},{2,0},{3,1},{4,6},{5,7},{6,4},{7,5},{8,10},{9,11},{10,... | collective-permute-start | bytes 405512 | tf_op jit(solution)/shard_map/ppermute | solution.py:436
  20.3 1.5 %collective-permute-start.9 = (f32[264,128]{1,0:T(8,128)S(1)}, f32[264,128]{1,0:T(8,128)S(1)}, u32[]{:S(2)}, u32[]{:S(2)}) collective-permute-start(f32[264,128]{1,0:T(8,128)S(1)} %get-tuple-element.60), channel_id=1, source_target_pairs={{0,4},{1,5},{2,6},{3,7},{4,0},{5,1},{6,2},{7,3},{8,12},{9,13},{10,... | collective-permute-start | bytes 405512 | tf_op jit(solution)/shard_map/ppermute | solution.py:436
  21.8 0.0 collective-permute-done.1.refs_2_
  21.8 0.0 collective-permute-start.10
  21.8 0.9 %collective-permute-done.2.refs_3_ = f32[384,128]{1,0:T(8,128)S(1)} collective-permute-done((f32[384,128]{1,0:T(8,128)S(1)}, f32[384,128]{1,0:T(8,128)S(1)}, u32[]{:S(2)}, u32[]{:S(2)}) %collective-permute-start.2) | collective-permute-done | bytes 196640 | tf_op jit(solution)/shard_map/ppermute | solution.py:436
  22.8 0.0 collective-permute-done.3.refs_4_
  22.8 0.7 %merge.5 = (f32[144,128]{1,0:T(8,128)S(1)}, f32[144,128]{1,0:T(8,128)S(1)}, f32[144,128]{1,0:T(8,128)S(1)}, f32[144,128]{1,0:T(8,128)S(1)}) custom-call(s32[128]{0:T(128)S(1)} %copy-done, f32[384,128]{1,0:T(8,128)S(1)} %get-tuple-element.48.refs_1_, f32[384,128]{1,0:T(8,128)S(1)} %collective-permute-done.1.refs_2_, ...), custom_call_target="tpu_custom_call" | custom-call | tf_op jit(solution)/shard_map/merge/pallas_call | solution.py:362
  23.5 2.7 %collective-permute-start.5 = (f32[144,128]{1,0:T(8,128)S(1)}, f32[144,128]{1,0:T(8,128)S(1)}, u32[]{:S(2)}, u32[]{:S(2)}) collective-permute-start(f32[144,128]{1,0:T(8,128)S(1)} %get-tuple-element.54), channel_id=1, source_target_pairs={{0,16},{1,17},{2,18},{3,19},{4,20},{5,21},{6,22},{7,23},{8,24},{9,... | collective-permute-start | bytes 221192 | tf_op jit(solution)/shard_map/ppermute | solution.py:436
  26.1 1.4 %collective-permute-start.6 = (f32[144,128]{1,0:T(8,128)S(1)}, f32[144,128]{1,0:T(8,128)S(1)}, u32[]{:S(2)}, u32[]{:S(2)}) collective-permute-start(f32[144,128]{1,0:T(8,128)S(1)} %get-tuple-element.55), channel_id=1, source_target_pairs={{0,24},{1,25},{2,26},{3,27},{4,28},{5,29},{6,30},{7,31},{8,16},{9,... | collective-permute-start | bytes 221192 | tf_op jit(solution)/shard_map/ppermute | solution.py:436
  27.5 0.2 collective-permute-start.4
  27.7 0.8 %collective-permute-done.9.refs_3_ = f32[264,128]{1,0:T(8,128)S(1)} collective-permute-done((f32[264,128]{1,0:T(8,128)S(1)}, f32[264,128]{1,0:T(8,128)S(1)}, u32[]{:S(2)}, u32[]{:S(2)}) %collective-permute-start.9) | collective-permute-done | bytes 135200 | tf_op jit(solution)/shard_map/ppermute | solution.py:436
  28.6 0.7 %merge.7 = (f32[104,128]{1,0:T(8,128)S(1)}, f32[104,128]{1,0:T(8,128)S(1)}, f32[104,128]{1,0:T(8,128)S(1)}, f32[104,128]{1,0:T(8,128)S(1)}) custom-call(s32[128]{0:T(128)S(1)} %copy-done, f32[264,128]{1,0:T(8,128)S(1)} %get-tuple-element.58.refs_1_, f32[264,128]{1,0:T(8,128)S(1)} %collective-permute-done.8.refs_2_, ...), custom_call_target="tpu_custom_call" | custom-call | tf_op jit(solution)/shard_map/merge/pallas_call | solution.py:362
  29.3 2.7 %collective-permute-start.12 = (f32[104,128]{1,0:T(8,128)S(1)}, f32[104,128]{1,0:T(8,128)S(1)}, u32[]{:S(2)}, u32[]{:S(2)}) collective-permute-start(f32[104,128]{1,0:T(8,128)S(1)} %get-tuple-element.67), channel_id=1, source_target_pairs={{0,16},{1,17},{2,18},{3,19},{4,20},{5,21},{6,22},{7,23},{8,24},{9,... | collective-permute-start | bytes 159752 | tf_op jit(solution)/shard_map/ppermute | solution.py:436
  31.9 1.4 %collective-permute-start.13 = (f32[104,128]{1,0:T(8,128)S(1)}, f32[104,128]{1,0:T(8,128)S(1)}, u32[]{:S(2)}, u32[]{:S(2)}) collective-permute-start(f32[104,128]{1,0:T(8,128)S(1)} %get-tuple-element.68), channel_id=1, source_target_pairs={{0,24},{1,25},{2,26},{3,27},{4,28},{5,29},{6,30},{7,31},{8,16},{9,... | collective-permute-start | bytes 159752 | tf_op jit(solution)/shard_map/ppermute | solution.py:436
  33.3 2.1 %collective-permute-start.11 = (f32[104,128]{1,0:T(8,128)S(1)}, f32[104,128]{1,0:T(8,128)S(1)}, u32[]{:S(2)}, u32[]{:S(2)}) collective-permute-start(f32[104,128]{1,0:T(8,128)S(1)} %get-tuple-element.66), channel_id=1, source_target_pairs={{0,8},{1,9},{2,10},{3,11},{4,12},{5,13},{6,14},{7,15},{8,0},{9,1},... | collective-permute-start | bytes 159752 | tf_op jit(solution)/shard_map/ppermute | solution.py:436
  35.4 0.7 %collective-permute-done.12.refs_6_ = f32[104,128]{1,0:T(8,128)S(1)} collective-permute-done((f32[104,128]{1,0:T(8,128)S(1)}, f32[104,128]{1,0:T(8,128)S(1)}, u32[]{:S(2)}, u32[]{:S(2)}) %collective-permute-start.12) | collective-permute-done | bytes 53280 | tf_op jit(solution)/shard_map/ppermute | solution.py:436
  36.1 1.8 %collective-permute-done.13.refs_7_ = f32[104,128]{1,0:T(8,128)S(1)} collective-permute-done((f32[104,128]{1,0:T(8,128)S(1)}, f32[104,128]{1,0:T(8,128)S(1)}, u32[]{:S(2)}, u32[]{:S(2)}) %collective-permute-start.13) | collective-permute-done | bytes 53280 | tf_op jit(solution)/shard_map/ppermute | solution.py:436
  38.0 0.1 collective-permute-done.11.refs_5_
  38.1 2.0 %finish.1 = f32[4,80,128]{2,1,0:T(8,128)} custom-call(s32[128]{0:T(128)S(1)} %copy-done, f32[144,128]{1,0:T(8,128)S(1)} %get-tuple-element.52.refs_0_, f32[144,128]{1,0:T(8,128)S(1)} %collective-permute-done.4.refs_1_, f32[144,128]{1,0:T(8,128)S(1)} %collective-permute-done.5.refs_2_, f32[144,128]{1,0:T(8,128)S(1)} %collective-permute-done.6.refs_3_, ...), custom_call_target="tpu_custom_call" | custom-call | tf_op jit(solution)/shard_map/finish/pallas_call | solution.py:421
  (8 shorter events, 0.0 us)
Async XLA Ops:
  4.7 4.2 %collective-permute-start = (f32[2640,128]{1,0:T(8,128)S(1)}, f32[2640,128]{1,0:T(8,128)S(1)}, u32[]{:S(2)}, u32[]{:S(2)}) collective-permute-start(f32[2640,128]{1,0:T(8,128)S(1)} %get-tuple-element.40), channel_id=1, source_target_pairs={{0,1},{1,0},{2,3},{3,2},{4,5},{5,4},{6,7},{7,6},{8,9},{9,8},{10,11... | collective-permute-start | bytes 4055048 | tf_op jit(solution)/shard_map/ppermute | solution.py:436
  8.8 4.2 %copy-start.1 = (f32[80,5]{0,1:T(8,128)S(1)}, f32[80,5]{0,1:T(8,128)}, u32[]{:S(2)}) copy-start(f32[80,5]{0,1:T(8,128)} %param.9) | copy-start | bytes 4804
  9.0 12.8 %collective-permute-start.1 = (f32[384,128]{1,0:T(8,128)S(1)}, f32[384,128]{1,0:T(8,128)S(1)}, u32[]{:S(2)}, u32[]{:S(2)}) collective-permute-start(f32[384,128]{1,0:T(8,128)S(1)} %get-tuple-element.49), channel_id=1, source_target_pairs={{0,2},{1,3},{2,0},{3,1},{4,6},{5,7},{6,4},{7,5},{8,10},{9,11},{10,... | collective-permute-start | bytes 589832 | tf_op jit(solution)/shard_map/ppermute | solution.py:436
  11.5 11.2 %collective-permute-start.2 = (f32[384,128]{1,0:T(8,128)S(1)}, f32[384,128]{1,0:T(8,128)S(1)}, u32[]{:S(2)}, u32[]{:S(2)}) collective-permute-start(f32[384,128]{1,0:T(8,128)S(1)} %get-tuple-element.50), channel_id=1, source_target_pairs={{0,4},{1,5},{2,6},{3,7},{4,0},{5,1},{6,2},{7,3},{8,12},{9,13},{10,... | collective-permute-start | bytes 589832 | tf_op jit(solution)/shard_map/ppermute | solution.py:436
  13.1 9.7 %collective-permute-start.3 = (f32[384,128]{1,0:T(8,128)S(1)}, f32[384,128]{1,0:T(8,128)S(1)}, u32[]{:S(2)}, u32[]{:S(2)}) collective-permute-start(f32[384,128]{1,0:T(8,128)S(1)} %get-tuple-element.51), channel_id=1, source_target_pairs={{0,6},{1,7},{2,4},{3,5},{4,2},{5,3},{6,0},{7,1},{8,14},{9,15},{10,... | collective-permute-start | bytes 589832 | tf_op jit(solution)/shard_map/ppermute | solution.py:436
  17.0 5.8 %copy-start = (s32[128]{0:T(128)S(1)}, s32[128]{0:T(128)}, u32[]{:S(2)}) copy-start(s32[128]{0:T(128)} %tile_owner.3) | copy-start | bytes 1540
  17.0 1.2 %collective-permute-start.7 = (f32[8,128]{1,0:T(8,128)S(1)}, f32[8,128]{1,0:T(8,128)S(1)}, u32[]{:S(2)}, u32[]{:S(2)}) collective-permute-start(f32[8,128]{1,0:T(8,128)S(1)} %coefs.1.refs_2_), channel_id=1, source_target_pairs={{0,1},{1,0},{2,3},{3,2},{4,5},{5,4},{6,7},{7,6},{8,9},{9,8},{10,11... | collective-permute-start | bytes 12296 | tf_op jit(solution)/shard_map/ppermute | solution.py:436
  18.3 9.2 %collective-permute-start.8 = (f32[264,128]{1,0:T(8,128)S(1)}, f32[264,128]{1,0:T(8,128)S(1)}, u32[]{:S(2)}, u32[]{:S(2)}) collective-permute-start(f32[264,128]{1,0:T(8,128)S(1)} %get-tuple-element.59), channel_id=1, source_target_pairs={{0,2},{1,3},{2,0},{3,1},{4,6},{5,7},{6,4},{7,5},{8,10},{9,11},{10,... | collective-permute-start | bytes 405512 | tf_op jit(solution)/shard_map/ppermute | solution.py:436
  20.3 8.3 %collective-permute-start.9 = (f32[264,128]{1,0:T(8,128)S(1)}, f32[264,128]{1,0:T(8,128)S(1)}, u32[]{:S(2)}, u32[]{:S(2)}) collective-permute-start(f32[264,128]{1,0:T(8,128)S(1)} %get-tuple-element.60), channel_id=1, source_target_pairs={{0,4},{1,5},{2,6},{3,7},{4,0},{5,1},{6,2},{7,3},{8,12},{9,13},{10,... | collective-permute-start | bytes 405512 | tf_op jit(solution)/shard_map/ppermute | solution.py:436
  21.8 6.7 %collective-permute-start.10 = (f32[264,128]{1,0:T(8,128)S(1)}, f32[264,128]{1,0:T(8,128)S(1)}, u32[]{:S(2)}, u32[]{:S(2)}) collective-permute-start(f32[264,128]{1,0:T(8,128)S(1)} %get-tuple-element.61), channel_id=1, source_target_pairs={{0,6},{1,7},{2,4},{3,5},{4,2},{5,3},{6,0},{7,1},{8,14},{9,15},{10,... | collective-permute-start | bytes 405512 | tf_op jit(solution)/shard_map/ppermute | solution.py:436
  23.5 9.8 %collective-permute-start.5 = (f32[144,128]{1,0:T(8,128)S(1)}, f32[144,128]{1,0:T(8,128)S(1)}, u32[]{:S(2)}, u32[]{:S(2)}) collective-permute-start(f32[144,128]{1,0:T(8,128)S(1)} %get-tuple-element.54), channel_id=1, source_target_pairs={{0,16},{1,17},{2,18},{3,19},{4,20},{5,21},{6,22},{7,23},{8,24},{9,... | collective-permute-start | bytes 221192 | tf_op jit(solution)/shard_map/ppermute | solution.py:436
  26.1 7.1 %collective-permute-start.6 = (f32[144,128]{1,0:T(8,128)S(1)}, f32[144,128]{1,0:T(8,128)S(1)}, u32[]{:S(2)}, u32[]{:S(2)}) collective-permute-start(f32[144,128]{1,0:T(8,128)S(1)} %get-tuple-element.55), channel_id=1, source_target_pairs={{0,24},{1,25},{2,26},{3,27},{4,28},{5,29},{6,30},{7,31},{8,16},{9,... | collective-permute-start | bytes 221192 | tf_op jit(solution)/shard_map/ppermute | solution.py:436
  27.5 10.5 %collective-permute-start.4 = (f32[144,128]{1,0:T(8,128)S(1)}, f32[144,128]{1,0:T(8,128)S(1)}, u32[]{:S(2)}, u32[]{:S(2)}) collective-permute-start(f32[144,128]{1,0:T(8,128)S(1)} %get-tuple-element.53), channel_id=1, source_target_pairs={{0,8},{1,9},{2,10},{3,11},{4,12},{5,13},{6,14},{7,15},{8,0},{9,1},... | collective-permute-start | bytes 221192 | tf_op jit(solution)/shard_map/ppermute | solution.py:436
  29.3 6.9 %collective-permute-start.12 = (f32[104,128]{1,0:T(8,128)S(1)}, f32[104,128]{1,0:T(8,128)S(1)}, u32[]{:S(2)}, u32[]{:S(2)}) collective-permute-start(f32[104,128]{1,0:T(8,128)S(1)} %get-tuple-element.67), channel_id=1, source_target_pairs={{0,16},{1,17},{2,18},{3,19},{4,20},{5,21},{6,22},{7,23},{8,24},{9,... | collective-permute-start | bytes 159752 | tf_op jit(solution)/shard_map/ppermute | solution.py:436
  31.9 6.0 %collective-permute-start.13 = (f32[104,128]{1,0:T(8,128)S(1)}, f32[104,128]{1,0:T(8,128)S(1)}, u32[]{:S(2)}, u32[]{:S(2)}) collective-permute-start(f32[104,128]{1,0:T(8,128)S(1)} %get-tuple-element.68), channel_id=1, source_target_pairs={{0,24},{1,25},{2,26},{3,27},{4,28},{5,29},{6,30},{7,31},{8,16},{9,... | collective-permute-start | bytes 159752 | tf_op jit(solution)/shard_map/ppermute | solution.py:436
  33.3 4.8 %collective-permute-start.11 = (f32[104,128]{1,0:T(8,128)S(1)}, f32[104,128]{1,0:T(8,128)S(1)}, u32[]{:S(2)}, u32[]{:S(2)}) collective-permute-start(f32[104,128]{1,0:T(8,128)S(1)} %get-tuple-element.66), channel_id=1, source_target_pairs={{0,8},{1,9},{2,10},{3,11},{4,12},{5,13},{6,14},{7,15},{8,0},{9,1},... | collective-permute-start | bytes 159752 | tf_op jit(solution)/shard_map/ppermute | solution.py:436

commit v8 on v7

--- a/solution.py
+++ b/solution.py
@@ -85,7 +85,7 @@
 
 def sample_kernel(
     plan, block_ids, tile_ids, tile_owner, series, weights,
-    keep, send, picked, held, pick_sems, weight_sems,
+    keep, send, residues, picked, held, inverse, pick_sems, weight_sems,
 ):
     frames, width = plan.frames, plan.block_width
     groups = plan.entries // GROUP
@@ -110,6 +110,11 @@
     keep[...] = jnp.zeros_like(keep)
     send[...] = jnp.zeros_like(send)
     device = lax.axis_index(AXIS)
+    for residue in range(plan.devices):
+        inverse[tile_owner[residue]] = residue
+    for place in range(residues.shape[0]):
+        own = inverse[device ^ plan.relative(place, len(plan.widths) - 1)]
+        residues[place] = jnp.full(residues.shape[1:], own, jnp.int32)
     spare = plan.owners[0] * plan.slots[0]
 
     def group(g, carry):
@@ -151,11 +156,16 @@
         functools.partial(sample_kernel, plan),
         name="sample",
         in_specs=[smem, smem, smem, hbm, hbm],
-        out_specs=[vmem, vmem],
-        out_shape=[block, block],
+        out_specs=[vmem, vmem, vmem],
+        out_shape=[
+            block,
+            block,
+            jax.ShapeDtypeStruct((plan.owners[-2], 8, LANES), jnp.int32),
+        ],
         scratch_shapes=[
             pltpu.VMEM((plan.entries, frames, width), jnp.float32),
             pltpu.VMEM(weights.shape, weights.dtype),
+            pltpu.SMEM((plan.devices,), jnp.int32),
             pltpu.SemaphoreType.DMA((plan.entries,)),
             pltpu.SemaphoreType.DMA((plan.entries // GROUP,)),
         ],
@@ -269,34 +279,29 @@
     )(in_hbm(series), in_hbm(noise_mask.reshape(1, voxels)), *arrays)
 
 
-def note_owners(plan, tile_owner, inverse):
-    for residue in range(plan.devices):
-        inverse[tile_owner[residue]] = residue
-
-
-def add_tiles(plan, stage, inverse, sources, place, slot, height, skip=0, rows=None):
-    rows = height if rows is None else rows
+def add_tiles(plan, stage, residue, sources, place, slot, height):
     device = lax.axis_index(AXIS)
     done, after = plan.done[stage], plan.done[stage + 1]
     slots, devices, tiles = plan.slots[stage], plan.devices, plan.tiles
-    residue = inverse[device ^ plan.relative(place, stage + 1)]
     last = stage + 1 == len(plan.widths)
     base = 0 if last else ((device >> after) << after) * plan.owned
     start = base + ((residue - base) & (devices - 1))
     if not last and plan.by_parity(stage + 1):
-        slot = (start >> plan.log) + slot & 1
+        slot = ((start >> plan.log) + slot) & 1
     tile = (start + slot * devices) & (tiles - 1)
-    total = None
+    total = [jnp.zeros((8, LANES), jnp.float32)] * (height // 8)
     for digit, source in enumerate(sources):
         sender = device ^ (digit << done)
         first = ((sender >> done) << done) * plan.owned
         offset = (tile - first) & (tiles - 1)
         there = offset < slots * devices
-        at = place * slots + jnp.minimum(plan.slot(stage, tile, offset), slots - 1)
-        value = source[pl.ds(pl.multiple_of(at * height + skip, 8), rows), :]
-        value = jnp.where(there, value, 0.0)
-        total = value if total is None else total + value
-    return total
+        at = plan.slot(stage, tile, offset)
+        for other in range(slots):
+            chosen = there & (at == other)
+            for i in range(height // 8):
+                rows = pl.ds((place * slots + other) * height + 8 * i, 8)
+                total[i] = total[i] + jnp.where(chosen, source[rows, :], 0.0)
+    return jnp.concatenate(total, axis=0)
 
 
 def add_coefs(sources):
@@ -311,8 +316,7 @@
     fan = 1 << plan.widths[stage]
     plain = plan.by_parity(stage) and plan.by_parity(stage + 1)
     if not plain:
-        tile_owner, inverse, refs = refs[0], refs[-1], refs[1:-1]
-        note_owners(plan, tile_owner, inverse)
+        residues, refs = refs[0], refs[1:]
     sources, outs = refs[:fan], refs[fan:]
     coefs = None
     if fresh:
@@ -326,6 +330,7 @@
         for out in outs:
             out[pl.ds(size, COEF_ROWS), :] = coefs
     height, skip = (plan.frames, begin) if stage == 0 else (rows, 0)
+    assert plain or (skip == 0 and height == rows)
     for digit, out in enumerate(outs):
 
         def add(i, carry):
@@ -336,47 +341,42 @@
                 for source in sources[1:]:
                     value = value + source[read, :]
             else:
-                value = add_tiles(
-                    plan, stage, inverse, sources, place, slot, height, skip, rows
-                )
+                value = add_tiles(plan, stage, residues[place], sources, place, slot, rows)
             out[pl.ds(pl.multiple_of(i * rows, 8), rows), :] = value
             return carry
 
-        if count <= 4:
+        if count <= 4 or not plain:
             for i in range(count * slots):
                 add(i, 0)
         else:
             lax.fori_loop(0, count * slots, add, 0)
 
 
-def merge(plan, stage, span, riding, tile_owner, sources, coefs=()):
+def merge(plan, stage, span, riding, residues, sources, coefs=()):
     fan = 1 << plan.widths[stage + 1]
     rows = plan.tiles_in(stage + 1) * span[1] + (COEF_ROWS if riding else 0)
     block = jax.ShapeDtypeStruct((rows, LANES), jnp.float32)
     vmem = pl.BlockSpec(memory_space=pltpu.VMEM)
     arrays = list(sources) + list(coefs)
-    specs, scratch = [vmem] * len(arrays), []
     if not (plan.by_parity(stage) and plan.by_parity(stage + 1)):
-        arrays, specs = [tile_owner] + arrays, [pl.BlockSpec(memory_space=pltpu.SMEM)] + specs
-        scratch = [pltpu.SMEM((plan.devices,), jnp.int32)]
+        assert stage + 2 == len(plan.widths)
+        arrays = [residues] + arrays
     return pl.pallas_call(
         functools.partial(merge_kernel, plan, stage, span, len(coefs) > 0),
         name="merge",
-        in_specs=specs,
+        in_specs=[vmem] * len(arrays),
         out_specs=[vmem] * fan,
         out_shape=[block] * fan,
-        scratch_shapes=scratch,
         compiler_params=pltpu.CompilerParams(vmem_limit_bytes=32 << 20),
     )(*arrays)
 
 
-def finish_kernel(plan, comps, spans, tile_owner, *refs):
+def finish_kernel(plan, comps, spans, residues, *refs):
     stage = len(plan.widths) - 1
     fan = 1 << plan.widths[stage]
     parts = [refs[i * fan : (i + 1) * fan] for i in range(len(spans))]
-    out, inverse = refs[-2:]
+    out = refs[-1]
     frames = plan.frames
-    note_owners(plan, tile_owner, inverse)
     basis = add_coefs(parts[-1])
     lane = lax.broadcasted_iota(jnp.int32, basis.shape, 1)
     row = lax.broadcasted_iota(jnp.int32, basis.shape, 0)
@@ -392,7 +392,7 @@
     values = []
     for slot in range(plan.owned):
         pieces = [
-            add_tiles(plan, stage, inverse, sources, 0, slot, rows)
+            add_tiles(plan, stage, residues[0], sources, 0, slot, rows)
             for (begin, rows), sources in zip(spans, parts)
         ]
         values.append(jnp.concatenate(pieces, axis=0))
@@ -415,18 +415,17 @@
         out[slot] = value[:, slot * plan.tile_width : (slot + 1) * plan.tile_width]
 
 
-def finish(plan, comps, spans, tile_owner, parts):
+def finish(plan, comps, spans, residues, parts):
     vmem = pl.BlockSpec(memory_space=pltpu.VMEM)
     arrays = [block for part in parts for block in part]
     return pl.pallas_call(
         functools.partial(finish_kernel, plan, comps, spans),
         name="finish",
-        in_specs=[pl.BlockSpec(memory_space=pltpu.SMEM)] + [vmem] * len(arrays),
+        in_specs=[vmem] * (1 + len(arrays)),
         out_specs=vmem,
         out_shape=jax.ShapeDtypeStruct((plan.owned, plan.frames, plan.tile_width), jnp.float32),
-        scratch_shapes=[pltpu.SMEM((plan.devices,), jnp.int32)],
         compiler_params=pltpu.CompilerParams(vmem_limit_bytes=32 << 20),
-    )(tile_owner, *arrays)
+    )(residues, *arrays)
 
 
 def exchange(plan, stage, blocks):
@@ -447,15 +446,15 @@
     cut = frames * 3 // 5 // 8 * 8
     spans = [(0, cut), (cut, frames - cut)]
     steps = voxels // COEF_STEP
-    keep, send = sample(plan, series, sample_weights, block_ids, tile_ids, tile_owner)
+    keep, send, residues = sample(plan, series, sample_weights, block_ids, tile_ids, tile_owner)
     keep, send, marks = lax.optimization_barrier((keep, send, noise_mask))
     pair = exchange(plan, 0, [keep, send])
     grams = local_coefs(series, marks, 0, EARLY)
-    chunks = [merge(plan, 0, span, False, tile_owner, pair) for span in spans[:-1]]
+    chunks = [merge(plan, 0, span, False, residues, pair) for span in spans[:-1]]
     chunks[-1], grams = lax.optimization_barrier((chunks[-1], grams))
     coefs = local_coefs(series, noise_mask, EARLY + 1, steps - EARLY - 1, probes, grams)
     coefs = exchange(plan, 0, [coefs, coefs])
-    chunks.append(merge(plan, 0, spans[-1], True, tile_owner, pair, coefs))
+    chunks.append(merge(plan, 0, spans[-1], True, residues, pair, coefs))
     for stage in range(1, stages):
         for i, span in enumerate(spans):
             if stage + 1 == stages and i > 0:
@@ -465,8 +464,8 @@
             chunks[i] = exchange(plan, stage, chunks[i])
             if stage + 1 < stages:
                 riding = i + 1 == len(spans)
-                chunks[i] = merge(plan, stage, span, riding, tile_owner, chunks[i])
-    return finish(plan, probes.shape[1], spans, tile_owner, chunks)
+                chunks[i] = merge(plan, stage, span, riding, residues, chunks[i])
+    return finish(plan, probes.shape[1], spans, residues, chunks)
 
 
 def solution(mesh):

time: 40.3 us -> 39.2 us (0.973)
  Pallas kernels: 15.8 us -> 14.2 us
  waiting for transfers between devices: 5.61 us -> 6.15 us
    pallas_call x4, Pallas kernels: 1.55 us -> 0.48 us  [merge(): pl.pallas_call(functools.partial(merge_kernel, plan, stage, span, len(coe...]
    ppermute x14, waiting for transfers between devices: 5.61 us -> 6.15 us  [exchange(): received.append(lax.ppermute(blocks[digit], AXIS, pairs))]
    pallas_call x1, Pallas kernels: 2.02 us -> 1.51 us  [finish(): pl.pallas_call(functools.partial(finish_kernel, plan, comps, spans), name...]
  transfers between devices with their start and end apart: 14 -> 14, of which waited for: 6 -> 6; matrix products, arithmetic and copies ran while one was open for 0% -> 0% of each run, Pallas kernels for 22% -> 20%
where the time goes in v8:
time: 39.2 us; the launch traced here: 39.1 us
  starting transfers between devices  18.6 us (47%)
  Pallas kernels  14.2 us (36%)
  waiting for transfers between devices  6.15 us (16%)
    ppermute x14, starting transfers between devices, exchange(): received.append(lax.ppermute(blocks[digit], AXIS, pairs))  18.6 us
    pallas_call x2, Pallas kernels, local_coefs(): pl.pallas_call(functools.partial(gram_kernel, first, steps, more), name='...  7.52 us
    ppermute x14, waiting for transfers between devices, exchange(): received.append(lax.ppermute(blocks[digit], AXIS, pairs))  6.15 us
    pallas_call x1, Pallas kernels, sample(): pl.pallas_call(functools.partial(sample_kernel, plan), name='sample', in_...  4.68 us
    pallas_call x1, Pallas kernels, finish(): pl.pallas_call(functools.partial(finish_kernel, plan, comps, spans), name...  1.51 us
  transfers between devices with their start and end apart: 14, of which 6 were waited for; matrix products, arithmetic and copies ran while one was open for 0% of the time, Pallas kernels for 20%

profile of v8, /device:TPU:0, one launch (start us, length us, event | category | flops | bytes accessed | tf_op | source)
XLA Modules:
  0.0 39.1 jit_solution(2956256709514042638)
XLA Ops:
  0.0 4.7 %sample.1 = (f32[2640,128]{1,0:T(8,128)S(1)}, f32[2640,128]{1,0:T(8,128)S(1)}, s32[4,8,128]{2,1,0:T(8,128)S(1)}) custom-call(s32[48]{0:T(128)} %block_ids.1, s32[48]{0:T(128)} %tile_ids.1, s32[128]{0:T(128)} %tile_owner.1, f32[80,32768]{1,0:T(8,128)} %series.5, bf16[48,256,128]{2,1,0:T(8,128)(2,1)} %weights.1), custom_call_target="tpu_custom_call" | custom-call | tf_op jit(solution)/shard_map/sample/pallas_call | solution.py:155
  4.7 0.5 %collective-permute-start = (f32[2640,128]{1,0:T(8,128)S(1)}, f32[2640,128]{1,0:T(8,128)S(1)}, u32[]{:S(2)}, u32[]{:S(2)}) collective-permute-start(f32[2640,128]{1,0:T(8,128)S(1)} %get-tuple-element.42), channel_id=1, source_target_pairs={{0,1},{1,0},{2,3},{3,2},{4,5},{5,4},{6,7},{7,6},{8,9},{9,8},{10,11... | collective-permute-start | bytes 4055048 | tf_op jit(solution)/shard_map/ppermute | solution.py:435
  5.2 3.6 %gram.1 = (f32[160,80]{1,0:T(8,128)S(1)}, f32[80,4096]{1,0:T(8,128)S(1)}) custom-call(f32[80,32768]{1,0:T(8,128)} %series.5, s32[1,32768]{1,0:T(1,128)} %bitcast.4), custom_call_target="tpu_custom_call" | custom-call | flops 419430400 | bytes 5242880 | tf_op jit(solution)/shard_map/gram/pallas_call | solution.py:258
  8.8 0.0 copy-start
  8.9 0.1 merge.4
  9.0 2.6 %collective-permute-start.1 = (f32[384,128]{1,0:T(8,128)S(1)}, f32[384,128]{1,0:T(8,128)S(1)}, u32[]{:S(2)}, u32[]{:S(2)}) collective-permute-start(f32[384,128]{1,0:T(8,128)S(1)} %get-tuple-element.51), channel_id=1, source_target_pairs={{0,2},{1,3},{2,0},{3,1},{4,6},{5,7},{6,4},{7,5},{8,10},{9,11},{10,... | collective-permute-start | bytes 589832 | tf_op jit(solution)/shard_map/ppermute | solution.py:435
  11.5 1.5 %collective-permute-start.2 = (f32[384,128]{1,0:T(8,128)S(1)}, f32[384,128]{1,0:T(8,128)S(1)}, u32[]{:S(2)}, u32[]{:S(2)}) collective-permute-start(f32[384,128]{1,0:T(8,128)S(1)} %get-tuple-element.52), channel_id=1, source_target_pairs={{0,4},{1,5},{2,6},{3,7},{4,0},{5,1},{6,2},{7,3},{8,12},{9,13},{10,... | collective-permute-start | bytes 589832 | tf_op jit(solution)/shard_map/ppermute | solution.py:435
  13.1 0.0 collective-permute-start.3
  13.1 3.9 %coefs.1.refs_2_ = f32[8,128]{1,0:T(8,128)S(1)} custom-call(f32[80,32768]{1,0:T(8,128)} %series.5, s32[1,32768]{1,0:T(1,128)} %bitcast.5, f32[5,80]{1,0:T(8,128)S(1)} %bitcast.3, f32[160,80]{1,0:T(8,128)S(1)} %get-tuple-element.58.refs_1_, f32[80,4096]{1,0:T(8,128)S(1)} %get-tuple-element.59.refs_2_), custom_call_target="tpu_custom_call" | custom-call | flops 419430400 | bytes 5242880 | tf_op jit(solution)/shard_map/coefs/pallas_call | solution.py:258
  17.0 0.1 collective-permute-start.7
  17.0 1.2 %collective-permute-done.7.refs_3_ = f32[8,128]{1,0:T(8,128)S(1)} collective-permute-done((f32[8,128]{1,0:T(8,128)S(1)}, f32[8,128]{1,0:T(8,128)S(1)}, u32[]{:S(2)}, u32[]{:S(2)}) %collective-permute-start.7) | collective-permute-done | bytes 4128 | tf_op jit(solution)/shard_map/ppermute | solution.py:435
  18.2 0.1 merge.6
  18.2 2.0 %collective-permute-start.8 = (f32[264,128]{1,0:T(8,128)S(1)}, f32[264,128]{1,0:T(8,128)S(1)}, u32[]{:S(2)}, u32[]{:S(2)}) collective-permute-start(f32[264,128]{1,0:T(8,128)S(1)} %get-tuple-element.61), channel_id=1, source_target_pairs={{0,2},{1,3},{2,0},{3,1},{4,6},{5,7},{6,4},{7,5},{8,10},{9,11},{10,... | collective-permute-start | bytes 405512 | tf_op jit(solution)/shard_map/ppermute | solution.py:435
  20.3 1.5 %collective-permute-start.9 = (f32[264,128]{1,0:T(8,128)S(1)}, f32[264,128]{1,0:T(8,128)S(1)}, u32[]{:S(2)}, u32[]{:S(2)}) collective-permute-start(f32[264,128]{1,0:T(8,128)S(1)} %get-tuple-element.62), channel_id=1, source_target_pairs={{0,4},{1,5},{2,6},{3,7},{4,0},{5,1},{6,2},{7,3},{8,12},{9,13},{10,... | collective-permute-start | bytes 405512 | tf_op jit(solution)/shard_map/ppermute | solution.py:435
  21.8 0.0 collective-permute-start.10
  21.8 0.9 %collective-permute-done.2.refs_3_ = f32[384,128]{1,0:T(8,128)S(1)} collective-permute-done((f32[384,128]{1,0:T(8,128)S(1)}, f32[384,128]{1,0:T(8,128)S(1)}, u32[]{:S(2)}, u32[]{:S(2)}) %collective-permute-start.2) | collective-permute-done | bytes 196640 | tf_op jit(solution)/shard_map/ppermute | solution.py:435
  22.8 0.0 collective-permute-done.3.refs_4_
  22.8 0.2 merge.5
  23.0 2.7 %collective-permute-start.5 = (f32[144,128]{1,0:T(8,128)S(1)}, f32[144,128]{1,0:T(8,128)S(1)}, u32[]{:S(2)}, u32[]{:S(2)}) collective-permute-start(f32[144,128]{1,0:T(8,128)S(1)} %get-tuple-element.56), channel_id=1, source_target_pairs={{0,16},{1,17},{2,18},{3,19},{4,20},{5,21},{6,22},{7,23},{8,24},{9,... | collective-permute-start | bytes 221192 | tf_op jit(solution)/shard_map/ppermute | solution.py:435
  25.6 1.4 %collective-permute-start.6 = (f32[144,128]{1,0:T(8,128)S(1)}, f32[144,128]{1,0:T(8,128)S(1)}, u32[]{:S(2)}, u32[]{:S(2)}) collective-permute-start(f32[144,128]{1,0:T(8,128)S(1)} %get-tuple-element.57), channel_id=1, source_target_pairs={{0,24},{1,25},{2,26},{3,27},{4,28},{5,29},{6,30},{7,31},{8,16},{9,... | collective-permute-start | bytes 221192 | tf_op jit(solution)/shard_map/ppermute | solution.py:435
  27.0 0.0 collective-permute-done.8.refs_2_
  27.0 0.2 collective-permute-start.4
  27.2 1.4 %collective-permute-done.9.refs_3_ = f32[264,128]{1,0:T(8,128)S(1)} collective-permute-done((f32[264,128]{1,0:T(8,128)S(1)}, f32[264,128]{1,0:T(8,128)S(1)}, u32[]{:S(2)}, u32[]{:S(2)}) %collective-permute-start.9) | collective-permute-done | bytes 135200 | tf_op jit(solution)/shard_map/ppermute | solution.py:435
  28.6 0.0 collective-permute-done.10.refs_4_
  28.6 0.1 merge.7
  28.7 2.7 %collective-permute-start.12 = (f32[104,128]{1,0:T(8,128)S(1)}, f32[104,128]{1,0:T(8,128)S(1)}, u32[]{:S(2)}, u32[]{:S(2)}) collective-permute-start(f32[104,128]{1,0:T(8,128)S(1)} %get-tuple-element.69), channel_id=1, source_target_pairs={{0,16},{1,17},{2,18},{3,19},{4,20},{5,21},{6,22},{7,23},{8,24},{9,... | collective-permute-start | bytes 159752 | tf_op jit(solution)/shard_map/ppermute | solution.py:435
  31.4 1.4 %collective-permute-start.13 = (f32[104,128]{1,0:T(8,128)S(1)}, f32[104,128]{1,0:T(8,128)S(1)}, u32[]{:S(2)}, u32[]{:S(2)}) collective-permute-start(f32[104,128]{1,0:T(8,128)S(1)} %get-tuple-element.70), channel_id=1, source_target_pairs={{0,24},{1,25},{2,26},{3,27},{4,28},{5,29},{6,30},{7,31},{8,16},{9,... | collective-permute-start | bytes 159752 | tf_op jit(solution)/shard_map/ppermute | solution.py:435
  32.7 2.1 %collective-permute-start.11 = (f32[104,128]{1,0:T(8,128)S(1)}, f32[104,128]{1,0:T(8,128)S(1)}, u32[]{:S(2)}, u32[]{:S(2)}) collective-permute-start(f32[104,128]{1,0:T(8,128)S(1)} %get-tuple-element.68), channel_id=1, source_target_pairs={{0,8},{1,9},{2,10},{3,11},{4,12},{5,13},{6,14},{7,15},{8,0},{9,1},... | collective-permute-start | bytes 159752 | tf_op jit(solution)/shard_map/ppermute | solution.py:435
  34.9 0.7 %collective-permute-done.12.refs_6_ = f32[104,128]{1,0:T(8,128)S(1)} collective-permute-done((f32[104,128]{1,0:T(8,128)S(1)}, f32[104,128]{1,0:T(8,128)S(1)}, u32[]{:S(2)}, u32[]{:S(2)}) %collective-permute-start.12) | collective-permute-done | bytes 53280 | tf_op jit(solution)/shard_map/ppermute | solution.py:435
  35.6 1.8 %collective-permute-done.13.refs_7_ = f32[104,128]{1,0:T(8,128)S(1)} collective-permute-done((f32[104,128]{1,0:T(8,128)S(1)}, f32[104,128]{1,0:T(8,128)S(1)}, u32[]{:S(2)}, u32[]{:S(2)}) %collective-permute-start.13) | collective-permute-done | bytes 53280 | tf_op jit(solution)/shard_map/ppermute | solution.py:435
  37.4 0.1 collective-permute-done.11.refs_5_
  37.6 1.5 %finish.1 = f32[4,80,128]{2,1,0:T(8,128)} custom-call(s32[4,8,128]{2,1,0:T(8,128)S(1)} %get-tuple-element.38.refs_0_.residues, f32[144,128]{1,0:T(8,128)S(1)} %get-tuple-element.54.refs_0_, f32[144,128]{1,0:T(8,128)S(1)} %collective-permute-done.4.refs_1_, f32[144,128]{1,0:T(8,128)S(1)} %collective-permute-done.5.refs_2_, ...), custom_call_target="tpu_custom_call" | custom-call | tf_op jit(solution)/shard_map/finish/pallas_call | solution.py:421
  (6 shorter events, 0.0 us)
Async XLA Ops:
  4.7 4.2 %collective-permute-start = (f32[2640,128]{1,0:T(8,128)S(1)}, f32[2640,128]{1,0:T(8,128)S(1)}, u32[]{:S(2)}, u32[]{:S(2)}) collective-permute-start(f32[2640,128]{1,0:T(8,128)S(1)} %get-tuple-element.42), channel_id=1, source_target_pairs={{0,1},{1,0},{2,3},{3,2},{4,5},{5,4},{6,7},{7,6},{8,9},{9,8},{10,11... | collective-permute-start | bytes 4055048 | tf_op jit(solution)/shard_map/ppermute | solution.py:435
  8.8 4.2 %copy-start = (f32[80,5]{0,1:T(8,128)S(1)}, f32[80,5]{0,1:T(8,128)}, u32[]{:S(2)}) copy-start(f32[80,5]{0,1:T(8,128)} %param.9) | copy-start | bytes 4804
  9.0 12.8 %collective-permute-start.1 = (f32[384,128]{1,0:T(8,128)S(1)}, f32[384,128]{1,0:T(8,128)S(1)}, u32[]{:S(2)}, u32[]{:S(2)}) collective-permute-start(f32[384,128]{1,0:T(8,128)S(1)} %get-tuple-element.51), channel_id=1, source_target_pairs={{0,2},{1,3},{2,0},{3,1},{4,6},{5,7},{6,4},{7,5},{8,10},{9,11},{10,... | collective-permute-start | bytes 589832 | tf_op jit(solution)/shard_map/ppermute | solution.py:435
  11.5 11.2 %collective-permute-start.2 = (f32[384,128]{1,0:T(8,128)S(1)}, f32[384,128]{1,0:T(8,128)S(1)}, u32[]{:S(2)}, u32[]{:S(2)}) collective-permute-start(f32[384,128]{1,0:T(8,128)S(1)} %get-tuple-element.52), channel_id=1, source_target_pairs={{0,4},{1,5},{2,6},{3,7},{4,0},{5,1},{6,2},{7,3},{8,12},{9,13},{10,... | collective-permute-start | bytes 589832 | tf_op jit(solution)/shard_map/ppermute | solution.py:435
  13.1 9.7 %collective-permute-start.3 = (f32[384,128]{1,0:T(8,128)S(1)}, f32[384,128]{1,0:T(8,128)S(1)}, u32[]{:S(2)}, u32[]{:S(2)}) collective-permute-start(f32[384,128]{1,0:T(8,128)S(1)} %get-tuple-element.53), channel_id=1, source_target_pairs={{0,6},{1,7},{2,4},{3,5},{4,2},{5,3},{6,0},{7,1},{8,14},{9,15},{10,... | collective-permute-start | bytes 589832 | tf_op jit(solution)/shard_map/ppermute | solution.py:435
  17.0 1.2 %collective-permute-start.7 = (f32[8,128]{1,0:T(8,128)S(1)}, f32[8,128]{1,0:T(8,128)S(1)}, u32[]{:S(2)}, u32[]{:S(2)}) collective-permute-start(f32[8,128]{1,0:T(8,128)S(1)} %coefs.1.refs_2_), channel_id=1, source_target_pairs={{0,1},{1,0},{2,3},{3,2},{4,5},{5,4},{6,7},{7,6},{8,9},{9,8},{10,11... | collective-permute-start | bytes 12296 | tf_op jit(solution)/shard_map/ppermute | solution.py:435
  18.2 8.7 %collective-permute-start.8 = (f32[264,128]{1,0:T(8,128)S(1)}, f32[264,128]{1,0:T(8,128)S(1)}, u32[]{:S(2)}, u32[]{:S(2)}) collective-permute-start(f32[264,128]{1,0:T(8,128)S(1)} %get-tuple-element.61), channel_id=1, source_target_pairs={{0,2},{1,3},{2,0},{3,1},{4,6},{5,7},{6,4},{7,5},{8,10},{9,11},{10,... | collective-permute-start | bytes 405512 | tf_op jit(solution)/shard_map/ppermute | solution.py:435
  20.3 8.3 %collective-permute-start.9 = (f32[264,128]{1,0:T(8,128)S(1)}, f32[264,128]{1,0:T(8,128)S(1)}, u32[]{:S(2)}, u32[]{:S(2)}) collective-permute-start(f32[264,128]{1,0:T(8,128)S(1)} %get-tuple-element.62), channel_id=1, source_target_pairs={{0,4},{1,5},{2,6},{3,7},{4,0},{5,1},{6,2},{7,3},{8,12},{9,13},{10,... | collective-permute-start | bytes 405512 | tf_op jit(solution)/shard_map/ppermute | solution.py:435
  21.8 6.8 %collective-permute-start.10 = (f32[264,128]{1,0:T(8,128)S(1)}, f32[264,128]{1,0:T(8,128)S(1)}, u32[]{:S(2)}, u32[]{:S(2)}) collective-permute-start(f32[264,128]{1,0:T(8,128)S(1)} %get-tuple-element.63), channel_id=1, source_target_pairs={{0,6},{1,7},{2,4},{3,5},{4,2},{5,3},{6,0},{7,1},{8,14},{9,15},{10,... | collective-permute-start | bytes 405512 | tf_op jit(solution)/shard_map/ppermute | solution.py:435
  23.0 9.8 %collective-permute-start.5 = (f32[144,128]{1,0:T(8,128)S(1)}, f32[144,128]{1,0:T(8,128)S(1)}, u32[]{:S(2)}, u32[]{:S(2)}) collective-permute-start(f32[144,128]{1,0:T(8,128)S(1)} %get-tuple-element.56), channel_id=1, source_target_pairs={{0,16},{1,17},{2,18},{3,19},{4,20},{5,21},{6,22},{7,23},{8,24},{9,... | collective-permute-start | bytes 221192 | tf_op jit(solution)/shard_map/ppermute | solution.py:435
  25.6 7.1 %collective-permute-start.6 = (f32[144,128]{1,0:T(8,128)S(1)}, f32[144,128]{1,0:T(8,128)S(1)}, u32[]{:S(2)}, u32[]{:S(2)}) collective-permute-start(f32[144,128]{1,0:T(8,128)S(1)} %get-tuple-element.57), channel_id=1, source_target_pairs={{0,24},{1,25},{2,26},{3,27},{4,28},{5,29},{6,30},{7,31},{8,16},{9,... | collective-permute-start | bytes 221192 | tf_op jit(solution)/shard_map/ppermute | solution.py:435
  27.0 10.4 %collective-permute-start.4 = (f32[144,128]{1,0:T(8,128)S(1)}, f32[144,128]{1,0:T(8,128)S(1)}, u32[]{:S(2)}, u32[]{:S(2)}) collective-permute-start(f32[144,128]{1,0:T(8,128)S(1)} %get-tuple-element.55), channel_id=1, source_target_pairs={{0,8},{1,9},{2,10},{3,11},{4,12},{5,13},{6,14},{7,15},{8,0},{9,1},... | collective-permute-start | bytes 221192 | tf_op jit(solution)/shard_map/ppermute | solution.py:435
  28.7 6.9 %collective-permute-start.12 = (f32[104,128]{1,0:T(8,128)S(1)}, f32[104,128]{1,0:T(8,128)S(1)}, u32[]{:S(2)}, u32[]{:S(2)}) collective-permute-start(f32[104,128]{1,0:T(8,128)S(1)} %get-tuple-element.69), channel_id=1, source_target_pairs={{0,16},{1,17},{2,18},{3,19},{4,20},{5,21},{6,22},{7,23},{8,24},{9,... | collective-permute-start | bytes 159752 | tf_op jit(solution)/shard_map/ppermute | solution.py:435
  31.4 6.0 %collective-permute-start.13 = (f32[104,128]{1,0:T(8,128)S(1)}, f32[104,128]{1,0:T(8,128)S(1)}, u32[]{:S(2)}, u32[]{:S(2)}) collective-permute-start(f32[104,128]{1,0:T(8,128)S(1)} %get-tuple-element.70), channel_id=1, source_target_pairs={{0,24},{1,25},{2,26},{3,27},{4,28},{5,29},{6,30},{7,31},{8,16},{9,... | collective-permute-start | bytes 159752 | tf_op jit(solution)/shard_map/ppermute | solution.py:435
  32.7 4.8 %collective-permute-start.11 = (f32[104,128]{1,0:T(8,128)S(1)}, f32[104,128]{1,0:T(8,128)S(1)}, u32[]{:S(2)}, u32[]{:S(2)}) collective-permute-start(f32[104,128]{1,0:T(8,128)S(1)} %get-tuple-element.68), channel_id=1, source_target_pairs={{0,8},{1,9},{2,10},{3,11},{4,12},{5,13},{6,14},{7,15},{8,0},{9,1},... | collective-permute-start | bytes 159752 | tf_op jit(solution)/shard_map/ppermute | solution.py:435

commit v9 on v8

--- a/solution.py
+++ b/solution.py
@@ -85,7 +85,7 @@
 
 def sample_kernel(
     plan, block_ids, tile_ids, tile_owner, series, weights,
-    keep, send, residues, picked, held, inverse, pick_sems, weight_sems,
+    keep, send, residues, ahead, picked, held, inverse, pick_sems, weight_sems, sem,
 ):
     frames, width = plan.frames, plan.block_width
     groups = plan.entries // GROUP
@@ -107,6 +107,8 @@
         return carry
 
     lax.fori_loop(0, groups, begin, 0)
+    ahead_copy = pltpu.make_async_copy(series.at[:, pl.ds(0, COEF_STEP)], ahead, sem)
+    ahead_copy.start()
     keep[...] = jnp.zeros_like(keep)
     send[...] = jnp.zeros_like(send)
     device = lax.axis_index(AXIS)
@@ -143,6 +145,7 @@
         return carry
 
     lax.fori_loop(0, groups, group, 0)
+    ahead_copy.wait()
 
 
 def sample(plan, series, weights, block_ids, tile_ids, tile_owner):
@@ -156,11 +159,12 @@
         functools.partial(sample_kernel, plan),
         name="sample",
         in_specs=[smem, smem, smem, hbm, hbm],
-        out_specs=[vmem, vmem, vmem],
+        out_specs=[vmem] * 4,
         out_shape=[
             block,
             block,
             jax.ShapeDtypeStruct((plan.owners[-2], 8, LANES), jnp.int32),
+            jax.ShapeDtypeStruct((frames, COEF_STEP), series.dtype),
         ],
         scratch_shapes=[
             pltpu.VMEM((plan.entries, frames, width), jnp.float32),
@@ -168,6 +172,7 @@
             pltpu.SMEM((plan.devices,), jnp.int32),
             pltpu.SemaphoreType.DMA((plan.entries,)),
             pltpu.SemaphoreType.DMA((plan.entries // GROUP,)),
+            pltpu.SemaphoreType.DMA,
         ],
         compiler_params=pltpu.CompilerParams(
             vmem_limit_bytes=held_bytes + 8 * block.shape[0] * LANES + (6 << 20)
@@ -194,20 +199,20 @@
 def gram_kernel(first, steps, more, series, mask, *refs):
     columns = COEF_STEP
     if more:
-        gram, following, held, marks, halves, masked, sems, mark_sem = refs
+        here, gram, following, held, marks, halves, masked, sems, mark_sem = refs
         gram[...] = jnp.zeros_like(gram)
     else:
-        probes, before, following, coefs = refs[:4]
+        probes, before, here, coefs = refs[:4]
         held, marks, halves, masked, sems, mark_sem, gram = refs[4:]
         gram[...] = before[...]
         first, steps = first - 1, steps + 1
 
     def fetch(step):
         span = pl.ds((first + step) * columns, columns)
-        target = following if more and step == steps else held.at[step - (not more)]
+        target = following if more and step == steps else held.at[step - 1]
         return pltpu.make_async_copy(series.at[:, span], target, sems.at[step])
 
-    start = 0 if more else 1
+    start = 1
     end = steps + 1 if more else steps
     mark_copy = pltpu.make_async_copy(
         mask.at[:, pl.ds(first * columns, steps * columns)], marks, mark_sem
@@ -217,7 +222,7 @@
         fetch(step).start()
     mark_copy.wait()
     for step in range(steps):
-        values = following
+        values = here
         if step >= start:
             fetch(step).wait()
             values = held.at[step - start]
@@ -245,7 +250,7 @@
     coefs[0 : rows.shape[0], 0:frames] = made
 
 
-def local_coefs(series, noise_mask, first, steps, probes=None, before=()):
+def local_coefs(series, noise_mask, first, steps, before, probes=None):
     frames, voxels = series.shape
     more = probes is None
     vmem = pl.BlockSpec(memory_space=pltpu.VMEM)
@@ -253,7 +258,7 @@
     gram = jax.ShapeDtypeStruct((2 * frames, frames), jnp.float32)
     step = jax.ShapeDtypeStruct((frames, COEF_STEP), series.dtype)
     coefs = jax.ShapeDtypeStruct((COEF_ROWS, LANES), jnp.float32)
-    arrays = [] if more else [probes.T, *before]
+    arrays = [*before] if more else [probes.T, *before]
     total = steps if more else steps + 1
     return pl.pallas_call(
         functools.partial(gram_kernel, first, steps, more),
@@ -262,7 +267,7 @@
         out_specs=[vmem, vmem] if more else vmem,
         out_shape=[gram, step] if more else coefs,
         scratch_shapes=[
-            pltpu.VMEM((steps, frames, COEF_STEP), series.dtype),
+            pltpu.VMEM((total - 1, frames, COEF_STEP), series.dtype),
             pltpu.VMEM((1, total * COEF_STEP), noise_mask.dtype),
             pltpu.VMEM((2 * frames, COEF_STEP), jnp.bfloat16),
             pltpu.VMEM((frames, COEF_STEP), jnp.bfloat16),
@@ -446,13 +451,13 @@
     cut = frames * 3 // 5 // 8 * 8
     spans = [(0, cut), (cut, frames - cut)]
     steps = voxels // COEF_STEP
-    keep, send, residues = sample(plan, series, sample_weights, block_ids, tile_ids, tile_owner)
+    keep, send, residues, ahead = sample(plan, series, sample_weights, block_ids, tile_ids, tile_owner)
     keep, send, marks = lax.optimization_barrier((keep, send, noise_mask))
     pair = exchange(plan, 0, [keep, send])
-    grams = local_coefs(series, marks, 0, EARLY)
+    grams = local_coefs(series, marks, 0, EARLY, [ahead])
     chunks = [merge(plan, 0, span, False, residues, pair) for span in spans[:-1]]
     chunks[-1], grams = lax.optimization_barrier((chunks[-1], grams))
-    coefs = local_coefs(series, noise_mask, EARLY + 1, steps - EARLY - 1, probes, grams)
+    coefs = local_coefs(series, noise_mask, EARLY + 1, steps - EARLY - 1, grams, probes)
     coefs = exchange(plan, 0, [coefs, coefs])
     chunks.append(merge(plan, 0, spans[-1], True, residues, pair, coefs))
     for stage in range(1, stages):

time: 39.2 us -> 38.9 us (level)
  Pallas kernels: 14.2 us -> 13.8 us
    pallas_call x2, Pallas kernels: 7.52 us -> 7.02 us  [local_coefs(): pl.pallas_call(functools.partial(gram_kernel, first, steps, more), name='...]
  transfers between devices with their start and end apart: 14 -> 14, of which waited for: 6 -> 6; matrix products, arithmetic and copies ran while one was open for 0% -> 0% of each run, Pallas kernels for 20% -> 19%
where the time goes in v9:
time: 38.9 us; the launch traced here: 38.7 us
  starting transfers between devices  18.6 us (48%)
  Pallas kernels  13.8 us (35%)
  waiting for transfers between devices  6.15 us (16%)
    ppermute x14, starting transfers between devices, exchange(): received.append(lax.ppermute(blocks[digit], AXIS, pairs))  18.6 us
    pallas_call x2, Pallas kernels, local_coefs(): pl.pallas_call(functools.partial(gram_kernel, first, steps, more), name='...  7.02 us
    ppermute x14, waiting for transfers between devices, exchange(): received.append(lax.ppermute(blocks[digit], AXIS, pairs))  6.15 us
    pallas_call x1, Pallas kernels, sample(): pl.pallas_call(functools.partial(sample_kernel, plan), name='sample', in_...  4.82 us
    pallas_call x1, Pallas kernels, finish(): pl.pallas_call(functools.partial(finish_kernel, plan, comps, spans), name...  1.51 us
  transfers between devices with their start and end apart: 14, of which 6 were waited for; matrix products, arithmetic and copies ran while one was open for 0% of the time, Pallas kernels for 19%

profile of v9, /device:TPU:0, one launch (start us, length us, event | category | flops | bytes accessed | tf_op | source)
XLA Modules:
  0.0 38.7 jit_solution(8395407226237738511)
XLA Ops:
  0.0 4.8 %sample.1 = (f32[2640,128]{1,0:T(8,128)S(1)}, f32[2640,128]{1,0:T(8,128)S(1)}, s32[4,8,128]{2,1,0:T(8,128)S(1)}, f32[80,4096]{1,0:T(8,128)S(1)}) custom-call(s32[48]{0:T(128)} %block_ids.1, s32[48]{0:T(128)} %tile_ids.1, s32[128]{0:T(128)} %tile_owner.1, f32[80,32768]{1,0:T(8,128)} %series.5, bf16[48,256,128]{2,1,0:T(8,128)(2,1)} %weights.1), custom_call_target="tpu_custom_call" | custom-call | tf_op jit(solution)/shard_map/sample/pallas_call | solution.py:158
  4.8 0.5 %collective-permute-start = (f32[2640,128]{1,0:T(8,128)S(1)}, f32[2640,128]{1,0:T(8,128)S(1)}, u32[]{:S(2)}, u32[]{:S(2)}) collective-permute-start(f32[2640,128]{1,0:T(8,128)S(1)} %get-tuple-element.43), channel_id=1, source_target_pairs={{0,1},{1,0},{2,3},{3,2},{4,5},{5,4},{6,7},{7,6},{8,9},{9,8},{10,11... | collective-permute-start | bytes 4055048 | tf_op jit(solution)/shard_map/ppermute | solution.py:440
  5.3 3.1 %gram.1 = (f32[160,80]{1,0:T(8,128)S(1)}, f32[80,4096]{1,0:T(8,128)S(1)}) custom-call(f32[80,32768]{1,0:T(8,128)} %series.5, s32[1,32768]{1,0:T(1,128)} %bitcast.4, f32[80,4096]{1,0:T(8,128)S(1)} %get-tuple-element.49.refs_0_), custom_call_target="tpu_custom_call" | custom-call | flops 419430400 | bytes 5242880 | tf_op jit(solution)/shard_map/gram/pallas_call | solution.py:263
  8.5 0.0 copy-start
  8.5 0.0 collective-permute-done.refs_1_
  8.5 0.1 merge.4
  8.6 2.6 %collective-permute-start.1 = (f32[384,128]{1,0:T(8,128)S(1)}, f32[384,128]{1,0:T(8,128)S(1)}, u32[]{:S(2)}, u32[]{:S(2)}) collective-permute-start(f32[384,128]{1,0:T(8,128)S(1)} %get-tuple-element.53), channel_id=1, source_target_pairs={{0,2},{1,3},{2,0},{3,1},{4,6},{5,7},{6,4},{7,5},{8,10},{9,11},{10,... | collective-permute-start | bytes 589832 | tf_op jit(solution)/shard_map/ppermute | solution.py:440
  11.2 1.5 %collective-permute-start.2 = (f32[384,128]{1,0:T(8,128)S(1)}, f32[384,128]{1,0:T(8,128)S(1)}, u32[]{:S(2)}, u32[]{:S(2)}) collective-permute-start(f32[384,128]{1,0:T(8,128)S(1)} %get-tuple-element.54), channel_id=1, source_target_pairs={{0,4},{1,5},{2,6},{3,7},{4,0},{5,1},{6,2},{7,3},{8,12},{9,13},{10,... | collective-permute-start | bytes 589832 | tf_op jit(solution)/shard_map/ppermute | solution.py:440
  12.7 0.0 collective-permute-start.3
  12.7 3.9 %coefs.1.refs_2_ = f32[8,128]{1,0:T(8,128)S(1)} custom-call(f32[80,32768]{1,0:T(8,128)} %series.5, s32[1,32768]{1,0:T(1,128)} %bitcast.5, f32[5,80]{1,0:T(8,128)S(1)} %bitcast.3, f32[160,80]{1,0:T(8,128)S(1)} %get-tuple-element.60.refs_1_, f32[80,4096]{1,0:T(8,128)S(1)} %get-tuple-element.61.refs_2_), custom_call_target="tpu_custom_call" | custom-call | flops 419430400 | bytes 5242880 | tf_op jit(solution)/shard_map/coefs/pallas_call | solution.py:263
  16.6 0.1 collective-permute-start.7
  16.7 1.2 %collective-permute-done.7.refs_3_ = f32[8,128]{1,0:T(8,128)S(1)} collective-permute-done((f32[8,128]{1,0:T(8,128)S(1)}, f32[8,128]{1,0:T(8,128)S(1)}, u32[]{:S(2)}, u32[]{:S(2)}) %collective-permute-start.7) | collective-permute-done | bytes 4128 | tf_op jit(solution)/shard_map/ppermute | solution.py:440
  17.8 0.1 merge.6
  17.9 2.0 %collective-permute-start.8 = (f32[264,128]{1,0:T(8,128)S(1)}, f32[264,128]{1,0:T(8,128)S(1)}, u32[]{:S(2)}, u32[]{:S(2)}) collective-permute-start(f32[264,128]{1,0:T(8,128)S(1)} %get-tuple-element.63), channel_id=1, source_target_pairs={{0,2},{1,3},{2,0},{3,1},{4,6},{5,7},{6,4},{7,5},{8,10},{9,11},{10,... | collective-permute-start | bytes 405512 | tf_op jit(solution)/shard_map/ppermute | solution.py:440
  19.9 1.5 %collective-permute-start.9 = (f32[264,128]{1,0:T(8,128)S(1)}, f32[264,128]{1,0:T(8,128)S(1)}, u32[]{:S(2)}, u32[]{:S(2)}) collective-permute-start(f32[264,128]{1,0:T(8,128)S(1)} %get-tuple-element.64), channel_id=1, source_target_pairs={{0,4},{1,5},{2,6},{3,7},{4,0},{5,1},{6,2},{7,3},{8,12},{9,13},{10,... | collective-permute-start | bytes 405512 | tf_op jit(solution)/shard_map/ppermute | solution.py:440
  21.4 0.0 collective-permute-start.10
  21.5 1.0 %collective-permute-done.2.refs_3_ = f32[384,128]{1,0:T(8,128)S(1)} collective-permute-done((f32[384,128]{1,0:T(8,128)S(1)}, f32[384,128]{1,0:T(8,128)S(1)}, u32[]{:S(2)}, u32[]{:S(2)}) %collective-permute-start.2) | collective-permute-done | bytes 196640 | tf_op jit(solution)/shard_map/ppermute | solution.py:440
  22.4 0.0 collective-permute-done.3.refs_4_
  22.4 0.2 merge.5
  22.6 2.7 %collective-permute-start.5 = (f32[144,128]{1,0:T(8,128)S(1)}, f32[144,128]{1,0:T(8,128)S(1)}, u32[]{:S(2)}, u32[]{:S(2)}) collective-permute-start(f32[144,128]{1,0:T(8,128)S(1)} %get-tuple-element.58), channel_id=1, source_target_pairs={{0,16},{1,17},{2,18},{3,19},{4,20},{5,21},{6,22},{7,23},{8,24},{9,... | collective-permute-start | bytes 221192 | tf_op jit(solution)/shard_map/ppermute | solution.py:440
  25.3 1.3 %collective-permute-start.6 = (f32[144,128]{1,0:T(8,128)S(1)}, f32[144,128]{1,0:T(8,128)S(1)}, u32[]{:S(2)}, u32[]{:S(2)}) collective-permute-start(f32[144,128]{1,0:T(8,128)S(1)} %get-tuple-element.59), channel_id=1, source_target_pairs={{0,24},{1,25},{2,26},{3,27},{4,28},{5,29},{6,30},{7,31},{8,16},{9,... | collective-permute-start | bytes 221192 | tf_op jit(solution)/shard_map/ppermute | solution.py:440
  26.6 0.0 collective-permute-done.8.refs_2_
  26.6 0.2 collective-permute-start.4
  26.8 1.4 %collective-permute-done.9.refs_3_ = f32[264,128]{1,0:T(8,128)S(1)} collective-permute-done((f32[264,128]{1,0:T(8,128)S(1)}, f32[264,128]{1,0:T(8,128)S(1)}, u32[]{:S(2)}, u32[]{:S(2)}) %collective-permute-start.9) | collective-permute-done | bytes 135200 | tf_op jit(solution)/shard_map/ppermute | solution.py:440
  28.2 0.1 merge.7
  28.4 2.7 %collective-permute-start.12 = (f32[104,128]{1,0:T(8,128)S(1)}, f32[104,128]{1,0:T(8,128)S(1)}, u32[]{:S(2)}, u32[]{:S(2)}) collective-permute-start(f32[104,128]{1,0:T(8,128)S(1)} %get-tuple-element.71), channel_id=1, source_target_pairs={{0,16},{1,17},{2,18},{3,19},{4,20},{5,21},{6,22},{7,23},{8,24},{9,... | collective-permute-start | bytes 159752 | tf_op jit(solution)/shard_map/ppermute | solution.py:440
  31.0 1.3 %collective-permute-start.13 = (f32[104,128]{1,0:T(8,128)S(1)}, f32[104,128]{1,0:T(8,128)S(1)}, u32[]{:S(2)}, u32[]{:S(2)}) collective-permute-start(f32[104,128]{1,0:T(8,128)S(1)} %get-tuple-element.72), channel_id=1, source_target_pairs={{0,24},{1,25},{2,26},{3,27},{4,28},{5,29},{6,30},{7,31},{8,16},{9,... | collective-permute-start | bytes 159752 | tf_op jit(solution)/shard_map/ppermute | solution.py:440
  32.4 2.2 %collective-permute-start.11 = (f32[104,128]{1,0:T(8,128)S(1)}, f32[104,128]{1,0:T(8,128)S(1)}, u32[]{:S(2)}, u32[]{:S(2)}) collective-permute-start(f32[104,128]{1,0:T(8,128)S(1)} %get-tuple-element.70), channel_id=1, source_target_pairs={{0,8},{1,9},{2,10},{3,11},{4,12},{5,13},{6,14},{7,15},{8,0},{9,1},... | collective-permute-start | bytes 159752 | tf_op jit(solution)/shard_map/ppermute | solution.py:440
  34.5 0.7 %collective-permute-done.12.refs_6_ = f32[104,128]{1,0:T(8,128)S(1)} collective-permute-done((f32[104,128]{1,0:T(8,128)S(1)}, f32[104,128]{1,0:T(8,128)S(1)}, u32[]{:S(2)}, u32[]{:S(2)}) %collective-permute-start.12) | collective-permute-done | bytes 53280 | tf_op jit(solution)/shard_map/ppermute | solution.py:440
  35.2 1.8 %collective-permute-done.13.refs_7_ = f32[104,128]{1,0:T(8,128)S(1)} collective-permute-done((f32[104,128]{1,0:T(8,128)S(1)}, f32[104,128]{1,0:T(8,128)S(1)}, u32[]{:S(2)}, u32[]{:S(2)}) %collective-permute-start.13) | collective-permute-done | bytes 53280 | tf_op jit(solution)/shard_map/ppermute | solution.py:440
  37.0 0.2 collective-permute-done.11.refs_5_
  37.2 1.5 %finish.1 = f32[4,80,128]{2,1,0:T(8,128)} custom-call(s32[4,8,128]{2,1,0:T(8,128)S(1)} %get-tuple-element.39.refs_0_.residues, f32[144,128]{1,0:T(8,128)S(1)} %get-tuple-element.56.refs_0_, f32[144,128]{1,0:T(8,128)S(1)} %collective-permute-done.4.refs_1_, f32[144,128]{1,0:T(8,128)S(1)} %collective-permute-done.5.refs_2_, ...), custom_call_target="tpu_custom_call" | custom-call | tf_op jit(solution)/shard_map/finish/pallas_call | solution.py:426
  (6 shorter events, 0.0 us)
Async XLA Ops:
  4.8 3.7 %collective-permute-start = (f32[2640,128]{1,0:T(8,128)S(1)}, f32[2640,128]{1,0:T(8,128)S(1)}, u32[]{:S(2)}, u32[]{:S(2)}) collective-permute-start(f32[2640,128]{1,0:T(8,128)S(1)} %get-tuple-element.43), channel_id=1, source_target_pairs={{0,1},{1,0},{2,3},{3,2},{4,5},{5,4},{6,7},{7,6},{8,9},{9,8},{10,11... | collective-permute-start | bytes 4055048 | tf_op jit(solution)/shard_map/ppermute | solution.py:440
  8.5 4.2 %copy-start = (f32[80,5]{0,1:T(8,128)S(1)}, f32[80,5]{0,1:T(8,128)}, u32[]{:S(2)}) copy-start(f32[80,5]{0,1:T(8,128)} %param.9) | copy-start | bytes 4804
  8.6 12.8 %collective-permute-start.1 = (f32[384,128]{1,0:T(8,128)S(1)}, f32[384,128]{1,0:T(8,128)S(1)}, u32[]{:S(2)}, u32[]{:S(2)}) collective-permute-start(f32[384,128]{1,0:T(8,128)S(1)} %get-tuple-element.53), channel_id=1, source_target_pairs={{0,2},{1,3},{2,0},{3,1},{4,6},{5,7},{6,4},{7,5},{8,10},{9,11},{10,... | collective-permute-start | bytes 589832 | tf_op jit(solution)/shard_map/ppermute | solution.py:440
  11.2 11.2 %collective-permute-start.2 = (f32[384,128]{1,0:T(8,128)S(1)}, f32[384,128]{1,0:T(8,128)S(1)}, u32[]{:S(2)}, u32[]{:S(2)}) collective-permute-start(f32[384,128]{1,0:T(8,128)S(1)} %get-tuple-element.54), channel_id=1, source_target_pairs={{0,4},{1,5},{2,6},{3,7},{4,0},{5,1},{6,2},{7,3},{8,12},{9,13},{10,... | collective-permute-start | bytes 589832 | tf_op jit(solution)/shard_map/ppermute | solution.py:440
  12.7 9.7 %collective-permute-start.3 = (f32[384,128]{1,0:T(8,128)S(1)}, f32[384,128]{1,0:T(8,128)S(1)}, u32[]{:S(2)}, u32[]{:S(2)}) collective-permute-start(f32[384,128]{1,0:T(8,128)S(1)} %get-tuple-element.55), channel_id=1, source_target_pairs={{0,6},{1,7},{2,4},{3,5},{4,2},{5,3},{6,0},{7,1},{8,14},{9,15},{10,... | collective-permute-start | bytes 589832 | tf_op jit(solution)/shard_map/ppermute | solution.py:440
  16.6 1.2 %collective-permute-start.7 = (f32[8,128]{1,0:T(8,128)S(1)}, f32[8,128]{1,0:T(8,128)S(1)}, u32[]{:S(2)}, u32[]{:S(2)}) collective-permute-start(f32[8,128]{1,0:T(8,128)S(1)} %coefs.1.refs_2_), channel_id=1, source_target_pairs={{0,1},{1,0},{2,3},{3,2},{4,5},{5,4},{6,7},{7,6},{8,9},{9,8},{10,11... | collective-permute-start | bytes 12296 | tf_op jit(solution)/shard_map/ppermute | solution.py:440
  17.9 8.7 %collective-permute-start.8 = (f32[264,128]{1,0:T(8,128)S(1)}, f32[264,128]{1,0:T(8,128)S(1)}, u32[]{:S(2)}, u32[]{:S(2)}) collective-permute-start(f32[264,128]{1,0:T(8,128)S(1)} %get-tuple-element.63), channel_id=1, source_target_pairs={{0,2},{1,3},{2,0},{3,1},{4,6},{5,7},{6,4},{7,5},{8,10},{9,11},{10,... | collective-permute-start | bytes 405512 | tf_op jit(solution)/shard_map/ppermute | solution.py:440
  19.9 8.3 %collective-permute-start.9 = (f32[264,128]{1,0:T(8,128)S(1)}, f32[264,128]{1,0:T(8,128)S(1)}, u32[]{:S(2)}, u32[]{:S(2)}) collective-permute-start(f32[264,128]{1,0:T(8,128)S(1)} %get-tuple-element.64), channel_id=1, source_target_pairs={{0,4},{1,5},{2,6},{3,7},{4,0},{5,1},{6,2},{7,3},{8,12},{9,13},{10,... | collective-permute-start | bytes 405512 | tf_op jit(solution)/shard_map/ppermute | solution.py:440
  21.4 6.8 %collective-permute-start.10 = (f32[264,128]{1,0:T(8,128)S(1)}, f32[264,128]{1,0:T(8,128)S(1)}, u32[]{:S(2)}, u32[]{:S(2)}) collective-permute-start(f32[264,128]{1,0:T(8,128)S(1)} %get-tuple-element.65), channel_id=1, source_target_pairs={{0,6},{1,7},{2,4},{3,5},{4,2},{5,3},{6,0},{7,1},{8,14},{9,15},{10,... | collective-permute-start | bytes 405512 | tf_op jit(solution)/shard_map/ppermute | solution.py:440
  22.6 9.8 %collective-permute-start.5 = (f32[144,128]{1,0:T(8,128)S(1)}, f32[144,128]{1,0:T(8,128)S(1)}, u32[]{:S(2)}, u32[]{:S(2)}) collective-permute-start(f32[144,128]{1,0:T(8,128)S(1)} %get-tuple-element.58), channel_id=1, source_target_pairs={{0,16},{1,17},{2,18},{3,19},{4,20},{5,21},{6,22},{7,23},{8,24},{9,... | collective-permute-start | bytes 221192 | tf_op jit(solution)/shard_map/ppermute | solution.py:440
  25.3 7.1 %collective-permute-start.6 = (f32[144,128]{1,0:T(8,128)S(1)}, f32[144,128]{1,0:T(8,128)S(1)}, u32[]{:S(2)}, u32[]{:S(2)}) collective-permute-start(f32[144,128]{1,0:T(8,128)S(1)} %get-tuple-element.59), channel_id=1, source_target_pairs={{0,24},{1,25},{2,26},{3,27},{4,28},{5,29},{6,30},{7,31},{8,16},{9,... | collective-permute-start | bytes 221192 | tf_op jit(solution)/shard_map/ppermute | solution.py:440
  26.6 10.4 %collective-permute-start.4 = (f32[144,128]{1,0:T(8,128)S(1)}, f32[144,128]{1,0:T(8,128)S(1)}, u32[]{:S(2)}, u32[]{:S(2)}) collective-permute-start(f32[144,128]{1,0:T(8,128)S(1)} %get-tuple-element.57), channel_id=1, source_target_pairs={{0,8},{1,9},{2,10},{3,11},{4,12},{5,13},{6,14},{7,15},{8,0},{9,1},... | collective-permute-start | bytes 221192 | tf_op jit(solution)/shard_map/ppermute | solution.py:440
  28.4 6.9 %collective-permute-start.12 = (f32[104,128]{1,0:T(8,128)S(1)}, f32[104,128]{1,0:T(8,128)S(1)}, u32[]{:S(2)}, u32[]{:S(2)}) collective-permute-start(f32[104,128]{1,0:T(8,128)S(1)} %get-tuple-element.71), channel_id=1, source_target_pairs={{0,16},{1,17},{2,18},{3,19},{4,20},{5,21},{6,22},{7,23},{8,24},{9,... | collective-permute-start | bytes 159752 | tf_op jit(solution)/shard_map/ppermute | solution.py:440
  31.0 6.0 %collective-permute-start.13 = (f32[104,128]{1,0:T(8,128)S(1)}, f32[104,128]{1,0:T(8,128)S(1)}, u32[]{:S(2)}, u32[]{:S(2)}) collective-permute-start(f32[104,128]{1,0:T(8,128)S(1)} %get-tuple-element.72), channel_id=1, source_target_pairs={{0,24},{1,25},{2,26},{3,27},{4,28},{5,29},{6,30},{7,31},{8,16},{9,... | collective-permute-start | bytes 159752 | tf_op jit(solution)/shard_map/ppermute | solution.py:440
  32.4 4.8 %collective-permute-start.11 = (f32[104,128]{1,0:T(8,128)S(1)}, f32[104,128]{1,0:T(8,128)S(1)}, u32[]{:S(2)}, u32[]{:S(2)}) collective-permute-start(f32[104,128]{1,0:T(8,128)S(1)} %get-tuple-element.70), channel_id=1, source_target_pairs={{0,8},{1,9},{2,10},{3,11},{4,12},{5,13},{6,14},{7,15},{8,0},{9,1},... | collective-permute-start | bytes 159752 | tf_op jit(solution)/shard_map/ppermute | solution.py:440

commit v10 on v9

--- a/solution.py
+++ b/solution.py
@@ -11,7 +11,7 @@
 HIGHEST = lax.Precision.HIGHEST
 LANES = 128
 COEF_ROWS = 8
-GROUP = 8
+GROUP = 12
 AHEAD = 3
 WIDE = 256
 COEF_STEP = 4096

time: 38.9 us -> 38.9 us (level)
  no operation moved by 1% of the time
where the time goes in v10:
time: 38.9 us; the launch traced here: 38.7 us
  starting transfers between devices  18.6 us (48%)
  Pallas kernels  13.8 us (35%)
  waiting for transfers between devices  6.15 us (16%)
    ppermute x14, starting transfers between devices, exchange(): received.append(lax.ppermute(blocks[digit], AXIS, pairs))  18.6 us
    pallas_call x2, Pallas kernels, local_coefs(): pl.pallas_call(functools.partial(gram_kernel, first, steps, more), name='...  7.02 us
    ppermute x14, waiting for transfers between devices, exchange(): received.append(lax.ppermute(blocks[digit], AXIS, pairs))  6.15 us
    pallas_call x1, Pallas kernels, sample(): pl.pallas_call(functools.partial(sample_kernel, plan), name='sample', in_...  4.8 us
    pallas_call x1, Pallas kernels, finish(): pl.pallas_call(functools.partial(finish_kernel, plan, comps, spans), name...  1.51 us
  transfers between devices with their start and end apart: 14, of which 6 were waited for; matrix products, arithmetic and copies ran while one was open for 0% of the time, Pallas kernels for 19%

profile of v10, /device:TPU:0, one launch (start us, length us, event | category | flops | bytes accessed | tf_op | source)
XLA Modules:
  0.0 38.7 jit_solution(7915794631108962690)
XLA Ops:
  0.0 4.8 %sample.1 = (f32[2640,128]{1,0:T(8,128)S(1)}, f32[2640,128]{1,0:T(8,128)S(1)}, s32[4,8,128]{2,1,0:T(8,128)S(1)}, f32[80,4096]{1,0:T(8,128)S(1)}) custom-call(s32[48]{0:T(128)} %block_ids.1, s32[48]{0:T(128)} %tile_ids.1, s32[128]{0:T(128)} %tile_owner.1, f32[80,32768]{1,0:T(8,128)} %series.5, bf16[48,256,128]{2,1,0:T(8,128)(2,1)} %weights.1), custom_call_target="tpu_custom_call" | custom-call | tf_op jit(solution)/shard_map/sample/pallas_call | solution.py:158
  4.8 0.5 %collective-permute-start = (f32[2640,128]{1,0:T(8,128)S(1)}, f32[2640,128]{1,0:T(8,128)S(1)}, u32[]{:S(2)}, u32[]{:S(2)}) collective-permute-start(f32[2640,128]{1,0:T(8,128)S(1)} %get-tuple-element.43), channel_id=1, source_target_pairs={{0,1},{1,0},{2,3},{3,2},{4,5},{5,4},{6,7},{7,6},{8,9},{9,8},{10,11... | collective-permute-start | bytes 4055048 | tf_op jit(solution)/shard_map/ppermute | solution.py:440
  5.3 3.1 %gram.1 = (f32[160,80]{1,0:T(8,128)S(1)}, f32[80,4096]{1,0:T(8,128)S(1)}) custom-call(f32[80,32768]{1,0:T(8,128)} %series.5, s32[1,32768]{1,0:T(1,128)} %bitcast.4, f32[80,4096]{1,0:T(8,128)S(1)} %get-tuple-element.49.refs_0_), custom_call_target="tpu_custom_call" | custom-call | flops 419430400 | bytes 5242880 | tf_op jit(solution)/shard_map/gram/pallas_call | solution.py:263
  8.5 0.0 copy-start
  8.5 0.1 merge.4
  8.6 2.6 %collective-permute-start.1 = (f32[384,128]{1,0:T(8,128)S(1)}, f32[384,128]{1,0:T(8,128)S(1)}, u32[]{:S(2)}, u32[]{:S(2)}) collective-permute-start(f32[384,128]{1,0:T(8,128)S(1)} %get-tuple-element.53), channel_id=1, source_target_pairs={{0,2},{1,3},{2,0},{3,1},{4,6},{5,7},{6,4},{7,5},{8,10},{9,11},{10,... | collective-permute-start | bytes 589832 | tf_op jit(solution)/shard_map/ppermute | solution.py:440
  11.2 1.5 %collective-permute-start.2 = (f32[384,128]{1,0:T(8,128)S(1)}, f32[384,128]{1,0:T(8,128)S(1)}, u32[]{:S(2)}, u32[]{:S(2)}) collective-permute-start(f32[384,128]{1,0:T(8,128)S(1)} %get-tuple-element.54), channel_id=1, source_target_pairs={{0,4},{1,5},{2,6},{3,7},{4,0},{5,1},{6,2},{7,3},{8,12},{9,13},{10,... | collective-permute-start | bytes 589832 | tf_op jit(solution)/shard_map/ppermute | solution.py:440
  12.7 0.0 collective-permute-start.3
  12.7 3.9 %coefs.1.refs_2_ = f32[8,128]{1,0:T(8,128)S(1)} custom-call(f32[80,32768]{1,0:T(8,128)} %series.5, s32[1,32768]{1,0:T(1,128)} %bitcast.5, f32[5,80]{1,0:T(8,128)S(1)} %bitcast.3, f32[160,80]{1,0:T(8,128)S(1)} %get-tuple-element.60.refs_1_, f32[80,4096]{1,0:T(8,128)S(1)} %get-tuple-element.61.refs_2_), custom_call_target="tpu_custom_call" | custom-call | flops 419430400 | bytes 5242880 | tf_op jit(solution)/shard_map/coefs/pallas_call | solution.py:263
  16.6 0.1 collective-permute-start.7
  16.7 1.2 %collective-permute-done.7.refs_3_ = f32[8,128]{1,0:T(8,128)S(1)} collective-permute-done((f32[8,128]{1,0:T(8,128)S(1)}, f32[8,128]{1,0:T(8,128)S(1)}, u32[]{:S(2)}, u32[]{:S(2)}) %collective-permute-start.7) | collective-permute-done | bytes 4128 | tf_op jit(solution)/shard_map/ppermute | solution.py:440
  17.8 0.1 merge.6
  17.9 2.0 %collective-permute-start.8 = (f32[264,128]{1,0:T(8,128)S(1)}, f32[264,128]{1,0:T(8,128)S(1)}, u32[]{:S(2)}, u32[]{:S(2)}) collective-permute-start(f32[264,128]{1,0:T(8,128)S(1)} %get-tuple-element.63), channel_id=1, source_target_pairs={{0,2},{1,3},{2,0},{3,1},{4,6},{5,7},{6,4},{7,5},{8,10},{9,11},{10,... | collective-permute-start | bytes 405512 | tf_op jit(solution)/shard_map/ppermute | solution.py:440
  19.9 1.5 %collective-permute-start.9 = (f32[264,128]{1,0:T(8,128)S(1)}, f32[264,128]{1,0:T(8,128)S(1)}, u32[]{:S(2)}, u32[]{:S(2)}) collective-permute-start(f32[264,128]{1,0:T(8,128)S(1)} %get-tuple-element.64), channel_id=1, source_target_pairs={{0,4},{1,5},{2,6},{3,7},{4,0},{5,1},{6,2},{7,3},{8,12},{9,13},{10,... | collective-permute-start | bytes 405512 | tf_op jit(solution)/shard_map/ppermute | solution.py:440
  21.4 0.0 collective-permute-done.1.refs_2_
  21.4 0.0 collective-permute-start.10
  21.4 0.9 %collective-permute-done.2.refs_3_ = f32[384,128]{1,0:T(8,128)S(1)} collective-permute-done((f32[384,128]{1,0:T(8,128)S(1)}, f32[384,128]{1,0:T(8,128)S(1)}, u32[]{:S(2)}, u32[]{:S(2)}) %collective-permute-start.2) | collective-permute-done | bytes 196640 | tf_op jit(solution)/shard_map/ppermute | solution.py:440
  22.4 0.2 merge.5
  22.6 2.7 %collective-permute-start.5 = (f32[144,128]{1,0:T(8,128)S(1)}, f32[144,128]{1,0:T(8,128)S(1)}, u32[]{:S(2)}, u32[]{:S(2)}) collective-permute-start(f32[144,128]{1,0:T(8,128)S(1)} %get-tuple-element.58), channel_id=1, source_target_pairs={{0,16},{1,17},{2,18},{3,19},{4,20},{5,21},{6,22},{7,23},{8,24},{9,... | collective-permute-start | bytes 221192 | tf_op jit(solution)/shard_map/ppermute | solution.py:440
  25.2 1.3 %collective-permute-start.6 = (f32[144,128]{1,0:T(8,128)S(1)}, f32[144,128]{1,0:T(8,128)S(1)}, u32[]{:S(2)}, u32[]{:S(2)}) collective-permute-start(f32[144,128]{1,0:T(8,128)S(1)} %get-tuple-element.59), channel_id=1, source_target_pairs={{0,24},{1,25},{2,26},{3,27},{4,28},{5,29},{6,30},{7,31},{8,16},{9,... | collective-permute-start | bytes 221192 | tf_op jit(solution)/shard_map/ppermute | solution.py:440
  26.6 0.0 collective-permute-done.8.refs_2_
  26.6 0.2 collective-permute-start.4
  26.8 1.4 %collective-permute-done.9.refs_3_ = f32[264,128]{1,0:T(8,128)S(1)} collective-permute-done((f32[264,128]{1,0:T(8,128)S(1)}, f32[264,128]{1,0:T(8,128)S(1)}, u32[]{:S(2)}, u32[]{:S(2)}) %collective-permute-start.9) | collective-permute-done | bytes 135200 | tf_op jit(solution)/shard_map/ppermute | solution.py:440
  28.2 0.1 merge.7
  28.3 2.7 %collective-permute-start.12 = (f32[104,128]{1,0:T(8,128)S(1)}, f32[104,128]{1,0:T(8,128)S(1)}, u32[]{:S(2)}, u32[]{:S(2)}) collective-permute-start(f32[104,128]{1,0:T(8,128)S(1)} %get-tuple-element.71), channel_id=1, source_target_pairs={{0,16},{1,17},{2,18},{3,19},{4,20},{5,21},{6,22},{7,23},{8,24},{9,... | collective-permute-start | bytes 159752 | tf_op jit(solution)/shard_map/ppermute | solution.py:440
  31.0 1.3 %collective-permute-start.13 = (f32[104,128]{1,0:T(8,128)S(1)}, f32[104,128]{1,0:T(8,128)S(1)}, u32[]{:S(2)}, u32[]{:S(2)}) collective-permute-start(f32[104,128]{1,0:T(8,128)S(1)} %get-tuple-element.72), channel_id=1, source_target_pairs={{0,24},{1,25},{2,26},{3,27},{4,28},{5,29},{6,30},{7,31},{8,16},{9,... | collective-permute-start | bytes 159752 | tf_op jit(solution)/shard_map/ppermute | solution.py:440
  32.3 0.0 collective-permute-done.5.refs_2_
  32.3 2.2 %collective-permute-start.11 = (f32[104,128]{1,0:T(8,128)S(1)}, f32[104,128]{1,0:T(8,128)S(1)}, u32[]{:S(2)}, u32[]{:S(2)}) collective-permute-start(f32[104,128]{1,0:T(8,128)S(1)} %get-tuple-element.70), channel_id=1, source_target_pairs={{0,8},{1,9},{2,10},{3,11},{4,12},{5,13},{6,14},{7,15},{8,0},{9,1},... | collective-permute-start | bytes 159752 | tf_op jit(solution)/shard_map/ppermute | solution.py:440
  34.5 0.7 %collective-permute-done.12.refs_6_ = f32[104,128]{1,0:T(8,128)S(1)} collective-permute-done((f32[104,128]{1,0:T(8,128)S(1)}, f32[104,128]{1,0:T(8,128)S(1)}, u32[]{:S(2)}, u32[]{:S(2)}) %collective-permute-start.12) | collective-permute-done | bytes 53280 | tf_op jit(solution)/shard_map/ppermute | solution.py:440
  35.2 1.8 %collective-permute-done.13.refs_7_ = f32[104,128]{1,0:T(8,128)S(1)} collective-permute-done((f32[104,128]{1,0:T(8,128)S(1)}, f32[104,128]{1,0:T(8,128)S(1)}, u32[]{:S(2)}, u32[]{:S(2)}) %collective-permute-start.13) | collective-permute-done | bytes 53280 | tf_op jit(solution)/shard_map/ppermute | solution.py:440
  37.0 0.2 collective-permute-done.11.refs_5_
  37.2 1.5 %finish.1 = f32[4,80,128]{2,1,0:T(8,128)} custom-call(s32[4,8,128]{2,1,0:T(8,128)S(1)} %get-tuple-element.39.refs_0_.residues, f32[144,128]{1,0:T(8,128)S(1)} %get-tuple-element.56.refs_0_, f32[144,128]{1,0:T(8,128)S(1)} %collective-permute-done.4.refs_1_, f32[144,128]{1,0:T(8,128)S(1)} %collective-permute-done.5.refs_2_, ...), custom_call_target="tpu_custom_call" | custom-call | tf_op jit(solution)/shard_map/finish/pallas_call | solution.py:426
  (6 shorter events, 0.0 us)
Async XLA Ops:
  4.8 3.7 %collective-permute-start = (f32[2640,128]{1,0:T(8,128)S(1)}, f32[2640,128]{1,0:T(8,128)S(1)}, u32[]{:S(2)}, u32[]{:S(2)}) collective-permute-start(f32[2640,128]{1,0:T(8,128)S(1)} %get-tuple-element.43), channel_id=1, source_target_pairs={{0,1},{1,0},{2,3},{3,2},{4,5},{5,4},{6,7},{7,6},{8,9},{9,8},{10,11... | collective-permute-start | bytes 4055048 | tf_op jit(solution)/shard_map/ppermute | solution.py:440
  8.5 4.2 %copy-start = (f32[80,5]{0,1:T(8,128)S(1)}, f32[80,5]{0,1:T(8,128)}, u32[]{:S(2)}) copy-start(f32[80,5]{0,1:T(8,128)} %param.9) | copy-start | bytes 4804
  8.6 12.8 %collective-permute-start.1 = (f32[384,128]{1,0:T(8,128)S(1)}, f32[384,128]{1,0:T(8,128)S(1)}, u32[]{:S(2)}, u32[]{:S(2)}) collective-permute-start(f32[384,128]{1,0:T(8,128)S(1)} %get-tuple-element.53), channel_id=1, source_target_pairs={{0,2},{1,3},{2,0},{3,1},{4,6},{5,7},{6,4},{7,5},{8,10},{9,11},{10,... | collective-permute-start | bytes 589832 | tf_op jit(solution)/shard_map/ppermute | solution.py:440
  11.2 11.2 %collective-permute-start.2 = (f32[384,128]{1,0:T(8,128)S(1)}, f32[384,128]{1,0:T(8,128)S(1)}, u32[]{:S(2)}, u32[]{:S(2)}) collective-permute-start(f32[384,128]{1,0:T(8,128)S(1)} %get-tuple-element.54), channel_id=1, source_target_pairs={{0,4},{1,5},{2,6},{3,7},{4,0},{5,1},{6,2},{7,3},{8,12},{9,13},{10,... | collective-permute-start | bytes 589832 | tf_op jit(solution)/shard_map/ppermute | solution.py:440
  12.7 9.7 %collective-permute-start.3 = (f32[384,128]{1,0:T(8,128)S(1)}, f32[384,128]{1,0:T(8,128)S(1)}, u32[]{:S(2)}, u32[]{:S(2)}) collective-permute-start(f32[384,128]{1,0:T(8,128)S(1)} %get-tuple-element.55), channel_id=1, source_target_pairs={{0,6},{1,7},{2,4},{3,5},{4,2},{5,3},{6,0},{7,1},{8,14},{9,15},{10,... | collective-permute-start | bytes 589832 | tf_op jit(solution)/shard_map/ppermute | solution.py:440
  16.6 1.2 %collective-permute-start.7 = (f32[8,128]{1,0:T(8,128)S(1)}, f32[8,128]{1,0:T(8,128)S(1)}, u32[]{:S(2)}, u32[]{:S(2)}) collective-permute-start(f32[8,128]{1,0:T(8,128)S(1)} %coefs.1.refs_2_), channel_id=1, source_target_pairs={{0,1},{1,0},{2,3},{3,2},{4,5},{5,4},{6,7},{7,6},{8,9},{9,8},{10,11... | collective-permute-start | bytes 12296 | tf_op jit(solution)/shard_map/ppermute | solution.py:440
  17.9 8.7 %collective-permute-start.8 = (f32[264,128]{1,0:T(8,128)S(1)}, f32[264,128]{1,0:T(8,128)S(1)}, u32[]{:S(2)}, u32[]{:S(2)}) collective-permute-start(f32[264,128]{1,0:T(8,128)S(1)} %get-tuple-element.63), channel_id=1, source_target_pairs={{0,2},{1,3},{2,0},{3,1},{4,6},{5,7},{6,4},{7,5},{8,10},{9,11},{10,... | collective-permute-start | bytes 405512 | tf_op jit(solution)/shard_map/ppermute | solution.py:440
  19.9 8.3 %collective-permute-start.9 = (f32[264,128]{1,0:T(8,128)S(1)}, f32[264,128]{1,0:T(8,128)S(1)}, u32[]{:S(2)}, u32[]{:S(2)}) collective-permute-start(f32[264,128]{1,0:T(8,128)S(1)} %get-tuple-element.64), channel_id=1, source_target_pairs={{0,4},{1,5},{2,6},{3,7},{4,0},{5,1},{6,2},{7,3},{8,12},{9,13},{10,... | collective-permute-start | bytes 405512 | tf_op jit(solution)/shard_map/ppermute | solution.py:440
  21.4 6.8 %collective-permute-start.10 = (f32[264,128]{1,0:T(8,128)S(1)}, f32[264,128]{1,0:T(8,128)S(1)}, u32[]{:S(2)}, u32[]{:S(2)}) collective-permute-start(f32[264,128]{1,0:T(8,128)S(1)} %get-tuple-element.65), channel_id=1, source_target_pairs={{0,6},{1,7},{2,4},{3,5},{4,2},{5,3},{6,0},{7,1},{8,14},{9,15},{10,... | collective-permute-start | bytes 405512 | tf_op jit(solution)/shard_map/ppermute | solution.py:440
  22.6 9.8 %collective-permute-start.5 = (f32[144,128]{1,0:T(8,128)S(1)}, f32[144,128]{1,0:T(8,128)S(1)}, u32[]{:S(2)}, u32[]{:S(2)}) collective-permute-start(f32[144,128]{1,0:T(8,128)S(1)} %get-tuple-element.58), channel_id=1, source_target_pairs={{0,16},{1,17},{2,18},{3,19},{4,20},{5,21},{6,22},{7,23},{8,24},{9,... | collective-permute-start | bytes 221192 | tf_op jit(solution)/shard_map/ppermute | solution.py:440
  25.2 7.1 %collective-permute-start.6 = (f32[144,128]{1,0:T(8,128)S(1)}, f32[144,128]{1,0:T(8,128)S(1)}, u32[]{:S(2)}, u32[]{:S(2)}) collective-permute-start(f32[144,128]{1,0:T(8,128)S(1)} %get-tuple-element.59), channel_id=1, source_target_pairs={{0,24},{1,25},{2,26},{3,27},{4,28},{5,29},{6,30},{7,31},{8,16},{9,... | collective-permute-start | bytes 221192 | tf_op jit(solution)/shard_map/ppermute | solution.py:440
  26.6 10.4 %collective-permute-start.4 = (f32[144,128]{1,0:T(8,128)S(1)}, f32[144,128]{1,0:T(8,128)S(1)}, u32[]{:S(2)}, u32[]{:S(2)}) collective-permute-start(f32[144,128]{1,0:T(8,128)S(1)} %get-tuple-element.57), channel_id=1, source_target_pairs={{0,8},{1,9},{2,10},{3,11},{4,12},{5,13},{6,14},{7,15},{8,0},{9,1},... | collective-permute-start | bytes 221192 | tf_op jit(solution)/shard_map/ppermute | solution.py:440
  28.3 6.9 %collective-permute-start.12 = (f32[104,128]{1,0:T(8,128)S(1)}, f32[104,128]{1,0:T(8,128)S(1)}, u32[]{:S(2)}, u32[]{:S(2)}) collective-permute-start(f32[104,128]{1,0:T(8,128)S(1)} %get-tuple-element.71), channel_id=1, source_target_pairs={{0,16},{1,17},{2,18},{3,19},{4,20},{5,21},{6,22},{7,23},{8,24},{9,... | collective-permute-start | bytes 159752 | tf_op jit(solution)/shard_map/ppermute | solution.py:440
  31.0 6.0 %collective-permute-start.13 = (f32[104,128]{1,0:T(8,128)S(1)}, f32[104,128]{1,0:T(8,128)S(1)}, u32[]{:S(2)}, u32[]{:S(2)}) collective-permute-start(f32[104,128]{1,0:T(8,128)S(1)} %get-tuple-element.72), channel_id=1, source_target_pairs={{0,24},{1,25},{2,26},{3,27},{4,28},{5,29},{6,30},{7,31},{8,16},{9,... | collective-permute-start | bytes 159752 | tf_op jit(solution)/shard_map/ppermute | solution.py:440
  32.3 4.8 %collective-permute-start.11 = (f32[104,128]{1,0:T(8,128)S(1)}, f32[104,128]{1,0:T(8,128)S(1)}, u32[]{:S(2)}, u32[]{:S(2)}) collective-permute-start(f32[104,128]{1,0:T(8,128)S(1)} %get-tuple-element.70), channel_id=1, source_target_pairs={{0,8},{1,9},{2,10},{3,11},{4,12},{5,13},{6,14},{7,15},{8,0},{9,1},... | collective-permute-start | bytes 159752 | tf_op jit(solution)/shard_map/ppermute | solution.py:440
